TPU v7x, 32 devices: a whole 2x2x4 slice. The times are simulated.
32 devices in a mesh: gx: 4 (over z), gy: 2 (over x), gz: 4 (over y, core).
Axes of the slice: x: 2, y: 2, z: 4, core: 2. Of those that a mesh axis runs over, the one named last changes fastest.
Arguments:
- charges: float32 [32, 2, 4, 512], P('gx', 'gy', 'gz'), may hold values from -3 to 3
- offsets: float32 [3, 32, 2, 4, 512], P(None, 'gx', 'gy', 'gz'), may hold values from 0 to 1
- cells: int32 [2, 32, 2, 4, 512], P(None, 'gx', 'gy', 'gz'), may hold values from 0 to 511, as said below
- kernel: bfloat16 [17, 17, 17], replicated, may hold values from -0.078125 to 0.078125
Outputs:
- potential: float32 [32, 16, 512], P('gx', 'gy', 'gz')
- forces: float32 [3, 32, 2, 4, 512], P(None, 'gx', 'gy', 'gz')
Inputs may be any that keep to these rules, and one draw needn't show every extreme that they name: cells[0] lies in the block of 8 rows that belongs to the atom's second index (index g: g * 8 to g * 8 + 7); cells[1] lies likewise in the block of 128 that belongs to its third index.
All inputs are finite; a program needn't handle non-finite values.
Results may differ from a plain program's by a relative error of at most 0.0029.
Values may be sent and summed in bfloat16 or wider, within the bound.
No kernel may reach another device: no remote copies, remote signals or barrier semaphores. Data moves between devices by JAX's collectives and lax.ppermute only.
A program may use at most 64 MiB of HBM per device.

v0:
```python
import functools

import jax
import jax.numpy as jnp
from jax import lax
from jax.experimental import pallas as pl
from jax.experimental.pallas import tpu as pltpu
from jax.sharding import PartitionSpec as P

CY = 8
CZ = 128
EXT = 3
ROWS = 16
LANES = 32
GROUPS = 128 // LANES

F32 = jnp.float32
BF16 = jnp.bfloat16


def spline(fraction):
    remain = 1.0 - fraction
    values = [
        remain**3 / 6.0,
        (3.0 * fraction**3 - 6.0 * fraction**2 + 4.0) / 6.0,
        (-3.0 * fraction**3 + 3.0 * fraction**2 + 3.0 * fraction + 1.0) / 6.0,
        fraction**3 / 6.0,
    ]
    slopes = [
        -0.5 * remain**2,
        1.5 * fraction**2 - 2.0 * fraction,
        -1.5 * fraction**2 + fraction + 0.5,
        0.5 * fraction**2,
    ]
    return values, slopes


def pick(distance, four):
    out = jnp.zeros((), F32)
    for c in reversed(range(4)):
        out = jnp.where(distance == c, four[c], out)
    return out


def split(x):
    high = x.astype(BF16)
    return high, (x - high.astype(F32)).astype(BF16)


def nt_dot(a, b):
    return lax.dot_general(a, b, (((1,), (1,)), ((), ())), preferred_element_type=F32)


def iota(shape, dim):
    return lax.broadcasted_iota(jnp.int32, shape, dim)


def spread_kernel(tiles, chunks, group_planes, charge_ref, offset_ref, cell_ref, main_ref, z0_ref, z1_ref, acc):
    rows_total = tiles * chunks
    acc[...] = jnp.zeros_like(acc)
    row = iota((CZ + 2 * LANES, 128), 0)
    lower = row - CZ
    upper = row - CZ - LANES
    z_of_row = jnp.where(
        row < CZ,
        row,
        jnp.where(
            lower < LANES,
            jnp.where(lower < LANES // 2, lower, lower - LANES),
            jnp.where(upper < LANES // 2, CZ + upper, CZ - LANES + upper),
        ),
    )
    y_row = iota((ROWS, 128), 0)
    y_of_row = jnp.where(y_row < 12, y_row, y_row - ROWS)
    for t in range(tiles):
        s_high, s_low, z_high, z_low = [], [], [], []
        for j in range(chunks):
            r = t * chunks + j
            charge = charge_ref[pl.ds(r, 1), :]
            xv, _ = spline(offset_ref[pl.ds(r, 1), :])
            yv, _ = spline(offset_ref[pl.ds(rows_total + r, 1), :])
            zv, _ = spline(offset_ref[pl.ds(2 * rows_total + r, 1), :])
            cy = cell_ref[pl.ds(r, 1), :] & (CY - 1)
            cz = cell_ref[pl.ds(rows_total + r, 1), :] & (CZ - 1)
            y_dense = pick(y_of_row - (cy - 1), yv)
            z_dense = pick(z_of_row - (cz - 1), zv)
            s = jnp.concatenate([y_dense * (charge * xv[k]) for k in range(4)], 0)
            high, low = split(s)
            s_high.append(high)
            s_low.append(low)
            high, low = split(z_dense)
            z_high.append(high)
            z_low.append(low)
        s_high = jnp.concatenate(s_high, 1)
        s_low = jnp.concatenate(s_low, 1)
        z_high = jnp.concatenate(z_high, 1)
        z_low = jnp.concatenate(z_low, 1)
        both = nt_dot(jnp.concatenate([s_high, s_low], 0), z_high)
        got = both[: 4 * ROWS] + both[4 * ROWS :] + nt_dot(s_high, z_low)
        acc[t * ROWS : (t + 4) * ROWS, : CZ + 2 * LANES] += got
    planes = tiles + EXT
    main_ref[...] = acc[: planes * ROWS, :CZ]
    group = group_planes * ROWS
    lane = iota((group, 128), 1)
    lower_out = jnp.zeros((group, 128), F32)
    upper_out = jnp.zeros((group, 128), F32)
    for g in range(GROUPS):
        edge = acc[g * group : (g + 1) * group, CZ : CZ + 128]
        low = jnp.where(lane < LANES, edge, 0.0)
        high = jnp.where((lane >= LANES) & (lane < 2 * LANES), edge, 0.0)
        lower_out = lower_out + (pltpu.roll(low, g * LANES, 1) if g else low)
        upper_out = upper_out + pltpu.roll(high, (g * LANES - LANES) % 128, 1)
    even = lax.rem(lax.axis_index("gz"), 2) == 0
    z0_ref[...] = jnp.where(even, upper_out, lower_out)
    z1_ref[...] = jnp.where(even, lower_out, upper_out)


def z_fold_kernel(tiles, group_planes, main_ref, z0_ref, z1_ref, got0_ref, got1_ref, out_ref):
    planes = tiles + EXT
    group = group_planes * ROWS
    even = lax.rem(lax.axis_index("gz"), 2) == 0
    z0, z1, got0, got1 = z0_ref[...], z1_ref[...], got0_ref[...], got1_ref[...]
    own_upper = jnp.where(even, z0, z1)
    own_lower = jnp.where(even, z1, z0)
    right_lower = jnp.where(even, got0, got1)
    left_upper = jnp.where(even, got1, got0)
    lane = iota((group, 128), 1)
    first = (lane & (LANES - 1)) < LANES // 2
    halo = jnp.where(first, right_lower + own_upper, left_upper + own_lower)
    inner = jnp.where(first, left_upper, right_lower)
    for g in range(GROUPS):
        count = min(group, planes * ROWS - g * group)
        low = pltpu.roll(inner, (-g * LANES) % 128, 1) if g else inner
        high = pltpu.roll(inner, (128 - LANES - g * LANES) % 128, 1)
        add = jnp.where(lane < LANES // 2, low, jnp.where(lane >= 128 - LANES // 2, high, 0.0))
        out_ref[g * group : g * group + count, :] = (
            main_ref[g * group : g * group + count, :] + add[:count]
        )
    out_ref[planes * ROWS : planes * ROWS + group, :] = halo


def y_fold_kernel(n_gy, units, tiles, group_planes, *refs):
    sources, (out_ref, far_ref) = refs[:n_gy], refs[n_gy:]
    half = iota((CY, 128), 0) < CY // 2
    wide = n_gy * CY
    planes = tiles + EXT
    for u in range(units):
        blocks = [None] * n_gy

        def add(b, value):
            b = b % n_gy
            blocks[b] = value if blocks[b] is None else blocks[b] + value

        for b, ref in enumerate(sources):
            add(b, ref[u * ROWS : u * ROWS + CY, :])
            rest = ref[u * ROWS + CY : (u + 1) * ROWS, :]
            if n_gy == 2:
                add(b + 1, rest)
            else:
                add(b + 1, jnp.where(half, rest, 0.0))
                add(b - 1, jnp.where(half, 0.0, rest))
        value = jnp.concatenate(blocks, 0).astype(BF16)
        out_ref[u * wide : (u + 1) * wide, :] = value
        if u < EXT:
            far_ref[u * wide : (u + 1) * wide, :] = value
        elif planes - EXT <= u:
            v = u - (planes - EXT) + EXT
            far_ref[v * wide : (v + 1) * wide, :] = value


def field_kernel(
    tiles, chunks, group_planes, wide, span,
    own_ref, got1_ref, got3_ref, lower_ref, upper_ref, band_ref,
    charge_ref, offset_ref, cell_ref, potential_ref, force_ref, window, samples,
):
    planes = tiles + EXT
    radius = span // 2
    even = lax.rem(lax.axis_index("gx"), 2) == 0
    got1, got3 = got1_ref[...], got3_ref[...]
    right = jnp.where(even, got1, got3)
    left = jnp.where(even, got3, got1)
    own = own_ref[...]
    lane = iota((wide, 128), 1)
    margin = planes * wide

    def main(block, p):
        return block[p * wide : (p + 1) * wide].astype(F32)

    def edge(block, p, base=margin):
        g, q = divmod(p, group_planes)
        packed = block[base + q * wide : base + (q + 1) * wide].astype(F32)
        low = pltpu.roll(packed, (-g * LANES) % 128, 1) if g else packed
        high = pltpu.roll(packed, (128 - LANES - g * LANES) % 128, 1)
        return jnp.where(lane < LANES // 2, low, jnp.where(lane >= 128 - LANES // 2, high, 0.0))

    far_low, far_high = lower_ref[...], upper_ref[...]
    far_base = 2 * EXT * wide
    for x in range(2 * radius + planes):
        terms = []
        if x < planes:
            terms.append((main(left, x), edge(left, x)))
        if 0 <= x - tiles < planes:
            terms.append((main(own, x - tiles), edge(own, x - tiles)))
        if 0 <= x - 2 * tiles < planes:
            terms.append((main(right, x - 2 * tiles), edge(right, x - 2 * tiles)))
        if x < EXT:
            terms.append((main(far_low, EXT + x), edge(far_low, planes - EXT + x, far_base)))
        if 0 <= x - 3 * tiles < EXT:
            terms.append((main(far_high, x - 3 * tiles), edge(far_high, x - 3 * tiles, far_base)))
        window[x * wide : (x + 1) * wide, :128] = sum(a for a, _ in terms).astype(BF16)
        window[x * wide : (x + 1) * wide, 128:] = sum(b for _, b in terms).astype(BF16)

    band = band_ref[...]
    for x in range(planes):
        part = jnp.dot(
            band, window[x * wide : (x + span) * wide, :], preferred_element_type=F32
        )
        total = part[radius * ROWS : (radius + 1) * ROWS]
        for k in range(span):
            if k != radius:
                total = total + pltpu.roll(part[k * ROWS : (k + 1) * ROWS], (radius - k) % 256, 1)
        if 1 <= x <= tiles:
            potential_ref[x - 1] = total[:CY, :CZ]
        for c in range(4):
            moved = total if c == 1 else pltpu.roll(total, (1 - c) % 256, 1)
            samples[c, x * ROWS : (x + 1) * ROWS, :] = moved[:, :128]

    rows_total = tiles * chunks
    per = 8 // chunks
    upper_half = [iota((8, 128), 0) >= chunks * h for h in range(per)]
    for pair in range(tiles // per):
        rows = pl.ds(pair * 8, 8)
        charge = charge_ref[rows, :]
        xv, xs = spline(offset_ref[pl.ds(pair * 8, 8), :])
        yv, ys = spline(offset_ref[pl.ds(rows_total + pair * 8, 8), :])
        zv, zs = spline(offset_ref[pl.ds(2 * rows_total + pair * 8, 8), :])
        cy = cell_ref[pl.ds(pair * 8, 8), :] & (CY - 1)
        cz = cell_ref[pl.ds(rows_total + pair * 8, 8), :] & (CZ - 1)
        plain = [jnp.zeros((8, 128), F32) for _ in range(4)]
        along_y = [jnp.zeros((8, 128), F32) for _ in range(4)]
        along_z = [jnp.zeros((8, 128), F32) for _ in range(4)]
        for y in range(-1, CY + 2):
            distance = y + 1 - cy
            y_value = pick(distance, yv)
            y_slope = pick(distance, ys)
            row = y % ROWS
            for k in range(4):
                value = jnp.zeros((8, 128), F32)
                slope = jnp.zeros((8, 128), F32)
                for c in range(4):
                    source = None
                    for h in range(per):
                        at = (pair * per + h + k) * ROWS + row
                        line = jnp.broadcast_to(samples[c, at : at + 1, :], (8, 128))
                        source = line if h == 0 else jnp.where(upper_half[h], line, source)
                    picked = jnp.take_along_axis(source, cz, axis=1)
                    value = value + zv[c] * picked
                    slope = slope + zs[c] * picked
                plain[k] = plain[k] + y_value * value
                along_y[k] = along_y[k] + y_slope * value
                along_z[k] = along_z[k] + y_value * slope
        force_ref[0, rows, :] = -charge * sum(xs[k] * plain[k] for k in range(4))
        force_ref[1, rows, :] = -charge * sum(xv[k] * along_y[k] for k in range(4))
        force_ref[2, rows, :] = -charge * sum(xv[k] * along_z[k] for k in range(4))


def band_matrix(kernel, wide):
    span = kernel.shape[0]
    radius = span // 2
    row = jnp.arange(ROWS, dtype=jnp.int32)
    y_of_row = jnp.where(row < 12, row, row - ROWS)
    column = jnp.arange(wide, dtype=jnp.int32)
    tap = jnp.arange(span, dtype=jnp.int32)
    gap = column[None, None, :] - y_of_row[None, :, None] + radius - tap[:, None, None]
    chosen = (jnp.remainder(gap, wide) == 0).astype(BF16)
    band = jnp.einsum("ijk,jry->kriy", kernel, chosen, preferred_element_type=F32)
    return band.astype(BF16).reshape(span * ROWS, span * wide)


def vmem(n):
    return [pl.BlockSpec(memory_space=pltpu.VMEM)] * n


def local(charges, offsets, cells, kernel):
    n_gx, n_gy, n_gz = (lax.axis_size(axis) for axis in ("gx", "gy", "gz"))
    tiles, slots = charges.shape[0], charges.shape[3]
    span = kernel.shape[0]
    chunks = slots // 128
    rows = tiles * chunks
    planes = tiles + EXT
    group_planes = -(-planes // GROUPS)
    group = group_planes * ROWS
    wide = n_gy * CY
    charge = charges.reshape(rows, 128)
    offset = offsets.reshape(3 * rows, 128)
    cell = cells.reshape(2 * rows, 128)

    def shape(*dims, kind=F32):
        return jax.ShapeDtypeStruct(dims, kind)

    near = lambda n: [(i, i ^ 1) for i in range(n)]
    other = lambda n: [(i, (i + 1 if i % 2 else i - 1) % n) for i in range(n)]
    shift = lambda n, s: [(i, (i + s) % n) for i in range(n)]

    main, z0, z1 = pl.pallas_call(
        functools.partial(spread_kernel, tiles, chunks, group_planes),
        out_shape=(shape(planes * ROWS, 128), shape(group, 128), shape(group, 128)),
        in_specs=vmem(3),
        out_specs=tuple(vmem(3)),
        scratch_shapes=[pltpu.VMEM((GROUPS * group, CZ + 128), F32)],
        name="spread",
    )(charge, offset, cell)
    got0 = lax.ppermute(z0, "gz", near(n_gz))
    got1 = lax.ppermute(z1, "gz", other(n_gz))
    units = planes + group_planes
    block = pl.pallas_call(
        functools.partial(z_fold_kernel, tiles, group_planes),
        out_shape=shape(units * ROWS, 128),
        in_specs=vmem(5),
        out_specs=vmem(1)[0],
        name="z_fold",
    )(main, z0, z1, got0, got1)
    sources = [block] + [lax.ppermute(block, "gy", shift(n_gy, -s)) for s in range(1, n_gy)]
    mine, far = pl.pallas_call(
        functools.partial(y_fold_kernel, n_gy, units, tiles, group_planes),
        out_shape=(shape(units * wide, 128, kind=BF16), shape((2 * EXT + group_planes) * wide, 128, kind=BF16)),
        in_specs=vmem(n_gy),
        out_specs=tuple(vmem(2)),
        name="y_fold",
    )(*sources)
    x1 = lax.ppermute(mine, "gx", near(n_gx))
    if n_gx == 4:
        lower = upper = lax.ppermute(far, "gx", shift(n_gx, 2))
    else:
        lower = lax.ppermute(far, "gx", shift(n_gx, 2))
        upper = lax.ppermute(far, "gx", shift(n_gx, -2))
    x3 = lax.ppermute(mine, "gx", other(n_gx))
    band = band_matrix(kernel, wide)
    potential, forces = pl.pallas_call(
        functools.partial(field_kernel, tiles, chunks, group_planes, wide, span),
        out_shape=(shape(tiles, CY, CZ), shape(3, rows, 128)),
        in_specs=vmem(9),
        out_specs=tuple(vmem(2)),
        scratch_shapes=[
            pltpu.VMEM(((2 * (span // 2) + planes) * wide, 256), BF16),
            pltpu.VMEM((4, planes * ROWS, 128), F32),
        ],
        name="field",
    )(mine, x1, x3, lower, upper, band, charge, offset, cell)
    return potential, forces.reshape(3, tiles, 1, 1, slots)


def solution(mesh):
    placed = (
        P("gx", "gy", "gz", None),
        P(None, "gx", "gy", "gz", None),
        P(None, "gx", "gy", "gz", None),
        P(),
    )
    return jax.shard_map(
        local,
        mesh=mesh,
        in_specs=placed,
        out_specs=(P("gx", "gy", "gz"), P(None, "gx", "gy", "gz", None)),
        check_vma=False,
    )
```

profile of v0, /device:TPU:0, one launch (start us, length us, event | category | flops | bytes accessed | tf_op | source)
XLA Modules:
  0.0 34.7 jit_solution(9351131654325273336)
XLA Ops:
  0.6 0.0 copy-start
  0.6 3.6 %spread.1 = (f32[176,128]{1,0:T(8,128)}, f32[48,128]{1,0:T(8,128)}, f32[48,128]{1,0:T(8,128)}) custom-call(f32[32,128]{1,0:T(8,128)} %bitcast.18, f32[96,128]{1,0:T(8,128)} %bitcast.14, s32[64,128]{1,0:T(8,128)} %bitcast.16), custom_call_target="tpu_custom_call" | custom-call | tf_op jit(solution)/shard_map/spread/pallas_call | solution.py:305
  4.3 0.5 %collective-permute-start = (f32[48,128]{1,0:T(8,128)}, f32[48,128]{1,0:T(8,128)S(1)}, u32[]{:S(2)}, u32[]{:S(2)}) collective-permute-start(f32[48,128]{1,0:T(8,128)} %get-tuple-element.10.z0_ref), channel_id=1, source_target_pairs={{0,1},{1,0},{2,3},{3,2},{4,5},{5,4},{6,7},{7,6},{8,9},{9,8},{10,11... | collective-permute-start | bytes 73736 | tf_op jit(solution)/shard_map/ppermute | solution.py:313
  4.8 2.6 %collective-permute-start.1 = (f32[48,128]{1,0:T(8,128)}, f32[48,128]{1,0:T(8,128)S(1)}, u32[]{:S(2)}, u32[]{:S(2)}) collective-permute-start(f32[48,128]{1,0:T(8,128)} %get-tuple-element.11.z1_ref), channel_id=1, source_target_pairs={{0,3},{1,2},{2,1},{3,0},{4,7},{5,6},{6,5},{7,4},{8,11},{9,10},{10,... | collective-permute-start | bytes 73736 | tf_op jit(solution)/shard_map/ppermute | solution.py:314
  7.4 0.0 collective-permute-done.got0_ref
  7.4 1.8 %collective-permute-done.1.got1_ref = f32[48,128]{1,0:T(8,128)S(1)} collective-permute-done((f32[48,128]{1,0:T(8,128)}, f32[48,128]{1,0:T(8,128)S(1)}, u32[]{:S(2)}, u32[]{:S(2)}) %collective-permute-start.1) | collective-permute-done | bytes 24608 | tf_op jit(solution)/shard_map/ppermute | solution.py:314
  9.2 0.6 %copy-done.6 = f32[48,128]{1,0:T(8,128)} copy-done((f32[48,128]{1,0:T(8,128)}, f32[48,128]{1,0:T(8,128)S(1)}, u32[]{:S(2)}) %copy-start.6) | copy-done | bytes 24600
  9.8 1.7 %z_fold.1.refs_0_ = f32[224,128]{1,0:T(8,128)} custom-call(f32[176,128]{1,0:T(8,128)} %get-tuple-element.9.main_ref, f32[48,128]{1,0:T(8,128)} %get-tuple-element.10.z0_ref, f32[48,128]{1,0:T(8,128)} %get-tuple-element.11.z1_ref, f32[48,128]{1,0:T(8,128)} %copy-done.5, f32[48,128]{1,0:T(8,128)} %copy-done.6), custom_call_target="tpu_custom_call" | custom-call | tf_op jit(solution)/shard_map/z_fold/pallas_call | solution.py:316
  11.5 1.5 %collective-permute-start.2 = (f32[224,128]{1,0:T(8,128)}, f32[224,128]{1,0:T(8,128)S(1)}, u32[]{:S(2)}, u32[]{:S(2)}) collective-permute-start(f32[224,128]{1,0:T(8,128)} %z_fold.1.refs_0_), channel_id=1, source_target_pairs={{0,4},{4,0},{1,5},{5,1},{2,6},{6,2},{3,7},{7,3},{8,12},{12,8},{9,1... | collective-permute-start | bytes 344072 | tf_op jit(solution)/shard_map/ppermute | solution.py:323
  13.0 0.1 subtract_add_fusion
  13.1 4.0 %collective-permute-done.2.refs_1_ = f32[224,128]{1,0:T(8,128)S(1)} collective-permute-done((f32[224,128]{1,0:T(8,128)}, f32[224,128]{1,0:T(8,128)S(1)}, u32[]{:S(2)}, u32[]{:S(2)}) %collective-permute-start.2) | collective-permute-done | bytes 114720 | tf_op jit(solution)/shard_map/ppermute | solution.py:323
  17.0 0.6 %copy-done.2 = f32[224,128]{1,0:T(8,128)} copy-done((f32[224,128]{1,0:T(8,128)}, f32[224,128]{1,0:T(8,128)S(1)}, u32[]{:S(2)}) %copy-start.2) | copy-done | bytes 114712
  17.7 1.6 %y_fold.1 = (bf16[224,128]{1,0:T(8,128)(2,1)}, bf16[144,128]{1,0:T(8,128)(2,1)}) custom-call(f32[224,128]{1,0:T(8,128)} %z_fold.1.refs_0_, f32[224,128]{1,0:T(8,128)} %copy-done.2), custom_call_target="tpu_custom_call" | custom-call | tf_op jit(solution)/shard_map/y_fold/pallas_call | solution.py:324
  19.3 3.9 %collective-permute-start.4 = (bf16[224,128]{1,0:T(8,128)(2,1)}, bf16[224,128]{1,0:T(8,128)(2,1)S(1)}, u32[]{:S(2)}, u32[]{:S(2)}) collective-permute-start(bf16[224,128]{1,0:T(8,128)(2,1)} %get-tuple-element.12.own_ref), channel_id=1, source_target_pairs={{0,24},{8,16},{16,8},{24,0},{1,25},{9,17},{17,9},{25,1},{2,26},{10... | collective-permute-start | bytes 172040 | tf_op jit(solution)/shard_map/ppermute | solution.py:337
  23.1 0.0 collective-permute-start.3
  23.1 0.6 %collective-permute-start.5 = (bf16[144,128]{1,0:T(8,128)(2,1)}, bf16[144,128]{1,0:T(8,128)(2,1)S(1)}, u32[]{:S(2)}, u32[]{:S(2)}) collective-permute-start(bf16[144,128]{1,0:T(8,128)(2,1)} %get-tuple-element.13), channel_id=1, source_target_pairs={{0,16},{8,24},{16,0},{24,8},{1,17},{9,25},{17,1},{25,9},{2,18},{10... | collective-permute-start | bytes 110600 | tf_op jit(solution)/shard_map/ppermute | solution.py:333
  23.7 0.5 %fusion = bf16[17,16,17,16]{0,3,2,1:T(8,128)(2,1)S(1)} fusion(bf16[17,17,17]{2,1,0:T(8,128)(2,1)S(1)} %copy-done, s32[16,16]{1,0:T(8,128)S(1)} %subtract_add_fusion), kind=kOutput, calls=%fused_computation.1 | convolution fusion | flops 2646016 | bytes 158818 | tf_op jit(solution)/shard_map/ijk,jry->kriy/dot_general | solution.py:276
  24.2 3.6 %copy.8 = bf16[17,16,17,16]{3,2,1,0:T(8,128)(2,1)S(1)} copy(bf16[17,16,17,16]{0,3,2,1:T(8,128)(2,1)S(1)} %fusion) | data formatting | bytes 295936 | tf_op jit(solution)/shard_map/convert_element_type | solution.py:277
  27.8 1.5 %reshape.55.band_ref = bf16[272,272]{1,0:T(8,128)(2,1)} reshape(bf16[17,16,17,16]{3,2,1,0:T(8,128)(2,1)S(1)} %copy.8) | data formatting | bytes 295936 | tf_op jit(solution)/shard_map/reshape | solution.py:277
  29.4 0.0 collective-permute-done.3.got1_ref
  29.4 0.6 %copy-done.1 = bf16[144,128]{1,0:T(8,128)(2,1)} copy-done((bf16[144,128]{1,0:T(8,128)(2,1)}, bf16[144,128]{1,0:T(8,128)(2,1)S(1)}, u32[]{:S(2)}) %copy-start.1) | copy-done | bytes 36888
  30.0 0.0 copy-done.3
  30.0 0.6 %copy-done.4 = bf16[224,128]{1,0:T(8,128)(2,1)} copy-done((bf16[224,128]{1,0:T(8,128)(2,1)}, bf16[224,128]{1,0:T(8,128)(2,1)S(1)}, u32[]{:S(2)}) %copy-start.4) | copy-done | bytes 57368
  30.7 4.1 %field.1 = (f32[8,8,128]{2,1,0:T(8,128)}, f32[3,32,128]{2,1,0:T(8,128)}) custom-call(bf16[224,128]{1,0:T(8,128)(2,1)} %get-tuple-element.12.own_ref, bf16[224,128]{1,0:T(8,128)(2,1)} %copy-done.4, bf16[224,128]{1,0:T(8,128)(2,1)} %copy-done.3, bf16[144,128]{1,0:T(8,128)(2,1)} %copy-done.1, bf16[144,128]{1,0:T(8,128)(2,1)} %copy-done.1, ...), custom_call_target="tpu_custom_call" | custom-call | tf_op jit(solution)/shard_map/field/pallas_call | solution.py:339
  (11 shorter events, 0.0 us)
Async XLA Ops:
  0.6 23.1 %copy-start = (bf16[17,17,17]{2,1,0:T(8,128)(2,1)S(1)}, bf16[17,17,17]{2,1,0:T(8,128)(2,1)}, u32[]{:S(2)}) copy-start(bf16[17,17,17]{2,1,0:T(8,128)(2,1)} %param.7) | copy-start | bytes 29482
  4.3 3.1 %collective-permute-start = (f32[48,128]{1,0:T(8,128)}, f32[48,128]{1,0:T(8,128)S(1)}, u32[]{:S(2)}, u32[]{:S(2)}) collective-permute-start(f32[48,128]{1,0:T(8,128)} %get-tuple-element.10.z0_ref), channel_id=1, source_target_pairs={{0,1},{1,0},{2,3},{3,2},{4,5},{5,4},{6,7},{7,6},{8,9},{9,8},{10,11... | collective-permute-start | bytes 73736 | tf_op jit(solution)/shard_map/ppermute | solution.py:313
  4.8 4.4 %collective-permute-start.1 = (f32[48,128]{1,0:T(8,128)}, f32[48,128]{1,0:T(8,128)S(1)}, u32[]{:S(2)}, u32[]{:S(2)}) collective-permute-start(f32[48,128]{1,0:T(8,128)} %get-tuple-element.11.z1_ref), channel_id=1, source_target_pairs={{0,3},{1,2},{2,1},{3,0},{4,7},{5,6},{6,5},{7,4},{8,11},{9,10},{10,... | collective-permute-start | bytes 73736 | tf_op jit(solution)/shard_map/ppermute | solution.py:314
  7.4 1.8 %copy-start.5 = (f32[48,128]{1,0:T(8,128)}, f32[48,128]{1,0:T(8,128)S(1)}, u32[]{:S(2)}) copy-start(f32[48,128]{1,0:T(8,128)S(1)} %collective-permute-done.got0_ref) | copy-start | bytes 73732
  9.2 0.6 %copy-start.6 = (f32[48,128]{1,0:T(8,128)}, f32[48,128]{1,0:T(8,128)S(1)}, u32[]{:S(2)}) copy-start(f32[48,128]{1,0:T(8,128)S(1)} %collective-permute-done.1.got1_ref) | copy-start | bytes 73732
  11.5 5.6 %collective-permute-start.2 = (f32[224,128]{1,0:T(8,128)}, f32[224,128]{1,0:T(8,128)S(1)}, u32[]{:S(2)}, u32[]{:S(2)}) collective-permute-start(f32[224,128]{1,0:T(8,128)} %z_fold.1.refs_0_), channel_id=1, source_target_pairs={{0,4},{4,0},{1,5},{5,1},{2,6},{6,2},{3,7},{7,3},{8,12},{12,8},{9,1... | collective-permute-start | bytes 344072 | tf_op jit(solution)/shard_map/ppermute | solution.py:323
  17.0 0.6 %copy-start.2 = (f32[224,128]{1,0:T(8,128)}, f32[224,128]{1,0:T(8,128)S(1)}, u32[]{:S(2)}) copy-start(f32[224,128]{1,0:T(8,128)S(1)} %collective-permute-done.2.refs_1_) | copy-start | bytes 344068
  19.3 10.1 %collective-permute-start.4 = (bf16[224,128]{1,0:T(8,128)(2,1)}, bf16[224,128]{1,0:T(8,128)(2,1)S(1)}, u32[]{:S(2)}, u32[]{:S(2)}) collective-permute-start(bf16[224,128]{1,0:T(8,128)(2,1)} %get-tuple-element.12.own_ref), channel_id=1, source_target_pairs={{0,24},{8,16},{16,8},{24,0},{1,25},{9,17},{17,9},{25,1},{2,26},{10... | collective-permute-start | bytes 172040 | tf_op jit(solution)/shard_map/ppermute | solution.py:337
  23.1 6.3 %collective-permute-start.3 = (bf16[224,128]{1,0:T(8,128)(2,1)}, bf16[224,128]{1,0:T(8,128)(2,1)S(1)}, u32[]{:S(2)}, u32[]{:S(2)}) collective-permute-start(bf16[224,128]{1,0:T(8,128)(2,1)} %get-tuple-element.12.own_ref), channel_id=1, source_target_pairs={{0,8},{8,0},{16,24},{24,16},{1,9},{9,1},{17,25},{25,17},{2,10},{10... | collective-permute-start | bytes 172040 | tf_op jit(solution)/shard_map/ppermute | solution.py:331
  23.1 6.3 %collective-permute-start.5 = (bf16[144,128]{1,0:T(8,128)(2,1)}, bf16[144,128]{1,0:T(8,128)(2,1)S(1)}, u32[]{:S(2)}, u32[]{:S(2)}) collective-permute-start(bf16[144,128]{1,0:T(8,128)(2,1)} %get-tuple-element.13), channel_id=1, source_target_pairs={{0,16},{8,24},{16,0},{24,8},{1,17},{9,25},{17,1},{25,9},{2,18},{10... | collective-permute-start | bytes 110600 | tf_op jit(solution)/shard_map/ppermute | solution.py:333
  29.4 0.6 %copy-start.1 = (bf16[144,128]{1,0:T(8,128)(2,1)}, bf16[144,128]{1,0:T(8,128)(2,1)S(1)}, u32[]{:S(2)}) copy-start(bf16[144,128]{1,0:T(8,128)(2,1)S(1)} %collective-permute-done.5.lower_ref.upper_ref) | copy-start | bytes 110596
  29.4 0.6 %copy-start.3 = (bf16[224,128]{1,0:T(8,128)(2,1)}, bf16[224,128]{1,0:T(8,128)(2,1)S(1)}, u32[]{:S(2)}) copy-start(bf16[224,128]{1,0:T(8,128)(2,1)S(1)} %collective-permute-done.4.got3_ref) | copy-start | bytes 172036
  30.0 0.6 %copy-start.4 = (bf16[224,128]{1,0:T(8,128)(2,1)}, bf16[224,128]{1,0:T(8,128)(2,1)S(1)}, u32[]{:S(2)}) copy-start(bf16[224,128]{1,0:T(8,128)(2,1)S(1)} %collective-permute-done.3.got1_ref) | copy-start | bytes 172036
where the time goes:
time: 35 us; the launch traced here: 34.7 us
  Pallas kernels  11 us (31%)
  starting transfers between devices  9.06 us (26%)
  local copies, waits for them, and re-layouts  7.65 us (22%)
  waiting for transfers between devices  5.75 us (16%)
  between operations  0.68 us (2%)
  matrix products  0.51 us (1%)
    pallas_call x1, Pallas kernels, local(): pl.pallas_call(functools.partial(field_kernel, tiles, chunks, group_plane...  4.08 us
    ppermute x1, waiting for transfers between devices, local(): lax.ppermute(block, 'gy', shift(n_gy, -s))  3.95 us
    ppermute x1, starting transfers between devices, local(): x3 = lax.ppermute(mine, 'gx', other(n_gx))  3.85 us
    pallas_call x1, Pallas kernels, local(): pl.pallas_call(functools.partial(spread_kernel, tiles, chunks, group_plan...  3.65 us
    convert_element_type x1, local copies, waits for them, and re-layouts, band_matrix(): return band.astype(BF16).reshape(span * ROWS, span * wide)  3.62 us
    ppermute x1, starting transfers between devices, local(): got1 = lax.ppermute(z1, 'gz', other(n_gz))  2.62 us
    unnamed x14, local copies, waits for them, and re-layouts  2.49 us
    ppermute x1, waiting for transfers between devices, local(): got1 = lax.ppermute(z1, 'gz', other(n_gz))  1.78 us
  transfers between devices with their start and end apart: 6, of which 2 were waited for; matrix products, arithmetic and copies ran while one was open for 17% of the time, Pallas kernels for 0%

commit v1 on v0

--- a/solution.py
+++ b/solution.py
@@ -51,63 +51,88 @@
     return lax.dot_general(a, b, (((1,), (1,)), ((), ())), preferred_element_type=F32)
 
 
-def iota(shape, dim):
-    return lax.broadcasted_iota(jnp.int32, shape, dim)
-
-
-def spread_kernel(tiles, chunks, group_planes, charge_ref, offset_ref, cell_ref, main_ref, z0_ref, z1_ref, acc):
-    rows_total = tiles * chunks
+def iota(shape, dim, kind=jnp.int32):
+    return lax.broadcasted_iota(kind, shape, dim)
+
+
+def tall(row, kind, count):
+    tile = jnp.broadcast_to(row, (16, 128)).astype(kind)
+    return jnp.concatenate([tile] * (count // 16), 0)
+
+
+def z_weights(z_of_row, cell, rows):
+    count = z_of_row.shape[0]
+    high = low = jnp.zeros((count, 128), BF16)
+    for c in range(4):
+        here = z_of_row == tall(cell + (c - 1), jnp.int16, count)
+        high = jnp.where(here, tall(rows[c], BF16, count), high)
+        low = jnp.where(here, tall(rows[4 + c], BF16, count), low)
+    return high, low
+
+
+def edge_kernel(
+    tiles, chunks, group_planes, charge_hbm, offset_hbm, cell_hbm,
+    z0_ref, z1_ref, high_ref, low_ref, weight_ref, cell_ref,
+    charge_in, offset_in, cell_in, x_rows, y_rows, acc, sems,
+):
+    copies = [
+        pltpu.make_async_copy(source, target, sems.at[n])
+        for n, (source, target) in enumerate(
+            ((charge_hbm, charge_in), (offset_hbm, offset_in), (cell_hbm, cell_in))
+        )
+    ]
+    for copy in copies:
+        copy.start()
+    rows = tiles * chunks
     acc[...] = jnp.zeros_like(acc)
-    row = iota((CZ + 2 * LANES, 128), 0)
-    lower = row - CZ
-    upper = row - CZ - LANES
+    row = iota((2 * LANES, 128), 0, jnp.int16)
+    upper = row - LANES
     z_of_row = jnp.where(
-        row < CZ,
-        row,
-        jnp.where(
-            lower < LANES,
-            jnp.where(lower < LANES // 2, lower, lower - LANES),
-            jnp.where(upper < LANES // 2, CZ + upper, CZ - LANES + upper),
-        ),
+        row < LANES,
+        jnp.where(row < LANES // 2, row, row - LANES),
+        jnp.where(upper < LANES // 2, CZ + upper, CZ - LANES + upper),
     )
     y_row = iota((ROWS, 128), 0)
     y_of_row = jnp.where(y_row < 12, y_row, y_row - ROWS)
+    for copy in copies:
+        copy.wait()
+    for r in range(0, rows, 8):
+        at = pl.ds(r, 8)
+        xv, _ = spline(offset_in[at, :])
+        yv, _ = spline(offset_in[pl.ds(rows + r, 8), :])
+        zv, _ = spline(offset_in[pl.ds(2 * rows + r, 8), :])
+        charge = charge_in[at, :]
+        for c in range(4):
+            x_rows[c, at, :] = charge * xv[c]
+            y_rows[c, at, :] = yv[c]
+            high = zv[c].astype(BF16).astype(F32)
+            weight_ref[c, at, :] = high
+            weight_ref[4 + c, at, :] = zv[c] - high
+        cell_ref[at, :] = cell_in[pl.ds(rows + r, 8), :] & (CZ - 1)
     for t in range(tiles):
-        s_high, s_low, z_high, z_low = [], [], [], []
+        parts = [], [], [], []
         for j in range(chunks):
-            r = t * chunks + j
-            charge = charge_ref[pl.ds(r, 1), :]
-            xv, _ = spline(offset_ref[pl.ds(r, 1), :])
-            yv, _ = spline(offset_ref[pl.ds(rows_total + r, 1), :])
-            zv, _ = spline(offset_ref[pl.ds(2 * rows_total + r, 1), :])
-            cy = cell_ref[pl.ds(r, 1), :] & (CY - 1)
-            cz = cell_ref[pl.ds(rows_total + r, 1), :] & (CZ - 1)
-            y_dense = pick(y_of_row - (cy - 1), yv)
-            z_dense = pick(z_of_row - (cz - 1), zv)
-            s = jnp.concatenate([y_dense * (charge * xv[k]) for k in range(4)], 0)
-            high, low = split(s)
-            s_high.append(high)
-            s_low.append(low)
-            high, low = split(z_dense)
-            z_high.append(high)
-            z_low.append(low)
-        s_high = jnp.concatenate(s_high, 1)
-        s_low = jnp.concatenate(s_low, 1)
-        z_high = jnp.concatenate(z_high, 1)
-        z_low = jnp.concatenate(z_low, 1)
+            at = pl.ds(t * chunks + j, 1)
+            cy = cell_in[at, :] & (CY - 1)
+            y_dense = pick(y_of_row - (cy - 1), [y_rows[c, at, :] for c in range(4)])
+            s = jnp.concatenate([y_dense * x_rows[k, at, :] for k in range(4)], 0)
+            z = z_weights(z_of_row, cell_ref[at, :], [weight_ref[c, at, :] for c in range(8)])
+            for part, value in zip(parts, split(s) + z):
+                part.append(value)
+        s_high, s_low, z_high, z_low = (jnp.concatenate(part, 1) for part in parts)
+        high_ref[t * 4 * ROWS : (t + 1) * 4 * ROWS, :] = s_high
+        low_ref[t * 4 * ROWS : (t + 1) * 4 * ROWS, :] = s_low
         both = nt_dot(jnp.concatenate([s_high, s_low], 0), z_high)
         got = both[: 4 * ROWS] + both[4 * ROWS :] + nt_dot(s_high, z_low)
-        acc[t * ROWS : (t + 4) * ROWS, : CZ + 2 * LANES] += got
-    planes = tiles + EXT
-    main_ref[...] = acc[: planes * ROWS, :CZ]
+        acc[t * ROWS : (t + 4) * ROWS, : 2 * LANES] += got
     group = group_planes * ROWS
     lane = iota((group, 128), 1)
     lower_out = jnp.zeros((group, 128), F32)
     upper_out = jnp.zeros((group, 128), F32)
     for g in range(GROUPS):
-        edge = acc[g * group : (g + 1) * group, CZ : CZ + 128]
+        edge = acc[g * group : (g + 1) * group, :]
         low = jnp.where(lane < LANES, edge, 0.0)
-        high = jnp.where((lane >= LANES) & (lane < 2 * LANES), edge, 0.0)
+        high = jnp.where(lane >= LANES, edge, 0.0)
         lower_out = lower_out + (pltpu.roll(low, g * LANES, 1) if g else low)
         upper_out = upper_out + pltpu.roll(high, (g * LANES - LANES) % 128, 1)
     even = lax.rem(lax.axis_index("gz"), 2) == 0
@@ -115,7 +140,25 @@
     z1_ref[...] = jnp.where(even, lower_out, upper_out)
 
 
-def z_fold_kernel(tiles, group_planes, main_ref, z0_ref, z1_ref, got0_ref, got1_ref, out_ref):
+def spread_kernel(tiles, chunks, high_ref, low_ref, weight_ref, cell_ref, main_ref):
+    main_ref[...] = jnp.zeros_like(main_ref)
+    z_of_row = iota((CZ, 128), 0, jnp.int16)
+    for t in range(tiles):
+        parts = [], []
+        for j in range(chunks):
+            at = pl.ds(t * chunks + j, 1)
+            z = z_weights(z_of_row, cell_ref[at, :], [weight_ref[c, at, :] for c in range(8)])
+            for part, value in zip(parts, z):
+                part.append(value)
+        z_high, z_low = (jnp.concatenate(part, 1) for part in parts)
+        s_high = high_ref[t * 4 * ROWS : (t + 1) * 4 * ROWS, :]
+        s_low = low_ref[t * 4 * ROWS : (t + 1) * 4 * ROWS, :]
+        both = nt_dot(jnp.concatenate([s_high, s_low], 0), z_high)
+        got = both[: 4 * ROWS] + both[4 * ROWS :] + nt_dot(s_high, z_low)
+        main_ref[t * ROWS : (t + 4) * ROWS, :] += got
+
+
+def z_fold_kernel(tiles, group_planes, main_ref, z0_ref, z1_ref, got0_ref, got1_ref, out_ref, sent_ref):
     planes = tiles + EXT
     group = group_planes * ROWS
     even = lax.rem(lax.axis_index("gz"), 2) == 0
@@ -133,10 +176,11 @@
         low = pltpu.roll(inner, (-g * LANES) % 128, 1) if g else inner
         high = pltpu.roll(inner, (128 - LANES - g * LANES) % 128, 1)
         add = jnp.where(lane < LANES // 2, low, jnp.where(lane >= 128 - LANES // 2, high, 0.0))
-        out_ref[g * group : g * group + count, :] = (
-            main_ref[g * group : g * group + count, :] + add[:count]
-        )
+        total = main_ref[g * group : g * group + count, :] + add[:count]
+        out_ref[g * group : g * group + count, :] = total
+        sent_ref[g * group : g * group + count, :] = total.astype(BF16)
     out_ref[planes * ROWS : planes * ROWS + group, :] = halo
+    sent_ref[planes * ROWS : planes * ROWS + group, :] = halo.astype(BF16)
 
 
 def y_fold_kernel(n_gy, units, tiles, group_planes, *refs):
@@ -152,8 +196,9 @@
             blocks[b] = value if blocks[b] is None else blocks[b] + value
 
         for b, ref in enumerate(sources):
-            add(b, ref[u * ROWS : u * ROWS + CY, :])
-            rest = ref[u * ROWS + CY : (u + 1) * ROWS, :]
+            both = ref[u * ROWS : (u + 1) * ROWS, :].astype(F32)
+            add(b, both[:CY])
+            rest = both[CY:]
             if n_gy == 2:
                 add(b + 1, rest)
             else:
@@ -210,7 +255,7 @@
         window[x * wide : (x + 1) * wide, :128] = sum(a for a, _ in terms).astype(BF16)
         window[x * wide : (x + 1) * wide, 128:] = sum(b for _, b in terms).astype(BF16)
 
-    band = band_ref[...]
+    band = band_ref[:, : span * wide]
     for x in range(planes):
         part = jnp.dot(
             band, window[x * wide : (x + span) * wide, :], preferred_element_type=F32
@@ -264,17 +309,37 @@
         force_ref[2, rows, :] = -charge * sum(xv[k] * along_z[k] for k in range(4))
 
 
-def band_matrix(kernel, wide):
-    span = kernel.shape[0]
+def band_kernel(wide, kernel_ref, out_ref, rows_ref):
+    span = kernel_ref.shape[0]
     radius = span // 2
-    row = jnp.arange(ROWS, dtype=jnp.int32)
-    y_of_row = jnp.where(row < 12, row, row - ROWS)
-    column = jnp.arange(wide, dtype=jnp.int32)
-    tap = jnp.arange(span, dtype=jnp.int32)
-    gap = column[None, None, :] - y_of_row[None, :, None] + radius - tap[:, None, None]
-    chosen = (jnp.remainder(gap, wide) == 0).astype(BF16)
-    band = jnp.einsum("ijk,jry->kriy", kernel, chosen, preferred_element_type=F32)
-    return band.astype(BF16).reshape(span * ROWS, span * wide)
+    columns = out_ref.shape[1]
+    base = jnp.zeros((span, columns), F32)
+    tap = iota((span, columns), 0)
+    column = iota((span, columns), 1)
+    for i in range(span):
+        place = jnp.where(
+            (column >= i * wide) & (column < (i + 1) * wide)
+            & (((column - tap + radius) & (wide - 1)) == 0),
+            1.0, 0.0,
+        ).astype(BF16)
+        base = base + lax.dot_general(
+            kernel_ref[i], place, (((0,), (0,)), ((), ())), preferred_element_type=F32
+        )
+    rows_ref[...] = jnp.zeros_like(rows_ref)
+    within = column & (wide - 1)
+    for y in range(-1, CY + 2):
+        shift = y % wide
+        moved = base
+        if shift:
+            moved = jnp.where(
+                within >= shift,
+                pltpu.roll(base, shift, 1),
+                pltpu.roll(base, (shift - wide) % columns, 1),
+            )
+        for tile in range(columns // 128):
+            rows_ref[tile, pl.ds(y % ROWS, span, stride=ROWS), :] = moved[:, tile * 128 : (tile + 1) * 128]
+    for tile in range(columns // 128):
+        out_ref[:, tile * 128 : (tile + 1) * 128] = rows_ref[tile].astype(BF16)
 
 
 def vmem(n):
@@ -291,6 +356,7 @@
     group_planes = -(-planes // GROUPS)
     group = group_planes * ROWS
     wide = n_gy * CY
+    band_columns = -(-span * wide // 128) * 128
     charge = charges.reshape(rows, 128)
     offset = offsets.reshape(3 * rows, 128)
     cell = cells.reshape(2 * rows, 128)
@@ -302,30 +368,54 @@
     other = lambda n: [(i, (i + 1 if i % 2 else i - 1) % n) for i in range(n)]
     shift = lambda n, s: [(i, (i + s) % n) for i in range(n)]
 
-    main, z0, z1 = pl.pallas_call(
-        functools.partial(spread_kernel, tiles, chunks, group_planes),
-        out_shape=(shape(planes * ROWS, 128), shape(group, 128), shape(group, 128)),
-        in_specs=vmem(3),
-        out_specs=tuple(vmem(3)),
-        scratch_shapes=[pltpu.VMEM((GROUPS * group, CZ + 128), F32)],
-        name="spread",
-    )(charge, offset, cell)
+    z0, z1, s_high, s_low, weights, z_cell = pl.pallas_call(
+        functools.partial(edge_kernel, tiles, chunks, group_planes),
+        out_shape=(
+            shape(group, 128), shape(group, 128),
+            shape(tiles * 4 * ROWS, slots, kind=BF16), shape(tiles * 4 * ROWS, slots, kind=BF16),
+            shape(8, rows, 128), shape(rows, 128, kind=jnp.int32),
+        ),
+        in_specs=[pl.BlockSpec(memory_space=pltpu.HBM)] * 3,
+        out_specs=tuple(vmem(6)),
+        scratch_shapes=[
+            pltpu.VMEM((rows, 128), F32),
+            pltpu.VMEM((3 * rows, 128), F32),
+            pltpu.VMEM((2 * rows, 128), jnp.int32),
+            pltpu.VMEM((4, rows, 128), F32),
+            pltpu.VMEM((4, rows, 128), F32),
+            pltpu.VMEM((GROUPS * group, 128), F32),
+            pltpu.SemaphoreType.DMA((3,)),
+        ],
+        compiler_params=pltpu.CompilerParams(vmem_limit_bytes=8 << 20),
+        name="edge",
+    )(*(pltpu.with_memory_space_constraint(x, pltpu.HBM) for x in (charge, offset, cell)))
     got0 = lax.ppermute(z0, "gz", near(n_gz))
     got1 = lax.ppermute(z1, "gz", other(n_gz))
+    main = pl.pallas_call(
+        functools.partial(spread_kernel, tiles, chunks),
+        out_shape=shape(planes * ROWS, 128),
+        in_specs=vmem(4),
+        out_specs=vmem(1)[0],
+        compiler_params=pltpu.CompilerParams(vmem_limit_bytes=8 << 20),
+        cost_estimate=pl.CostEstimate(flops=400_000_000, bytes_accessed=2_000_000, transcendentals=0),
+        name="spread",
+    )(s_high, s_low, weights, z_cell)
     units = planes + group_planes
-    block = pl.pallas_call(
+    block, sent = pl.pallas_call(
         functools.partial(z_fold_kernel, tiles, group_planes),
-        out_shape=shape(units * ROWS, 128),
+        out_shape=(shape(units * ROWS, 128), shape(units * ROWS, 128, kind=BF16)),
         in_specs=vmem(5),
-        out_specs=vmem(1)[0],
+        out_specs=tuple(vmem(2)),
+        compiler_params=pltpu.CompilerParams(vmem_limit_bytes=4 << 20),
         name="z_fold",
     )(main, z0, z1, got0, got1)
-    sources = [block] + [lax.ppermute(block, "gy", shift(n_gy, -s)) for s in range(1, n_gy)]
+    sources = [block] + [lax.ppermute(sent, "gy", shift(n_gy, -s)) for s in range(1, n_gy)]
     mine, far = pl.pallas_call(
         functools.partial(y_fold_kernel, n_gy, units, tiles, group_planes),
         out_shape=(shape(units * wide, 128, kind=BF16), shape((2 * EXT + group_planes) * wide, 128, kind=BF16)),
         in_specs=vmem(n_gy),
         out_specs=tuple(vmem(2)),
+        compiler_params=pltpu.CompilerParams(vmem_limit_bytes=4 << 20),
         name="y_fold",
     )(*sources)
     x1 = lax.ppermute(mine, "gx", near(n_gx))
@@ -335,7 +425,15 @@
         lower = lax.ppermute(far, "gx", shift(n_gx, 2))
         upper = lax.ppermute(far, "gx", shift(n_gx, -2))
     x3 = lax.ppermute(mine, "gx", other(n_gx))
-    band = band_matrix(kernel, wide)
+    band = pl.pallas_call(
+        functools.partial(band_kernel, wide),
+        out_shape=shape(span * ROWS, band_columns, kind=BF16),
+        in_specs=vmem(1),
+        out_specs=vmem(1)[0],
+        scratch_shapes=[pltpu.VMEM((band_columns // 128, span * ROWS, 128), F32)],
+        compiler_params=pltpu.CompilerParams(vmem_limit_bytes=8 << 20),
+        name="band",
+    )(kernel)
     potential, forces = pl.pallas_call(
         functools.partial(field_kernel, tiles, chunks, group_planes, wide, span),
         out_shape=(shape(tiles, CY, CZ), shape(3, rows, 128)),
@@ -345,6 +443,7 @@
             pltpu.VMEM(((2 * (span // 2) + planes) * wide, 256), BF16),
             pltpu.VMEM((4, planes * ROWS, 128), F32),
         ],
+        compiler_params=pltpu.CompilerParams(vmem_limit_bytes=16 << 20),
         name="field",
     )(mine, x1, x3, lower, upper, band, charge, offset, cell)
     return potential, forces.reshape(3, tiles, 1, 1, slots)

time: 35 us -> 24.6 us (0.70)
  local copies, waits for them, and re-layouts: 7.65 us -> 0.02 us
  Pallas kernels: 11 us -> 6.6 us
  waiting for transfers between devices: 5.75 us -> 7.58 us
  matrix products: 0.51 us -> 0 us
  starting transfers between devices: 9.06 us -> 9.46 us
    ppermute x1, waiting for transfers between devices: 0.01 us -> 4.44 us  [local(): lower = upper = lax.ppermute(far, 'gx', shift(n_gx, 2))]
    convert_element_type x1 -> x0, local copies, waits for them, and re-layouts: 3.62 us -> none  [band_matrix(): return band.astype(BF16).reshape(span * ROWS, span * wide)]
    unnamed x14 -> x8, local copies, waits for them, and re-layouts: 2.49 us -> 0.02 us
    ppermute x1, starting transfers between devices: 0.01 us -> 1.89 us  [local(): x1 = lax.ppermute(mine, 'gx', near(n_gx))]
    pallas_call x1, Pallas kernels: 1.6 us -> 0.02 us  [local(): pl.pallas_call(functools.partial(y_fold_kernel, n_gy, units, tiles, group...]
    pallas_call x1, Pallas kernels: 1.68 us -> 0.09 us  [local(): pl.pallas_call(functools.partial(z_fold_kernel, tiles, group_planes), out...]
    reshape x1 -> x0, local copies, waits for them, and re-layouts: 1.54 us -> none  [band_matrix(): return band.astype(BF16).reshape(span * ROWS, span * wide)]
    ppermute x1, waiting for transfers between devices: 3.95 us -> 2.51 us  [local(): lax.ppermute(sent, 'gy', shift(n_gy, -s))]
  transfers between devices with their start and end apart: 6 -> 6, of which waited for: 2 -> 3; matrix products, arithmetic and copies ran while one was open for 17% -> 0% of each run, Pallas kernels for 0% -> 6%
where the time goes in v1:
time: 24.6 us; the launch traced here: 24.4 us
  starting transfers between devices  9.46 us (38%)
  waiting for transfers between devices  7.58 us (31%)
  Pallas kernels  6.6 us (27%)
  between operations  0.7 us (3%)
    ppermute x1, waiting for transfers between devices, local(): lower = upper = lax.ppermute(far, 'gx', shift(n_gx, 2))  4.44 us
    pallas_call x1, Pallas kernels, local(): pl.pallas_call(functools.partial(field_kernel, tiles, chunks, group_plane...  3.08 us
    ppermute x1, starting transfers between devices, local(): got1 = lax.ppermute(z1, 'gz', other(n_gz))  2.61 us
    ppermute x1, waiting for transfers between devices, local(): lax.ppermute(sent, 'gy', shift(n_gy, -s))  2.51 us
    ppermute x1, starting transfers between devices, local(): x3 = lax.ppermute(mine, 'gx', other(n_gx))  2.48 us
    pallas_call x1, Pallas kernels, local(): pl.pallas_call(functools.partial(edge_kernel, tiles, chunks, group_planes...  1.9 us
    ppermute x1, starting transfers between devices, local(): x1 = lax.ppermute(mine, 'gx', near(n_gx))  1.89 us
    ppermute x1, starting transfers between devices, local(): lax.ppermute(sent, 'gy', shift(n_gy, -s))  1.74 us
  transfers between devices with their start and end apart: 6, of which 3 were waited for; matrix products, arithmetic and copies ran while one was open for 0% of the time, Pallas kernels for 6%

profile of v1, /device:TPU:0, one launch (start us, length us, event | category | flops | bytes accessed | tf_op | source)
XLA Modules:
  0.0 24.4 jit_solution(16040374893947019545)
XLA Ops:
  0.6 1.9 %edge.1 = (f32[48,128]{1,0:T(8,128)S(1)}, f32[48,128]{1,0:T(8,128)S(1)}, bf16[512,512]{1,0:T(8,128)(2,1)S(1)}, bf16[512,512]{1,0:T(8,128)(2,1)S(1)}, f32[8,32,128]{2,1,0:T(8,128)S(1)}, /*index=5*/s32[32,128]{1,0:T(8,128)S(1)}) custom-call(f32[32,128]{1,0:T(8,128)} %bitcast.8, f32[96,128]{1,0:T(8,128)} %bitcast.4, s32[64,128]{1,0:T(8,128)} %bitcast.6), custom_call_target="tpu_custom_call" | custom-call | tf_op jit(solution)/shard_map/edge/pallas_call | solution.py:371
  2.5 0.6 %collective-permute-start = (f32[48,128]{1,0:T(8,128)S(1)}, f32[48,128]{1,0:T(8,128)S(1)}, u32[]{:S(2)}, u32[]{:S(2)}) collective-permute-start(f32[48,128]{1,0:T(8,128)S(1)} %get-tuple-element.18.z0_ref), channel_id=1, source_target_pairs={{0,1},{1,0},{2,3},{3,2},{4,5},{5,4},{6,7},{7,6},{8,9},{9,8},{10,11... | collective-permute-start | bytes 73736 | tf_op jit(solution)/shard_map/ppermute | solution.py:392
  3.1 2.6 %collective-permute-start.1 = (f32[48,128]{1,0:T(8,128)S(1)}, f32[48,128]{1,0:T(8,128)S(1)}, u32[]{:S(2)}, u32[]{:S(2)}) collective-permute-start(f32[48,128]{1,0:T(8,128)S(1)} %get-tuple-element.19.z1_ref), channel_id=1, source_target_pairs={{0,3},{1,2},{2,1},{3,0},{4,7},{5,6},{6,5},{7,4},{8,11},{9,10},{10,... | collective-permute-start | bytes 73736 | tf_op jit(solution)/shard_map/ppermute | solution.py:393
  5.7 0.9 %spread.1.main_ref = f32[176,128]{1,0:T(8,128)S(1)} custom-call(bf16[512,512]{1,0:T(8,128)(2,1)S(1)} %get-tuple-element.14.high_ref, bf16[512,512]{1,0:T(8,128)(2,1)S(1)} %get-tuple-element.15.low_ref, f32[8,32,128]{2,1,0:T(8,128)S(1)} %get-tuple-element.16.weight_ref, s32[32,128]{1,0:T(8,128)S(1)} %get-tuple-element.17.cell_ref), custom_call_target="tpu_custom_call" | custom-call | flops 400000000 | bytes 2000000 | tf_op jit(solution)/shard_map/spread/pallas_call | solution.py:394
  6.6 0.0 collective-permute-done.got0_ref
  6.6 0.6 %collective-permute-done.1.got1_ref = f32[48,128]{1,0:T(8,128)S(1)} collective-permute-done((f32[48,128]{1,0:T(8,128)S(1)}, f32[48,128]{1,0:T(8,128)S(1)}, u32[]{:S(2)}, u32[]{:S(2)}) %collective-permute-start.1) | collective-permute-done | bytes 24608 | tf_op jit(solution)/shard_map/ppermute | solution.py:393
  7.2 0.1 z_fold.1
  7.3 0.0 copy-start.2
  7.3 1.7 %collective-permute-start.2 = (bf16[224,128]{1,0:T(8,128)(2,1)S(1)}, bf16[224,128]{1,0:T(8,128)(2,1)S(1)}, u32[]{:S(2)}, u32[]{:S(2)}) collective-permute-start(bf16[224,128]{1,0:T(8,128)(2,1)S(1)} %get-tuple-element.21), channel_id=1, source_target_pairs={{0,4},{4,0},{1,5},{5,1},{2,6},{6,2},{3,7},{7,3},{8,12},{12,8},{9,1... | collective-permute-start | bytes 172040 | tf_op jit(solution)/shard_map/ppermute | solution.py:412
  9.1 2.5 %collective-permute-done.2.refs_1_ = bf16[224,128]{1,0:T(8,128)(2,1)S(1)} collective-permute-done((bf16[224,128]{1,0:T(8,128)(2,1)S(1)}, bf16[224,128]{1,0:T(8,128)(2,1)S(1)}, u32[]{:S(2)}, u32[]{:S(2)}) %collective-permute-start.2) | collective-permute-done | bytes 57376 | tf_op jit(solution)/shard_map/ppermute | solution.py:412
  11.6 1.9 %collective-permute-start.3 = (bf16[224,128]{1,0:T(8,128)(2,1)S(1)}, bf16[224,128]{1,0:T(8,128)(2,1)S(1)}, u32[]{:S(2)}, u32[]{:S(2)}) collective-permute-start(bf16[224,128]{1,0:T(8,128)(2,1)S(1)} %get-tuple-element.22.own_ref), channel_id=1, source_target_pairs={{0,8},{8,0},{16,24},{24,16},{1,9},{9,1},{17,25},{25,17},{2,10},{10... | collective-permute-start | bytes 172040 | tf_op jit(solution)/shard_map/ppermute | solution.py:421
  13.5 2.5 %collective-permute-start.4 = (bf16[224,128]{1,0:T(8,128)(2,1)S(1)}, bf16[224,128]{1,0:T(8,128)(2,1)S(1)}, u32[]{:S(2)}, u32[]{:S(2)}) collective-permute-start(bf16[224,128]{1,0:T(8,128)(2,1)S(1)} %get-tuple-element.22.own_ref), channel_id=1, source_target_pairs={{0,24},{8,16},{16,8},{24,0},{1,25},{9,17},{17,9},{25,1},{2,26},{10... | collective-permute-start | bytes 172040 | tf_op jit(solution)/shard_map/ppermute | solution.py:427
  16.0 0.0 copy-start
  16.0 0.0 copy-start.1
  16.0 0.2 collective-permute-start.5
  16.2 0.0 copy-done.2
  16.2 0.6 %band.1.band_ref = bf16[272,384]{1,0:T(8,128)(2,1)S(1)} custom-call(bf16[17,17,17]{2,1,0:T(8,128)(2,1)S(1)} %copy-done.2), custom_call_target="tpu_custom_call" | custom-call | tf_op jit(solution)/shard_map/band/pallas_call | solution.py:428
  16.8 4.4 %collective-permute-done.5.lower_ref.upper_ref = bf16[144,128]{1,0:T(8,128)(2,1)S(1)} collective-permute-done((bf16[144,128]{1,0:T(8,128)(2,1)S(1)}, bf16[144,128]{1,0:T(8,128)(2,1)S(1)}, u32[]{:S(2)}, u32[]{:S(2)}) %collective-permute-start.5) | collective-permute-done | bytes 36896 | tf_op jit(solution)/shard_map/ppermute | solution.py:423
  21.2 0.0 collective-permute-done.3.got1_ref
  21.2 0.0 collective-permute-done.4.got3_ref
  21.2 0.0 copy-done
  21.2 0.0 copy-done.1
  21.3 0.0 copy-done.3
  21.3 3.1 %field.1 = (f32[8,8,128]{2,1,0:T(8,128)}, f32[3,32,128]{2,1,0:T(8,128)}) custom-call(bf16[224,128]{1,0:T(8,128)(2,1)S(1)} %get-tuple-element.22.own_ref, bf16[224,128]{1,0:T(8,128)(2,1)S(1)} %collective-permute-done.3.got1_ref, bf16[224,128]{1,0:T(8,128)(2,1)S(1)} %collective-permute-done.4.got3_ref, ...), custom_call_target="tpu_custom_call" | custom-call | tf_op jit(solution)/shard_map/field/pallas_call | solution.py:437
  (2 shorter events, 0.0 us)
Async XLA Ops:
  2.5 4.1 %collective-permute-start = (f32[48,128]{1,0:T(8,128)S(1)}, f32[48,128]{1,0:T(8,128)S(1)}, u32[]{:S(2)}, u32[]{:S(2)}) collective-permute-start(f32[48,128]{1,0:T(8,128)S(1)} %get-tuple-element.18.z0_ref), channel_id=1, source_target_pairs={{0,1},{1,0},{2,3},{3,2},{4,5},{5,4},{6,7},{7,6},{8,9},{9,8},{10,11... | collective-permute-start | bytes 73736 | tf_op jit(solution)/shard_map/ppermute | solution.py:392
  3.1 4.1 %collective-permute-start.1 = (f32[48,128]{1,0:T(8,128)S(1)}, f32[48,128]{1,0:T(8,128)S(1)}, u32[]{:S(2)}, u32[]{:S(2)}) collective-permute-start(f32[48,128]{1,0:T(8,128)S(1)} %get-tuple-element.19.z1_ref), channel_id=1, source_target_pairs={{0,3},{1,2},{2,1},{3,0},{4,7},{5,6},{6,5},{7,4},{8,11},{9,10},{10,... | collective-permute-start | bytes 73736 | tf_op jit(solution)/shard_map/ppermute | solution.py:393
  7.3 8.8 %copy-start.2 = (bf16[17,17,17]{2,1,0:T(8,128)(2,1)S(1)}, bf16[17,17,17]{2,1,0:T(8,128)(2,1)}, u32[]{:S(2)}) copy-start(bf16[17,17,17]{2,1,0:T(8,128)(2,1)} %kernel_ref.1) | copy-start | bytes 29482
  7.3 4.3 %collective-permute-start.2 = (bf16[224,128]{1,0:T(8,128)(2,1)S(1)}, bf16[224,128]{1,0:T(8,128)(2,1)S(1)}, u32[]{:S(2)}, u32[]{:S(2)}) collective-permute-start(bf16[224,128]{1,0:T(8,128)(2,1)S(1)} %get-tuple-element.21), channel_id=1, source_target_pairs={{0,4},{4,0},{1,5},{5,1},{2,6},{6,2},{3,7},{7,3},{8,12},{12,8},{9,1... | collective-permute-start | bytes 172040 | tf_op jit(solution)/shard_map/ppermute | solution.py:412
  11.6 9.6 %collective-permute-start.3 = (bf16[224,128]{1,0:T(8,128)(2,1)S(1)}, bf16[224,128]{1,0:T(8,128)(2,1)S(1)}, u32[]{:S(2)}, u32[]{:S(2)}) collective-permute-start(bf16[224,128]{1,0:T(8,128)(2,1)S(1)} %get-tuple-element.22.own_ref), channel_id=1, source_target_pairs={{0,8},{8,0},{16,24},{24,16},{1,9},{9,1},{17,25},{25,17},{2,10},{10... | collective-permute-start | bytes 172040 | tf_op jit(solution)/shard_map/ppermute | solution.py:421
  13.5 7.7 %collective-permute-start.4 = (bf16[224,128]{1,0:T(8,128)(2,1)S(1)}, bf16[224,128]{1,0:T(8,128)(2,1)S(1)}, u32[]{:S(2)}, u32[]{:S(2)}) collective-permute-start(bf16[224,128]{1,0:T(8,128)(2,1)S(1)} %get-tuple-element.22.own_ref), channel_id=1, source_target_pairs={{0,24},{8,16},{16,8},{24,0},{1,25},{9,17},{17,9},{25,1},{2,26},{10... | collective-permute-start | bytes 172040 | tf_op jit(solution)/shard_map/ppermute | solution.py:427
  16.0 5.3 %copy-start = (f32[3,8,1,1,512]{4,3,2,1,0:T(1,128)S(1)}, f32[3,8,1,1,512]{4,3,2,1,0:T(1,128)}, u32[]{:S(2)}) copy-start(f32[3,8,1,1,512]{4,3,2,1,0:T(1,128)} %param.5) | copy-start | bytes 147460
  16.0 5.3 %copy-start.1 = (s32[2,8,1,1,512]{4,3,2,1,0:T(1,128)S(1)}, s32[2,8,1,1,512]{4,3,2,1,0:T(1,128)}, u32[]{:S(2)}) copy-start(s32[2,8,1,1,512]{4,3,2,1,0:T(1,128)} %param.6) | copy-start | bytes 98308
  16.0 5.3 %copy-start.3 = (f32[8,1,1,512]{3,2,1,0:T(1,128)S(1)}, f32[8,1,1,512]{3,2,1,0:T(1,128)}, u32[]{:S(2)}) copy-start(f32[8,1,1,512]{3,2,1,0:T(1,128)} %param.4) | copy-start | bytes 49156
  16.0 5.3 %collective-permute-start.5 = (bf16[144,128]{1,0:T(8,128)(2,1)S(1)}, bf16[144,128]{1,0:T(8,128)(2,1)S(1)}, u32[]{:S(2)}, u32[]{:S(2)}) collective-permute-start(bf16[144,128]{1,0:T(8,128)(2,1)S(1)} %get-tuple-element.23), channel_id=1, source_target_pairs={{0,16},{8,24},{16,0},{24,8},{1,17},{9,25},{17,1},{25,9},{2,18},{10... | collective-permute-start | bytes 110600 | tf_op jit(solution)/shard_map/ppermute | solution.py:423

commit v2 on v1

--- a/solution.py
+++ b/solution.py
@@ -7,10 +7,13 @@
 from jax.experimental.pallas import tpu as pltpu
 from jax.sharding import PartitionSpec as P
 
+
 CY = 8
 CZ = 128
 EXT = 3
 ROWS = 16
+TALL = CY + EXT
+AHEAD = 4
 LANES = 32
 GROUPS = 128 // LANES
 
@@ -86,12 +89,7 @@
     rows = tiles * chunks
     acc[...] = jnp.zeros_like(acc)
     row = iota((2 * LANES, 128), 0, jnp.int16)
-    upper = row - LANES
-    z_of_row = jnp.where(
-        row < LANES,
-        jnp.where(row < LANES // 2, row, row - LANES),
-        jnp.where(upper < LANES // 2, CZ + upper, CZ - LANES + upper),
-    )
+    z_of_row = row - LANES // 2 + jnp.where(row < LANES, jnp.int16(0), jnp.int16(CZ - LANES))
     y_row = iota((ROWS, 128), 0)
     y_of_row = jnp.where(y_row < 12, y_row, y_row - ROWS)
     for copy in copies:
@@ -133,8 +131,8 @@
         edge = acc[g * group : (g + 1) * group, :]
         low = jnp.where(lane < LANES, edge, 0.0)
         high = jnp.where(lane >= LANES, edge, 0.0)
-        lower_out = lower_out + (pltpu.roll(low, g * LANES, 1) if g else low)
-        upper_out = upper_out + pltpu.roll(high, (g * LANES - LANES) % 128, 1)
+        lower_out = lower_out + pltpu.roll(low, (g * LANES - LANES // 2) % 128, 1)
+        upper_out = upper_out + pltpu.roll(high, (g * LANES - LANES // 2 - LANES) % 128, 1)
     even = lax.rem(lax.axis_index("gz"), 2) == 0
     z0_ref[...] = jnp.where(even, upper_out, lower_out)
     z1_ref[...] = jnp.where(even, lower_out, upper_out)
@@ -161,6 +159,7 @@
 def z_fold_kernel(tiles, group_planes, main_ref, z0_ref, z1_ref, got0_ref, got1_ref, out_ref, sent_ref):
     planes = tiles + EXT
     group = group_planes * ROWS
+    units = []
     even = lax.rem(lax.axis_index("gz"), 2) == 0
     z0, z1, got0, got1 = z0_ref[...], z1_ref[...], got0_ref[...], got1_ref[...]
     own_upper = jnp.where(even, z0, z1)
@@ -168,24 +167,35 @@
     right_lower = jnp.where(even, got0, got1)
     left_upper = jnp.where(even, got1, got0)
     lane = iota((group, 128), 1)
-    first = (lane & (LANES - 1)) < LANES // 2
+    first = ((lane + LANES // 2) & (LANES - 1)) >= LANES // 2
+    rim = (lane < LANES // 2) | (lane >= 128 - LANES // 2)
     halo = jnp.where(first, right_lower + own_upper, left_upper + own_lower)
     inner = jnp.where(first, left_upper, right_lower)
     for g in range(GROUPS):
         count = min(group, planes * ROWS - g * group)
-        low = pltpu.roll(inner, (-g * LANES) % 128, 1) if g else inner
-        high = pltpu.roll(inner, (128 - LANES - g * LANES) % 128, 1)
-        add = jnp.where(lane < LANES // 2, low, jnp.where(lane >= 128 - LANES // 2, high, 0.0))
+        add = jnp.where(rim, pltpu.roll(inner, (-g * LANES) % 128, 1) if g else inner, 0.0)
         total = main_ref[g * group : g * group + count, :] + add[:count]
         out_ref[g * group : g * group + count, :] = total
-        sent_ref[g * group : g * group + count, :] = total.astype(BF16)
+        units += [total[at : at + ROWS] for at in range(0, count, ROWS)]
     out_ref[planes * ROWS : planes * ROWS + group, :] = halo
-    sent_ref[planes * ROWS : planes * ROWS + group, :] = halo.astype(BF16)
-
-
-def y_fold_kernel(n_gy, units, tiles, group_planes, *refs):
+    units += [halo[at : at + ROWS] for at in range(0, group, ROWS)]
+    inner = [unit[:CY] for unit in units]
+    outer = [unit[CY:] for unit in units]
+    outer = [
+        pair[0] + pltpu.roll(pair[1], CY // 2, 0) if len(pair) > 1 else pair[0]
+        for pair in (outer[u : u + 2] for u in range(0, len(outer), 2))
+    ]
+    halves = inner + outer
+    halves += [jnp.zeros((CY, 128), F32)] * (len(halves) % 2)
+    for u in range(0, len(halves), 2):
+        sent_ref[u * CY : (u + 2) * CY, :] = jnp.concatenate(halves[u : u + 2], 0).astype(BF16)
+
+
+def y_fold_kernel(n_gy, units, tiles, *refs):
     sources, (out_ref, far_ref) = refs[:n_gy], refs[n_gy:]
     half = iota((CY, 128), 0) < CY // 2
+    filled = (iota((CY, 128), 0) < 2) | (iota((CY, 128), 0) == CY - 1)
+    values = [ref[...].astype(F32) for ref in sources]
     wide = n_gy * CY
     planes = tiles + EXT
     for u in range(units):
@@ -195,10 +205,16 @@
             b = b % n_gy
             blocks[b] = value if blocks[b] is None else blocks[b] + value
 
-        for b, ref in enumerate(sources):
-            both = ref[u * ROWS : (u + 1) * ROWS, :].astype(F32)
-            add(b, both[:CY])
-            rest = both[CY:]
+        for b, value in enumerate(values):
+            if b == 0:
+                first = value[u * ROWS : u * ROWS + CY]
+                rest = value[u * ROWS + CY : (u + 1) * ROWS]
+            else:
+                first = value[u * CY : (u + 1) * CY]
+                at = (units + u // 2) * CY
+                rest = value[at : at + CY]
+                rest = jnp.where(filled, pltpu.roll(rest, CY // 2, 0) if u % 2 else rest, 0.0)
+            add(b, first)
             if n_gy == 2:
                 add(b + 1, rest)
             else:
@@ -215,8 +231,8 @@
 
 def field_kernel(
     tiles, chunks, group_planes, wide, span,
-    own_ref, got1_ref, got3_ref, lower_ref, upper_ref, band_ref,
-    charge_ref, offset_ref, cell_ref, potential_ref, force_ref, window, samples,
+    own_ref, got1_ref, got3_ref, lower_ref, upper_ref, band_ref, y_ref,
+    charge_ref, offset_ref, cell_ref, potential_ref, force_ref, window, parts, samples,
 ):
     planes = tiles + EXT
     radius = span // 2
@@ -225,8 +241,9 @@
     right = jnp.where(even, got1, got3)
     left = jnp.where(even, got3, got1)
     own = own_ref[...]
+    margin = planes * wide
     lane = iota((wide, 128), 1)
-    margin = planes * wide
+    rim = (lane < LANES // 2) | (lane >= 128 - LANES // 2)
 
     def main(block, p):
         return block[p * wide : (p + 1) * wide].astype(F32)
@@ -234,9 +251,7 @@
     def edge(block, p, base=margin):
         g, q = divmod(p, group_planes)
         packed = block[base + q * wide : base + (q + 1) * wide].astype(F32)
-        low = pltpu.roll(packed, (-g * LANES) % 128, 1) if g else packed
-        high = pltpu.roll(packed, (128 - LANES - g * LANES) % 128, 1)
-        return jnp.where(lane < LANES // 2, low, jnp.where(lane >= 128 - LANES // 2, high, 0.0))
+        return pltpu.roll(packed, (-g * LANES) % 128, 1) if g else packed
 
     far_low, far_high = lower_ref[...], upper_ref[...]
     far_base = 2 * EXT * wide
@@ -253,63 +268,94 @@
         if 0 <= x - 3 * tiles < EXT:
             terms.append((main(far_high, x - 3 * tiles), edge(far_high, x - 3 * tiles, far_base)))
         window[x * wide : (x + 1) * wide, :128] = sum(a for a, _ in terms).astype(BF16)
-        window[x * wide : (x + 1) * wide, 128:] = sum(b for _, b in terms).astype(BF16)
-
-    band = band_ref[:, : span * wide]
-    for x in range(planes):
+        window[x * wide : (x + 1) * wide, 128:] = jnp.where(
+            rim, sum(b for _, b in terms), 0.0
+        ).astype(BF16)
+
+    taps = span * ROWS
+    for x in range(0, planes, AHEAD):
+        count = min(AHEAD, planes - x)
         part = jnp.dot(
-            band, window[x * wide : (x + span) * wide, :], preferred_element_type=F32
+            band_ref[: count * taps, : (span + count - 1) * wide],
+            window[x * wide : (x + span + count - 1) * wide, :],
+            preferred_element_type=F32,
         )
-        total = part[radius * ROWS : (radius + 1) * ROWS]
+        for n in range(count):
+            for k in range(span):
+                at = n * taps + k * ROWS
+                parts[k, (x + n) * TALL : (x + n + 1) * TALL, :] = part[at : at + TALL]
+    lane = iota((8, 128), 1)
+    for row in range(0, planes * TALL, 8):
+        total = parts[radius, row : row + 8, :128]
+        outside = [None] * 3
         for k in range(span):
-            if k != radius:
-                total = total + pltpu.roll(part[k * ROWS : (k + 1) * ROWS], (radius - k) % 256, 1)
-        if 1 <= x <= tiles:
-            potential_ref[x - 1] = total[:CY, :CZ]
-        for c in range(4):
-            moved = total if c == 1 else pltpu.roll(total, (1 - c) % 256, 1)
-            samples[c, x * ROWS : (x + 1) * ROWS, :] = moved[:, :128]
+            inner = parts[k, row : row + 8, :128]
+            outer = parts[k, row : row + 8, 128:]
+            step = radius - k
+            if step:
+                taken = lane >= 128 - step if step > 0 else lane < -step
+                total = total + pltpu.roll(jnp.where(taken, outer, inner), step % 128, 1)
+            for n, z in enumerate((-1, CZ, CZ + 1)):
+                at = z - step
+                value = inner if 0 <= at < CZ else outer
+                old = 0.0 if outside[n] is None else outside[n]
+                outside[n] = jnp.where(lane == at % 128, value, old)
+        below, above, beyond = (jnp.sum(v, axis=1, keepdims=True) for v in outside)
+        samples[0, row : row + 8, :] = jnp.where(lane == 0, below, pltpu.roll(total, 1, 1))
+        samples[1, row : row + 8, :] = total
+        samples[2, row : row + 8, :] = jnp.where(lane == CZ - 1, above, pltpu.roll(total, 127, 1))
+        samples[3, row : row + 8, :] = jnp.where(
+            lane == CZ - 1, beyond, jnp.where(lane == CZ - 2, above, pltpu.roll(total, 126, 1))
+        )
+    for x in range(tiles):
+        potential_ref[x] = samples[1, (x + 1) * TALL + 1 : (x + 1) * TALL + 1 + CY, :]
 
     rows_total = tiles * chunks
     per = 8 // chunks
+    pairs = tiles // per
     upper_half = [iota((8, 128), 0) >= chunks * h for h in range(per)]
-    for pair in range(tiles // per):
-        rows = pl.ds(pair * 8, 8)
-        charge = charge_ref[rows, :]
-        xv, xs = spline(offset_ref[pl.ds(pair * 8, 8), :])
-        yv, ys = spline(offset_ref[pl.ds(rows_total + pair * 8, 8), :])
-        zv, zs = spline(offset_ref[pl.ds(2 * rows_total + pair * 8, 8), :])
-        cy = cell_ref[pl.ds(pair * 8, 8), :] & (CY - 1)
-        cz = cell_ref[pl.ds(rows_total + pair * 8, 8), :] & (CZ - 1)
-        plain = [jnp.zeros((8, 128), F32) for _ in range(4)]
-        along_y = [jnp.zeros((8, 128), F32) for _ in range(4)]
-        along_z = [jnp.zeros((8, 128), F32) for _ in range(4)]
-        for y in range(-1, CY + 2):
-            distance = y + 1 - cy
-            y_value = pick(distance, yv)
-            y_slope = pick(distance, ys)
-            row = y % ROWS
-            for k in range(4):
-                value = jnp.zeros((8, 128), F32)
-                slope = jnp.zeros((8, 128), F32)
+    for p in range(pairs):
+        at = pl.ds(p * 8, 8)
+        cz = cell_ref[pl.ds(rows_total + p * 8, 8), :] & (CZ - 1)
+        zv, zs = spline(offset_ref[pl.ds(2 * rows_total + p * 8, 8), :])
+        xv, xs = spline(offset_ref[at, :])
+        force = [jnp.zeros((8, 128), F32)] * 3
+        for k in range(4):
+            plain = [jnp.zeros((8, 128), F32)] * 4
+            sloped = [jnp.zeros((8, 128), F32)] * 4
+            for y in range(TALL):
+                y_at = pl.ds((p * TALL + y) * 8, 8)
+                y_value = y_ref[0, y_at, :]
+                y_slope = y_ref[1, y_at, :]
                 for c in range(4):
                     source = None
                     for h in range(per):
-                        at = (pair * per + h + k) * ROWS + row
-                        line = jnp.broadcast_to(samples[c, at : at + 1, :], (8, 128))
+                        row = (p * per + k + h) * TALL + y
+                        line = jnp.broadcast_to(samples[c, row : row + 1, :], (8, 128))
                         source = line if h == 0 else jnp.where(upper_half[h], line, source)
                     picked = jnp.take_along_axis(source, cz, axis=1)
-                    value = value + zv[c] * picked
-                    slope = slope + zs[c] * picked
-                plain[k] = plain[k] + y_value * value
-                along_y[k] = along_y[k] + y_slope * value
-                along_z[k] = along_z[k] + y_value * slope
-        force_ref[0, rows, :] = -charge * sum(xs[k] * plain[k] for k in range(4))
-        force_ref[1, rows, :] = -charge * sum(xv[k] * along_y[k] for k in range(4))
-        force_ref[2, rows, :] = -charge * sum(xv[k] * along_z[k] for k in range(4))
-
-
-def band_kernel(wide, kernel_ref, out_ref, rows_ref):
+                    plain[c] = plain[c] + y_value * picked
+                    sloped[c] = sloped[c] + y_slope * picked
+            value = sum(zv[c] * plain[c] for c in range(4))
+            along_y = sum(zv[c] * sloped[c] for c in range(4))
+            along_z = sum(zs[c] * plain[c] for c in range(4))
+            force[0] = force[0] + xs[k] * value
+            force[1] = force[1] + xv[k] * along_y
+            force[2] = force[2] + xv[k] * along_z
+        charge = charge_ref[at, :]
+        for d in range(3):
+            force_ref[d, at, :] = -charge * force[d]
+
+
+def band_kernel(tiles, chunks, wide, kernel_ref, offset_ref, cell_ref, out_ref, y_ref, rows_ref):
+    rows_total = tiles * chunks
+    for p in range(rows_total // 8):
+        yv, ys = spline(offset_ref[pl.ds(rows_total + p * 8, 8), :])
+        cy = cell_ref[pl.ds(p * 8, 8), :] & (CY - 1)
+        for y in range(TALL):
+            at = pl.ds((p * TALL + y) * 8, 8)
+            y_ref[0, at, :] = pick(y - cy, yv)
+            y_ref[1, at, :] = pick(y - cy, ys)
     span = kernel_ref.shape[0]
     radius = span // 2
     columns = out_ref.shape[1]
@@ -337,9 +383,20 @@
                 pltpu.roll(base, (shift - wide) % columns, 1),
             )
         for tile in range(columns // 128):
-            rows_ref[tile, pl.ds(y % ROWS, span, stride=ROWS), :] = moved[:, tile * 128 : (tile + 1) * 128]
-    for tile in range(columns // 128):
-        out_ref[:, tile * 128 : (tile + 1) * 128] = rows_ref[tile].astype(BF16)
+            rows_ref[tile, pl.ds(y + 1, span, stride=ROWS), :] = moved[:, tile * 128 : (tile + 1) * 128]
+    taps = span * ROWS
+    for n in range(AHEAD):
+        for tile in range(columns // 128):
+            value = rows_ref[tile]
+            if n:
+                before = rows_ref[tile - 1] if tile else jnp.zeros_like(value)
+                shift = n * wide
+                value = jnp.where(
+                    iota(value.shape, 1) < shift,
+                    pltpu.roll(before, shift, 1),
+                    pltpu.roll(value, shift, 1),
+                )
+            out_ref[n * taps : (n + 1) * taps, tile * 128 : (tile + 1) * 128] = value.astype(BF16)
 
 
 def vmem(n):
@@ -356,7 +413,7 @@
     group_planes = -(-planes // GROUPS)
     group = group_planes * ROWS
     wide = n_gy * CY
-    band_columns = -(-span * wide // 128) * 128
+    band_columns = -(-(span + AHEAD - 1) * wide // 128) * 128
     charge = charges.reshape(rows, 128)
     offset = offsets.reshape(3 * rows, 128)
     cell = cells.reshape(2 * rows, 128)
@@ -403,7 +460,7 @@
     units = planes + group_planes
     block, sent = pl.pallas_call(
         functools.partial(z_fold_kernel, tiles, group_planes),
-        out_shape=(shape(units * ROWS, 128), shape(units * ROWS, 128, kind=BF16)),
+        out_shape=(shape(units * ROWS, 128), shape(-(-(units + -(-units // 2)) // 2) * 2 * CY, 128, kind=BF16)),
         in_specs=vmem(5),
         out_specs=tuple(vmem(2)),
         compiler_params=pltpu.CompilerParams(vmem_limit_bytes=4 << 20),
@@ -411,7 +468,7 @@
     )(main, z0, z1, got0, got1)
     sources = [block] + [lax.ppermute(sent, "gy", shift(n_gy, -s)) for s in range(1, n_gy)]
     mine, far = pl.pallas_call(
-        functools.partial(y_fold_kernel, n_gy, units, tiles, group_planes),
+        functools.partial(y_fold_kernel, n_gy, units, tiles),
         out_shape=(shape(units * wide, 128, kind=BF16), shape((2 * EXT + group_planes) * wide, 128, kind=BF16)),
         in_specs=vmem(n_gy),
         out_specs=tuple(vmem(2)),
@@ -419,33 +476,37 @@
         name="y_fold",
     )(*sources)
     x1 = lax.ppermute(mine, "gx", near(n_gx))
-    if n_gx == 4:
-        lower = upper = lax.ppermute(far, "gx", shift(n_gx, 2))
-    else:
-        lower = lax.ppermute(far, "gx", shift(n_gx, 2))
+    lower = lax.ppermute(far, "gx", shift(n_gx, 2))
+    upper = lower
+    if n_gx != 4:
         upper = lax.ppermute(far, "gx", shift(n_gx, -2))
     x3 = lax.ppermute(mine, "gx", other(n_gx))
-    band = pl.pallas_call(
-        functools.partial(band_kernel, wide),
-        out_shape=shape(span * ROWS, band_columns, kind=BF16),
-        in_specs=vmem(1),
-        out_specs=vmem(1)[0],
+    band, y_dense = pl.pallas_call(
+        functools.partial(band_kernel, tiles, chunks, wide),
+        out_shape=(
+            shape(AHEAD * span * ROWS, band_columns, kind=BF16),
+            shape(2, rows * TALL, 128),
+        ),
+        in_specs=vmem(3),
+        out_specs=tuple(vmem(2)),
         scratch_shapes=[pltpu.VMEM((band_columns // 128, span * ROWS, 128), F32)],
         compiler_params=pltpu.CompilerParams(vmem_limit_bytes=8 << 20),
+        cost_estimate=pl.CostEstimate(flops=400_000_000, bytes_accessed=2_000_000, transcendentals=0),
         name="band",
-    )(kernel)
+    )(kernel, offset, cell)
     potential, forces = pl.pallas_call(
         functools.partial(field_kernel, tiles, chunks, group_planes, wide, span),
         out_shape=(shape(tiles, CY, CZ), shape(3, rows, 128)),
-        in_specs=vmem(9),
+        in_specs=vmem(10),
         out_specs=tuple(vmem(2)),
         scratch_shapes=[
             pltpu.VMEM(((2 * (span // 2) + planes) * wide, 256), BF16),
-            pltpu.VMEM((4, planes * ROWS, 128), F32),
+            pltpu.VMEM((span, -(-planes * TALL // 8) * 8, 256), F32),
+            pltpu.VMEM((4, -(-planes * TALL // 8) * 8, 128), F32),
         ],
         compiler_params=pltpu.CompilerParams(vmem_limit_bytes=16 << 20),
         name="field",
-    )(mine, x1, x3, lower, upper, band, charge, offset, cell)
+    )(mine, x1, x3, lower, upper, band, y_dense, charge, offset, cell)
     return potential, forces.reshape(3, tiles, 1, 1, slots)
 
 

time: 24.6 us -> 24.2 us (0.984)
  waiting for transfers between devices: 7.58 us -> 7.12 us
  Pallas kernels: 6.6 us -> 6.85 us
    pallas_call x2, Pallas kernels: 0.63 us -> 1.01 us  [the longest x1 0.99 us: local(): pl.pallas_call(functools.partial(band_kernel, tiles, chunks, wide), out_s...]
    ppermute x1, waiting for transfers between devices: 4.44 us -> 4.13 us  [local(): lower = lax.ppermute(far, 'gx', shift(n_gx, 2))]
  transfers between devices with their start and end apart: 6 -> 6, of which waited for: 3 -> 3; matrix products, arithmetic and copies ran while one was open for 0% -> 0% of each run, Pallas kernels for 6% -> 8%
where the time goes in v2:
time: 24.2 us; the launch traced here: 24 us
  starting transfers between devices  9.32 us (39%)
  waiting for transfers between devices  7.12 us (29%)
  Pallas kernels  6.85 us (28%)
  between operations  0.68 us (3%)
    ppermute x1, waiting for transfers between devices, local(): lower = lax.ppermute(far, 'gx', shift(n_gx, 2))  4.13 us
    pallas_call x1, Pallas kernels, local(): pl.pallas_call(functools.partial(field_kernel, tiles, chunks, group_plane...  2.96 us
    ppermute x1, starting transfers between devices, local(): got1 = lax.ppermute(z1, 'gz', other(n_gz))  2.61 us
    ppermute x1, starting transfers between devices, local(): x3 = lax.ppermute(mine, 'gx', other(n_gx))  2.48 us
    ppermute x1, waiting for transfers between devices, local(): lax.ppermute(sent, 'gy', shift(n_gy, -s))  2.37 us
    pallas_call x1, Pallas kernels, local(): pl.pallas_call(functools.partial(edge_kernel, tiles, chunks, group_planes...  1.89 us
    ppermute x1, starting transfers between devices, local(): x1 = lax.ppermute(mine, 'gx', near(n_gx))  1.82 us
    ppermute x1, starting transfers between devices, local(): lax.ppermute(sent, 'gy', shift(n_gy, -s))  1.74 us
  transfers between devices with their start and end apart: 6, of which 3 were waited for; matrix products, arithmetic and copies ran while one was open for 0% of the time, Pallas kernels for 8%

profile of v2, /device:TPU:0, one launch (start us, length us, event | category | flops | bytes accessed | tf_op | source)
XLA Modules:
  0.0 24.0 jit_solution(3108631501501014503)
XLA Ops:
  0.6 1.9 %edge.1 = (f32[48,128]{1,0:T(8,128)S(1)}, f32[48,128]{1,0:T(8,128)S(1)}, bf16[512,512]{1,0:T(8,128)(2,1)S(1)}, bf16[512,512]{1,0:T(8,128)(2,1)S(1)}, f32[8,32,128]{2,1,0:T(8,128)S(1)}, /*index=5*/s32[32,128]{1,0:T(8,128)S(1)}) custom-call(f32[32,128]{1,0:T(8,128)} %bitcast.10, f32[96,128]{1,0:T(8,128)} %bitcast.4, s32[64,128]{1,0:T(8,128)} %bitcast.7), custom_call_target="tpu_custom_call" | custom-call | tf_op jit(solution)/shard_map/edge/pallas_call | solution.py:428
  2.5 0.6 %collective-permute-start = (f32[48,128]{1,0:T(8,128)S(1)}, f32[48,128]{1,0:T(8,128)S(1)}, u32[]{:S(2)}, u32[]{:S(2)}) collective-permute-start(f32[48,128]{1,0:T(8,128)S(1)} %get-tuple-element.20.z0_ref), channel_id=1, source_target_pairs={{0,1},{1,0},{2,3},{3,2},{4,5},{5,4},{6,7},{7,6},{8,9},{9,8},{10,11... | collective-permute-start | bytes 73736 | tf_op jit(solution)/shard_map/ppermute | solution.py:449
  3.1 2.6 %collective-permute-start.1 = (f32[48,128]{1,0:T(8,128)S(1)}, f32[48,128]{1,0:T(8,128)S(1)}, u32[]{:S(2)}, u32[]{:S(2)}) collective-permute-start(f32[48,128]{1,0:T(8,128)S(1)} %get-tuple-element.21.z1_ref), channel_id=1, source_target_pairs={{0,3},{1,2},{2,1},{3,0},{4,7},{5,6},{6,5},{7,4},{8,11},{9,10},{10,... | collective-permute-start | bytes 73736 | tf_op jit(solution)/shard_map/ppermute | solution.py:450
  5.7 0.9 %spread.1.main_ref = f32[176,128]{1,0:T(8,128)S(1)} custom-call(bf16[512,512]{1,0:T(8,128)(2,1)S(1)} %get-tuple-element.16.high_ref, bf16[512,512]{1,0:T(8,128)(2,1)S(1)} %get-tuple-element.17.low_ref, f32[8,32,128]{2,1,0:T(8,128)S(1)} %get-tuple-element.18.weight_ref, s32[32,128]{1,0:T(8,128)S(1)} %get-tuple-element.19.cell_ref), custom_call_target="tpu_custom_call" | custom-call | flops 400000000 | bytes 2000000 | tf_op jit(solution)/shard_map/spread/pallas_call | solution.py:451
  6.6 0.0 collective-permute-done.got0_ref
  6.6 0.6 %collective-permute-done.1.got1_ref = f32[48,128]{1,0:T(8,128)S(1)} collective-permute-done((f32[48,128]{1,0:T(8,128)S(1)}, f32[48,128]{1,0:T(8,128)S(1)}, u32[]{:S(2)}, u32[]{:S(2)}) %collective-permute-start.1) | collective-permute-done | bytes 24608 | tf_op jit(solution)/shard_map/ppermute | solution.py:450
  7.2 0.0 copy-start.3
  7.2 0.1 z_fold.1
  7.3 1.7 %collective-permute-start.2 = (bf16[176,128]{1,0:T(8,128)(2,1)S(1)}, bf16[176,128]{1,0:T(8,128)(2,1)S(1)}, u32[]{:S(2)}, u32[]{:S(2)}) collective-permute-start(bf16[176,128]{1,0:T(8,128)(2,1)S(1)} %get-tuple-element.23), channel_id=1, source_target_pairs={{0,4},{4,0},{1,5},{5,1},{2,6},{6,2},{3,7},{7,3},{8,12},{12,8},{9,1... | collective-permute-start | bytes 135176 | tf_op jit(solution)/shard_map/ppermute | solution.py:469
  9.1 2.4 %collective-permute-done.2.refs_1_ = bf16[176,128]{1,0:T(8,128)(2,1)S(1)} collective-permute-done((bf16[176,128]{1,0:T(8,128)(2,1)S(1)}, bf16[176,128]{1,0:T(8,128)(2,1)S(1)}, u32[]{:S(2)}, u32[]{:S(2)}) %collective-permute-start.2) | collective-permute-done | bytes 45088 | tf_op jit(solution)/shard_map/ppermute | solution.py:469
  11.4 0.0 copy-start
  11.4 0.0 copy-start.1
  11.5 1.8 %collective-permute-start.3 = (bf16[224,128]{1,0:T(8,128)(2,1)S(1)}, bf16[224,128]{1,0:T(8,128)(2,1)S(1)}, u32[]{:S(2)}, u32[]{:S(2)}) collective-permute-start(bf16[224,128]{1,0:T(8,128)(2,1)S(1)} %get-tuple-element.24.own_ref), channel_id=1, source_target_pairs={{0,8},{8,0},{16,24},{24,16},{1,9},{9,1},{17,25},{25,17},{2,10},{10... | collective-permute-start | bytes 172040 | tf_op jit(solution)/shard_map/ppermute | solution.py:478
  13.3 2.5 %collective-permute-start.4 = (bf16[224,128]{1,0:T(8,128)(2,1)S(1)}, bf16[224,128]{1,0:T(8,128)(2,1)S(1)}, u32[]{:S(2)}, u32[]{:S(2)}) collective-permute-start(bf16[224,128]{1,0:T(8,128)(2,1)S(1)} %get-tuple-element.24.own_ref), channel_id=1, source_target_pairs={{0,24},{8,16},{16,8},{24,0},{1,25},{9,17},{17,9},{25,1},{2,26},{10... | collective-permute-start | bytes 172040 | tf_op jit(solution)/shard_map/ppermute | solution.py:483
  15.8 0.1 collective-permute-start.5
  15.9 0.0 copy-done.3
  15.9 0.0 copy-done
  15.9 0.0 copy-done.1
  15.9 1.0 %band.1 = (bf16[1088,384]{1,0:T(8,128)(2,1)S(1)}, f32[2,352,128]{2,1,0:T(8,128)S(1)}) custom-call(bf16[17,17,17]{2,1,0:T(8,128)(2,1)S(1)} %copy-done.3, f32[96,128]{1,0:T(8,128)S(1)} %bitcast.5, s32[64,128]{1,0:T(8,128)S(1)} %bitcast.8), custom_call_target="tpu_custom_call" | custom-call | flops 400000000 | bytes 2000000 | tf_op jit(solution)/shard_map/band/pallas_call | solution.py:484
  16.9 4.1 %collective-permute-done.5.lower_ref.upper_ref = bf16[144,128]{1,0:T(8,128)(2,1)S(1)} collective-permute-done((bf16[144,128]{1,0:T(8,128)(2,1)S(1)}, bf16[144,128]{1,0:T(8,128)(2,1)S(1)}, u32[]{:S(2)}, u32[]{:S(2)}) %collective-permute-start.5) | collective-permute-done | bytes 36896 | tf_op jit(solution)/shard_map/ppermute | solution.py:479
  21.0 0.0 collective-permute-done.3.got1_ref
  21.0 0.0 collective-permute-done.4.got3_ref
  21.0 0.0 copy-done.2
  21.0 3.0 %field.1 = (f32[8,8,128]{2,1,0:T(8,128)}, f32[3,32,128]{2,1,0:T(8,128)}) custom-call(bf16[224,128]{1,0:T(8,128)(2,1)S(1)} %get-tuple-element.24.own_ref, bf16[224,128]{1,0:T(8,128)(2,1)S(1)} %collective-permute-done.3.got1_ref, bf16[224,128]{1,0:T(8,128)(2,1)S(1)} %collective-permute-done.4.got3_ref, ...), custom_call_target="tpu_custom_call" | custom-call | tf_op jit(solution)/shard_map/field/pallas_call | solution.py:497
  (2 shorter events, 0.0 us)
Async XLA Ops:
  2.5 4.1 %collective-permute-start = (f32[48,128]{1,0:T(8,128)S(1)}, f32[48,128]{1,0:T(8,128)S(1)}, u32[]{:S(2)}, u32[]{:S(2)}) collective-permute-start(f32[48,128]{1,0:T(8,128)S(1)} %get-tuple-element.20.z0_ref), channel_id=1, source_target_pairs={{0,1},{1,0},{2,3},{3,2},{4,5},{5,4},{6,7},{7,6},{8,9},{9,8},{10,11... | collective-permute-start | bytes 73736 | tf_op jit(solution)/shard_map/ppermute | solution.py:449
  3.1 4.1 %collective-permute-start.1 = (f32[48,128]{1,0:T(8,128)S(1)}, f32[48,128]{1,0:T(8,128)S(1)}, u32[]{:S(2)}, u32[]{:S(2)}) collective-permute-start(f32[48,128]{1,0:T(8,128)S(1)} %get-tuple-element.21.z1_ref), channel_id=1, source_target_pairs={{0,3},{1,2},{2,1},{3,0},{4,7},{5,6},{6,5},{7,4},{8,11},{9,10},{10,... | collective-permute-start | bytes 73736 | tf_op jit(solution)/shard_map/ppermute | solution.py:450
  7.2 8.7 %copy-start.3 = (bf16[17,17,17]{2,1,0:T(8,128)(2,1)S(1)}, bf16[17,17,17]{2,1,0:T(8,128)(2,1)}, u32[]{:S(2)}) copy-start(bf16[17,17,17]{2,1,0:T(8,128)(2,1)} %kernel_ref.1) | copy-start | bytes 29482
  7.3 4.1 %collective-permute-start.2 = (bf16[176,128]{1,0:T(8,128)(2,1)S(1)}, bf16[176,128]{1,0:T(8,128)(2,1)S(1)}, u32[]{:S(2)}, u32[]{:S(2)}) collective-permute-start(bf16[176,128]{1,0:T(8,128)(2,1)S(1)} %get-tuple-element.23), channel_id=1, source_target_pairs={{0,4},{4,0},{1,5},{5,1},{2,6},{6,2},{3,7},{7,3},{8,12},{12,8},{9,1... | collective-permute-start | bytes 135176 | tf_op jit(solution)/shard_map/ppermute | solution.py:469
  11.4 4.4 %copy-start = (f32[3,8,1,1,512]{4,3,2,1,0:T(1,128)S(1)}, f32[3,8,1,1,512]{4,3,2,1,0:T(1,128)}, u32[]{:S(2)}) copy-start(f32[3,8,1,1,512]{4,3,2,1,0:T(1,128)} %param.5) | copy-start | bytes 147460
  11.4 4.4 %copy-start.1 = (s32[2,8,1,1,512]{4,3,2,1,0:T(1,128)S(1)}, s32[2,8,1,1,512]{4,3,2,1,0:T(1,128)}, u32[]{:S(2)}) copy-start(s32[2,8,1,1,512]{4,3,2,1,0:T(1,128)} %param.6) | copy-start | bytes 98308
  11.5 9.6 %collective-permute-start.3 = (bf16[224,128]{1,0:T(8,128)(2,1)S(1)}, bf16[224,128]{1,0:T(8,128)(2,1)S(1)}, u32[]{:S(2)}, u32[]{:S(2)}) collective-permute-start(bf16[224,128]{1,0:T(8,128)(2,1)S(1)} %get-tuple-element.24.own_ref), channel_id=1, source_target_pairs={{0,8},{8,0},{16,24},{24,16},{1,9},{9,1},{17,25},{25,17},{2,10},{10... | collective-permute-start | bytes 172040 | tf_op jit(solution)/shard_map/ppermute | solution.py:478
  13.3 7.7 %collective-permute-start.4 = (bf16[224,128]{1,0:T(8,128)(2,1)S(1)}, bf16[224,128]{1,0:T(8,128)(2,1)S(1)}, u32[]{:S(2)}, u32[]{:S(2)}) collective-permute-start(bf16[224,128]{1,0:T(8,128)(2,1)S(1)} %get-tuple-element.24.own_ref), channel_id=1, source_target_pairs={{0,24},{8,16},{16,8},{24,0},{1,25},{9,17},{17,9},{25,1},{2,26},{10... | collective-permute-start | bytes 172040 | tf_op jit(solution)/shard_map/ppermute | solution.py:483
  15.8 5.3 %copy-start.2 = (f32[8,1,1,512]{3,2,1,0:T(1,128)S(1)}, f32[8,1,1,512]{3,2,1,0:T(1,128)}, u32[]{:S(2)}) copy-start(f32[8,1,1,512]{3,2,1,0:T(1,128)} %param.4) | copy-start | bytes 49156
  15.8 5.3 %collective-permute-start.5 = (bf16[144,128]{1,0:T(8,128)(2,1)S(1)}, bf16[144,128]{1,0:T(8,128)(2,1)S(1)}, u32[]{:S(2)}, u32[]{:S(2)}) collective-permute-start(bf16[144,128]{1,0:T(8,128)(2,1)S(1)} %get-tuple-element.25), channel_id=1, source_target_pairs={{0,16},{8,24},{16,0},{24,8},{1,17},{9,25},{17,1},{25,9},{2,18},{10... | collective-permute-start | bytes 110600 | tf_op jit(solution)/shard_map/ppermute | solution.py:479

commit v3 on v2

--- a/solution.py
+++ b/solution.py
@@ -14,6 +14,7 @@
 ROWS = 16
 TALL = CY + EXT
 AHEAD = 4
+STEP = -(-AHEAD * TALL // 8) * 8
 LANES = 32
 GROUPS = 128 // LANES
 
@@ -88,8 +89,8 @@
         copy.start()
     rows = tiles * chunks
     acc[...] = jnp.zeros_like(acc)
-    row = iota((2 * LANES, 128), 0, jnp.int16)
-    z_of_row = row - LANES // 2 + jnp.where(row < LANES, jnp.int16(0), jnp.int16(CZ - LANES))
+    row = iota((LANES, 128), 0, jnp.int16)
+    z_of_row = jnp.where(row < LANES // 2, row - 1, row + (CZ + 2 - LANES // 2 - 11))
     y_row = iota((ROWS, 128), 0)
     y_of_row = jnp.where(y_row < 12, y_row, y_row - ROWS)
     for copy in copies:
@@ -122,20 +123,20 @@
         low_ref[t * 4 * ROWS : (t + 1) * 4 * ROWS, :] = s_low
         both = nt_dot(jnp.concatenate([s_high, s_low], 0), z_high)
         got = both[: 4 * ROWS] + both[4 * ROWS :] + nt_dot(s_high, z_low)
-        acc[t * ROWS : (t + 4) * ROWS, : 2 * LANES] += got
+        acc[t * ROWS : (t + 4) * ROWS, :LANES] += got
     group = group_planes * ROWS
     lane = iota((group, 128), 1)
     lower_out = jnp.zeros((group, 128), F32)
     upper_out = jnp.zeros((group, 128), F32)
     for g in range(GROUPS):
         edge = acc[g * group : (g + 1) * group, :]
-        low = jnp.where(lane < LANES, edge, 0.0)
-        high = jnp.where(lane >= LANES, edge, 0.0)
-        lower_out = lower_out + pltpu.roll(low, (g * LANES - LANES // 2) % 128, 1)
-        upper_out = upper_out + pltpu.roll(high, (g * LANES - LANES // 2 - LANES) % 128, 1)
+        low = jnp.where(lane < LANES // 2, edge, 0.0)
+        high = jnp.where(lane >= LANES // 2, edge, 0.0)
+        lower_out = lower_out + pltpu.roll(low, (g * LANES - 1) % 128, 1)
+        upper_out = upper_out + pltpu.roll(high, (g * LANES - LANES // 2 - 9) % 128, 1)
     even = lax.rem(lax.axis_index("gz"), 2) == 0
-    z0_ref[...] = jnp.where(even, upper_out, lower_out)
-    z1_ref[...] = jnp.where(even, lower_out, upper_out)
+    z0_ref[...] = jnp.where(even, upper_out, lower_out).astype(BF16)
+    z1_ref[...] = jnp.where(even, lower_out, upper_out).astype(BF16)
 
 
 def spread_kernel(tiles, chunks, high_ref, low_ref, weight_ref, cell_ref, main_ref):
@@ -161,7 +162,7 @@
     group = group_planes * ROWS
     units = []
     even = lax.rem(lax.axis_index("gz"), 2) == 0
-    z0, z1, got0, got1 = z0_ref[...], z1_ref[...], got0_ref[...], got1_ref[...]
+    z0, z1, got0, got1 = (ref[...].astype(F32) for ref in (z0_ref, z1_ref, got0_ref, got1_ref))
     own_upper = jnp.where(even, z0, z1)
     own_lower = jnp.where(even, z1, z0)
     right_lower = jnp.where(even, got0, got1)
@@ -192,7 +193,7 @@
 
 
 def y_fold_kernel(n_gy, units, tiles, *refs):
-    sources, (out_ref, far_ref) = refs[:n_gy], refs[n_gy:]
+    sources, (out_ref, far_ref, exact_ref) = refs[:n_gy], refs[n_gy:]
     half = iota((CY, 128), 0) < CY // 2
     filled = (iota((CY, 128), 0) < 2) | (iota((CY, 128), 0) == CY - 1)
     values = [ref[...].astype(F32) for ref in sources]
@@ -220,18 +221,76 @@
             else:
                 add(b + 1, jnp.where(half, rest, 0.0))
                 add(b - 1, jnp.where(half, 0.0, rest))
-        value = jnp.concatenate(blocks, 0).astype(BF16)
+        exact = jnp.concatenate(blocks, 0)
+        value = exact.astype(BF16)
         out_ref[u * wide : (u + 1) * wide, :] = value
-        if u < EXT:
-            far_ref[u * wide : (u + 1) * wide, :] = value
-        elif planes - EXT <= u:
-            v = u - (planes - EXT) + EXT
+        if u < EXT or planes - EXT <= u:
+            v = u if u < EXT else u - planes + 2 * EXT
             far_ref[v * wide : (v + 1) * wide, :] = value
+            exact_ref[v * wide : (v + 1) * wide, :] = exact
+
+
+def along_z_taps(parts, row, radius):
+    lane = iota((8, 128), 1)
+    total = parts[radius, row : row + 8, :128]
+    outside = [jnp.zeros((8, 128), F32)] * 3
+    for k in range(2 * radius + 1):
+        inner = parts[k, row : row + 8, :128]
+        outer = parts[k, row : row + 8, 128:]
+        step = radius - k
+        if step:
+            taken = lane >= 128 - step if step > 0 else lane < -step
+            total = total + pltpu.roll(jnp.where(taken, outer, inner), step % 128, 1)
+        for n, z in enumerate((-1, CZ, CZ + 1)):
+            at = z - step
+            value = inner if 0 <= at < CZ else outer
+            outside[n] = jnp.where(lane == at % 128, value, outside[n])
+    return total, [jnp.sum(v, axis=1, keepdims=True) for v in outside]
+
+
+def rim_of(block, base, p, wide, group_planes):
+    g, q = divmod(p, group_planes)
+    packed = block[base + q * wide : base + (q + 1) * wide].astype(F32)
+    return pltpu.roll(packed, (-g * LANES) % 128, 1) if g else packed
+
+
+def own_kernel(tiles, group_planes, wide, span, own_ref, band_ref, total_ref, outside_ref, window, parts):
+    planes = tiles + EXT
+    radius = span // 2
+    alone = tiles - EXT
+    own = own_ref[...]
+    lane = iota((wide, 128), 1)
+    rim = (lane < LANES // 2) | (lane >= 128 - LANES // 2)
+    for n in range(alone):
+        rows = slice(n * wide, (n + 1) * wide)
+        p = EXT + n
+        window[rows, :128] = own[p * wide : (p + 1) * wide]
+        edge = rim_of(own, planes * wide, p, wide, group_planes)
+        window[rows, 128:] = jnp.where(rim, edge, 0.0).astype(BF16)
+    for x in range(0, planes, AHEAD):
+        first = (radius + EXT - x) * wide
+        part = jnp.dot(
+            band_ref[:, first : first + alone * wide], window[...], preferred_element_type=F32
+        )
+        at = row_of(x)
+        for k in range(span):
+            parts[k, at : at + STEP, :] = part[k * STEP : (k + 1) * STEP]
+    lane = iota((8, 128), 1)
+    for row in range(0, row_of(planes - 1) + TALL, 8):
+        total, outside = along_z_taps(parts, row, radius)
+        total_ref[row : row + 8, :] = total
+        outside_ref[row : row + 8, :] = jnp.where(
+            lane == 0, outside[0], jnp.where(lane == 1, outside[1], outside[2])
+        )
+
+
+def row_of(x):
+    return x // AHEAD * STEP + x % AHEAD * TALL
 
 
 def field_kernel(
     tiles, chunks, group_planes, wide, span,
-    own_ref, got1_ref, got3_ref, lower_ref, upper_ref, band_ref, y_ref,
+    own_ref, got1_ref, got3_ref, lower_ref, upper_ref, band_ref, total_ref, outside_ref, y_ref,
     charge_ref, offset_ref, cell_ref, potential_ref, force_ref, window, parts, samples,
 ):
     planes = tiles + EXT
@@ -242,6 +301,7 @@
     left = jnp.where(even, got3, got1)
     own = own_ref[...]
     margin = planes * wide
+    far_base = 2 * EXT * wide
     lane = iota((wide, 128), 1)
     rim = (lane < LANES // 2) | (lane >= 128 - LANES // 2)
 
@@ -249,58 +309,52 @@
         return block[p * wide : (p + 1) * wide].astype(F32)
 
     def edge(block, p, base=margin):
-        g, q = divmod(p, group_planes)
-        packed = block[base + q * wide : base + (q + 1) * wide].astype(F32)
-        return pltpu.roll(packed, (-g * LANES) % 128, 1) if g else packed
+        return rim_of(block, base, p, wide, group_planes)
 
     far_low, far_high = lower_ref[...], upper_ref[...]
-    far_base = 2 * EXT * wide
+    start, stop = radius + EXT, radius + tiles
+    place = 0
     for x in range(2 * radius + planes):
+        if start <= x < stop:
+            continue
         terms = []
         if x < planes:
             terms.append((main(left, x), edge(left, x)))
         if 0 <= x - tiles < planes:
-            terms.append((main(own, x - tiles), edge(own, x - tiles)))
+            p = x - tiles
+            v = p if p < EXT else p - planes + 2 * EXT
+            terms.append((main(own, v), edge(own, p, far_base)))
         if 0 <= x - 2 * tiles < planes:
             terms.append((main(right, x - 2 * tiles), edge(right, x - 2 * tiles)))
         if x < EXT:
             terms.append((main(far_low, EXT + x), edge(far_low, planes - EXT + x, far_base)))
         if 0 <= x - 3 * tiles < EXT:
             terms.append((main(far_high, x - 3 * tiles), edge(far_high, x - 3 * tiles, far_base)))
-        window[x * wide : (x + 1) * wide, :128] = sum(a for a, _ in terms).astype(BF16)
-        window[x * wide : (x + 1) * wide, 128:] = jnp.where(
+        rows = slice(place * wide, (place + 1) * wide)
+        place += 1
+        window[rows, :128] = sum(a for a, _ in terms).astype(BF16)
+        window[rows, 128:] = jnp.where(
             rim, sum(b for _, b in terms), 0.0
         ).astype(BF16)
 
-    taps = span * ROWS
     for x in range(0, planes, AHEAD):
         count = min(AHEAD, planes - x)
+        used = span + count - 1 - (stop - start)
         part = jnp.dot(
-            band_ref[: count * taps, : (span + count - 1) * wide],
-            window[x * wide : (x + span + count - 1) * wide, :],
+            band_ref[x // AHEAD, :, : used * wide],
+            window[x * wide : (x + used) * wide, :],
             preferred_element_type=F32,
         )
-        for n in range(count):
-            for k in range(span):
-                at = n * taps + k * ROWS
-                parts[k, (x + n) * TALL : (x + n + 1) * TALL, :] = part[at : at + TALL]
+        at = row_of(x)
+        for k in range(span):
+            parts[k, at : at + STEP, :] = part[k * STEP : (k + 1) * STEP]
     lane = iota((8, 128), 1)
-    for row in range(0, planes * TALL, 8):
-        total = parts[radius, row : row + 8, :128]
-        outside = [None] * 3
-        for k in range(span):
-            inner = parts[k, row : row + 8, :128]
-            outer = parts[k, row : row + 8, 128:]
-            step = radius - k
-            if step:
-                taken = lane >= 128 - step if step > 0 else lane < -step
-                total = total + pltpu.roll(jnp.where(taken, outer, inner), step % 128, 1)
-            for n, z in enumerate((-1, CZ, CZ + 1)):
-                at = z - step
-                value = inner if 0 <= at < CZ else outer
-                old = 0.0 if outside[n] is None else outside[n]
-                outside[n] = jnp.where(lane == at % 128, value, old)
-        below, above, beyond = (jnp.sum(v, axis=1, keepdims=True) for v in outside)
+    for row in range(0, row_of(planes - 1) + TALL, 8):
+        total, outside = along_z_taps(parts, row, radius)
+        total = total + total_ref[row : row + 8, :]
+        below, above, beyond = (
+            v + outside_ref[row : row + 8, n : n + 1] for n, v in enumerate(outside)
+        )
         samples[0, row : row + 8, :] = jnp.where(lane == 0, below, pltpu.roll(total, 1, 1))
         samples[1, row : row + 8, :] = total
         samples[2, row : row + 8, :] = jnp.where(lane == CZ - 1, above, pltpu.roll(total, 127, 1))
@@ -308,7 +362,7 @@
             lane == CZ - 1, beyond, jnp.where(lane == CZ - 2, above, pltpu.roll(total, 126, 1))
         )
     for x in range(tiles):
-        potential_ref[x] = samples[1, (x + 1) * TALL + 1 : (x + 1) * TALL + 1 + CY, :]
+        potential_ref[x] = samples[1, row_of(x + 1) + 1 : row_of(x + 1) + 1 + CY, :]
 
     rows_total = tiles * chunks
     per = 8 // chunks
@@ -330,7 +384,7 @@
                 for c in range(4):
                     source = None
                     for h in range(per):
-                        row = (p * per + k + h) * TALL + y
+                        row = row_of(p * per + k + h) + y
                         line = jnp.broadcast_to(samples[c, row : row + 1, :], (8, 128))
                         source = line if h == 0 else jnp.where(upper_half[h], line, source)
                     picked = jnp.take_along_axis(source, cz, axis=1)
@@ -347,7 +401,7 @@
             force_ref[d, at, :] = -charge * force[d]
 
 
-def band_kernel(tiles, chunks, wide, kernel_ref, offset_ref, cell_ref, out_ref, y_ref, rows_ref):
+def band_kernel(tiles, chunks, wide, kernel_ref, offset_ref, cell_ref, out_ref, other_ref, y_ref, rows_ref):
     rows_total = tiles * chunks
     for p in range(rows_total // 8):
         yv, ys = spline(offset_ref[pl.ds(rows_total + p * 8, 8), :])
@@ -382,21 +436,20 @@
                 pltpu.roll(base, shift, 1),
                 pltpu.roll(base, (shift - wide) % columns, 1),
             )
-        for tile in range(columns // 128):
-            rows_ref[tile, pl.ds(y + 1, span, stride=ROWS), :] = moved[:, tile * 128 : (tile + 1) * 128]
-    taps = span * ROWS
-    for n in range(AHEAD):
-        for tile in range(columns // 128):
-            value = rows_ref[tile]
-            if n:
-                before = rows_ref[tile - 1] if tile else jnp.zeros_like(value)
-                shift = n * wide
-                value = jnp.where(
-                    iota(value.shape, 1) < shift,
-                    pltpu.roll(before, shift, 1),
-                    pltpu.roll(value, shift, 1),
-                )
-            out_ref[n * taps : (n + 1) * taps, tile * 128 : (tile + 1) * 128] = value.astype(BF16)
+        for n in range(AHEAD):
+            there = pltpu.roll(moved, n * wide, 1) if n else moved
+            for tile in range(columns // 128):
+                at = pl.ds(n * TALL + y + 1, span, stride=STEP)
+                rows_ref[tile, at, :] = there[:, tile * 128 : (tile + 1) * 128]
+    alone = (tiles - EXT) * wide
+    whole = jnp.concatenate([rows_ref[tile] for tile in range(columns // 128)], 1)
+    out_ref[...] = whole.astype(BF16)
+    kept = other_ref.shape[2]
+    moved = pltpu.roll(whole, columns - alone, 1)[:, :kept]
+    lane = iota(moved.shape, 1)
+    for n in range(other_ref.shape[0]):
+        first = (radius + EXT - n * AHEAD) * wide
+        other_ref[n] = jnp.where(lane < first, whole[:, :kept], moved).astype(BF16)
 
 
 def vmem(n):
@@ -428,7 +481,7 @@
     z0, z1, s_high, s_low, weights, z_cell = pl.pallas_call(
         functools.partial(edge_kernel, tiles, chunks, group_planes),
         out_shape=(
-            shape(group, 128), shape(group, 128),
+            shape(group, 128, kind=BF16), shape(group, 128, kind=BF16),
             shape(tiles * 4 * ROWS, slots, kind=BF16), shape(tiles * 4 * ROWS, slots, kind=BF16),
             shape(8, rows, 128), shape(rows, 128, kind=jnp.int32),
         ),
@@ -467,11 +520,15 @@
         name="z_fold",
     )(main, z0, z1, got0, got1)
     sources = [block] + [lax.ppermute(sent, "gy", shift(n_gy, -s)) for s in range(1, n_gy)]
-    mine, far = pl.pallas_call(
+    mine, far, exact = pl.pallas_call(
         functools.partial(y_fold_kernel, n_gy, units, tiles),
-        out_shape=(shape(units * wide, 128, kind=BF16), shape((2 * EXT + group_planes) * wide, 128, kind=BF16)),
+        out_shape=(
+            shape(units * wide, 128, kind=BF16),
+            shape((2 * EXT + group_planes) * wide, 128, kind=BF16),
+            shape((2 * EXT + group_planes) * wide, 128),
+        ),
         in_specs=vmem(n_gy),
-        out_specs=tuple(vmem(2)),
+        out_specs=tuple(vmem(3)),
         compiler_params=pltpu.CompilerParams(vmem_limit_bytes=4 << 20),
         name="y_fold",
     )(*sources)
@@ -481,32 +538,49 @@
     if n_gx != 4:
         upper = lax.ppermute(far, "gx", shift(n_gx, -2))
     x3 = lax.ppermute(mine, "gx", other(n_gx))
-    band, y_dense = pl.pallas_call(
+    other_columns = -(-(span + AHEAD - 1 - (tiles - EXT)) * wide // 128) * 128
+    batches = -(-planes // AHEAD)
+    band_call = pl.pallas_call(
         functools.partial(band_kernel, tiles, chunks, wide),
         out_shape=(
-            shape(AHEAD * span * ROWS, band_columns, kind=BF16),
+            shape(span * STEP, band_columns, kind=BF16),
+            shape(batches, span * STEP, other_columns, kind=BF16),
             shape(2, rows * TALL, 128),
         ),
         in_specs=vmem(3),
-        out_specs=tuple(vmem(2)),
-        scratch_shapes=[pltpu.VMEM((band_columns // 128, span * ROWS, 128), F32)],
-        compiler_params=pltpu.CompilerParams(vmem_limit_bytes=8 << 20),
+        out_specs=tuple(vmem(3)),
+        scratch_shapes=[pltpu.VMEM((band_columns // 128, span * STEP, 128), F32)],
+        compiler_params=pltpu.CompilerParams(vmem_limit_bytes=16 << 20),
         cost_estimate=pl.CostEstimate(flops=400_000_000, bytes_accessed=2_000_000, transcendentals=0),
         name="band",
-    )(kernel, offset, cell)
+    )
+    band, band_other, y_dense = band_call(kernel, offset, cell)
+    own_total, own_outside = pl.pallas_call(
+        functools.partial(own_kernel, tiles, group_planes, wide, span),
+        out_shape=(shape(batches * STEP, 128), shape(batches * STEP, 128)),
+        in_specs=vmem(2),
+        out_specs=tuple(vmem(2)),
+        scratch_shapes=[
+            pltpu.VMEM(((tiles - EXT) * wide, 256), BF16),
+            pltpu.VMEM((span, batches * STEP, 256), F32),
+        ],
+        compiler_params=pltpu.CompilerParams(vmem_limit_bytes=12 << 20),
+        cost_estimate=pl.CostEstimate(flops=400_000_000, bytes_accessed=2_000_000, transcendentals=0),
+        name="own",
+    )(mine, band)
     potential, forces = pl.pallas_call(
         functools.partial(field_kernel, tiles, chunks, group_planes, wide, span),
         out_shape=(shape(tiles, CY, CZ), shape(3, rows, 128)),
-        in_specs=vmem(10),
+        in_specs=vmem(12),
         out_specs=tuple(vmem(2)),
         scratch_shapes=[
             pltpu.VMEM(((2 * (span // 2) + planes) * wide, 256), BF16),
-            pltpu.VMEM((span, -(-planes * TALL // 8) * 8, 256), F32),
-            pltpu.VMEM((4, -(-planes * TALL // 8) * 8, 128), F32),
+            pltpu.VMEM((span, -(-planes // AHEAD) * STEP, 256), F32),
+            pltpu.VMEM((4, -(-planes // AHEAD) * STEP, 128), F32),
         ],
         compiler_params=pltpu.CompilerParams(vmem_limit_bytes=16 << 20),
         name="field",
-    )(mine, x1, x3, lower, upper, band, y_dense, charge, offset, cell)
+    )(exact, x1, x3, lower, upper, band_other, own_total, own_outside, y_dense, charge, offset, cell)
     return potential, forces.reshape(3, tiles, 1, 1, slots)
 
 

time: 24.2 us -> 25.8 us (1.066)
  Pallas kernels: 6.85 us -> 8.6 us
    pallas_call x1 -> x2, Pallas kernels: 0.99 us -> 2.91 us  [the longest x1 1.84 us: local(): band, band_other, y_dense = band_call(kernel, offset, cell)]
  transfers between devices with their start and end apart: 6 -> 6, of which waited for: 3 -> 3; matrix products, arithmetic and copies ran while one was open for 0% -> 0% of each run, Pallas kernels for 8% -> 15%
where the time goes in v3:
time: 25.8 us; the launch traced here: 25.6 us
  starting transfers between devices  9.36 us (36%)
  Pallas kernels  8.6 us (33%)
  waiting for transfers between devices  6.97 us (27%)
  between operations  0.71 us (3%)
    ppermute x1, waiting for transfers between devices, local(): lower = lax.ppermute(far, 'gx', shift(n_gx, 2))  4.05 us
    pallas_call x1, Pallas kernels, local(): pl.pallas_call(functools.partial(field_kernel, tiles, chunks, group_plane...  2.9 us
    ppermute x1, starting transfers between devices, local(): got1 = lax.ppermute(z1, 'gz', other(n_gz))  2.62 us
    ppermute x1, starting transfers between devices, local(): x3 = lax.ppermute(mine, 'gx', other(n_gx))  2.48 us
    ppermute x1, waiting for transfers between devices, local(): lax.ppermute(sent, 'gy', shift(n_gy, -s))  2.4 us
    pallas_call x1, Pallas kernels, local(): band, band_other, y_dense = band_call(kernel, offset, cell)  1.84 us
    pallas_call x1, Pallas kernels, local(): pl.pallas_call(functools.partial(edge_kernel, tiles, chunks, group_planes...  1.8 us
    ppermute x1, starting transfers between devices, local(): x1 = lax.ppermute(mine, 'gx', near(n_gx))  1.8 us
  transfers between devices with their start and end apart: 6, of which 3 were waited for; matrix products, arithmetic and copies ran while one was open for 0% of the time, Pallas kernels for 15%

profile of v3, /device:TPU:0, one launch (start us, length us, event | category | flops | bytes accessed | tf_op | source)
XLA Modules:
  0.0 25.6 jit_solution(11106984236165181198)
XLA Ops:
  0.6 0.0 copy-start
  0.6 0.0 copy-start.1
  0.7 0.0 copy-start.3
  0.7 1.8 %edge.1 = (bf16[48,128]{1,0:T(8,128)(2,1)S(1)}, bf16[48,128]{1,0:T(8,128)(2,1)S(1)}, bf16[512,512]{1,0:T(8,128)(2,1)S(1)}, bf16[512,512]{1,0:T(8,128)(2,1)S(1)},...) custom-call(f32[32,128]{1,0:T(8,128)} %bitcast.10, f32[96,128]{1,0:T(8,128)} %bitcast.4, s32[64,128]{1,0:T(8,128)} %bitcast.7), custom_call_target="tpu_custom_call" | custom-call | tf_op jit(solution)/shard_map/edge/pallas_call | solution.py:481
  2.5 0.6 %collective-permute-start = (bf16[48,128]{1,0:T(8,128)(2,1)S(1)}, bf16[48,128]{1,0:T(8,128)(2,1)S(1)}, u32[]{:S(2)}, u32[]{:S(2)}) collective-permute-start(bf16[48,128]{1,0:T(8,128)(2,1)S(1)} %get-tuple-element.24.z0_ref), channel_id=1, source_target_pairs={{0,1},{1,0},{2,3},{3,2},{4,5},{5,4},{6,7},{7,6},{8,9},{9,8},{10,11... | collective-permute-start | bytes 36872 | tf_op jit(solution)/shard_map/ppermute | solution.py:502
  3.0 2.6 %collective-permute-start.1 = (bf16[48,128]{1,0:T(8,128)(2,1)S(1)}, bf16[48,128]{1,0:T(8,128)(2,1)S(1)}, u32[]{:S(2)}, u32[]{:S(2)}) collective-permute-start(bf16[48,128]{1,0:T(8,128)(2,1)S(1)} %get-tuple-element.25.z1_ref), channel_id=1, source_target_pairs={{0,3},{1,2},{2,1},{3,0},{4,7},{5,6},{6,5},{7,4},{8,11},{9,10},{10,... | collective-permute-start | bytes 36872 | tf_op jit(solution)/shard_map/ppermute | solution.py:503
  5.6 0.9 %spread.1.main_ref = f32[176,128]{1,0:T(8,128)S(1)} custom-call(bf16[512,512]{1,0:T(8,128)(2,1)S(1)} %get-tuple-element.20.high_ref, bf16[512,512]{1,0:T(8,128)(2,1)S(1)} %get-tuple-element.21.low_ref, f32[8,32,128]{2,1,0:T(8,128)S(1)} %get-tuple-element.22.weight_ref, s32[32,128]{1,0:T(8,128)S(1)} %get-tuple-element.23.cell_ref), custom_call_target="tpu_custom_call" | custom-call | flops 400000000 | bytes 2000000 | tf_op jit(solution)/shard_map/spread/pallas_call | solution.py:504
  6.5 0.0 collective-permute-done.got0_ref
  6.5 0.5 %collective-permute-done.1.got1_ref = bf16[48,128]{1,0:T(8,128)(2,1)S(1)} collective-permute-done((bf16[48,128]{1,0:T(8,128)(2,1)S(1)}, bf16[48,128]{1,0:T(8,128)(2,1)S(1)}, u32[]{:S(2)}, u32[]{:S(2)}) %collective-permute-start.1) | collective-permute-done | bytes 12320 | tf_op jit(solution)/shard_map/ppermute | solution.py:503
  7.1 0.1 z_fold.1
  7.1 1.7 %collective-permute-start.2 = (bf16[176,128]{1,0:T(8,128)(2,1)S(1)}, bf16[176,128]{1,0:T(8,128)(2,1)S(1)}, u32[]{:S(2)}, u32[]{:S(2)}) collective-permute-start(bf16[176,128]{1,0:T(8,128)(2,1)S(1)} %get-tuple-element.27), channel_id=1, source_target_pairs={{0,4},{4,0},{1,5},{5,1},{2,6},{6,2},{3,7},{7,3},{8,12},{12,8},{9,1... | collective-permute-start | bytes 135176 | tf_op jit(solution)/shard_map/ppermute | solution.py:522
  8.9 2.4 %collective-permute-done.2.refs_1_ = bf16[176,128]{1,0:T(8,128)(2,1)S(1)} collective-permute-done((bf16[176,128]{1,0:T(8,128)(2,1)S(1)}, bf16[176,128]{1,0:T(8,128)(2,1)S(1)}, u32[]{:S(2)}, u32[]{:S(2)}) %collective-permute-start.2) | collective-permute-done | bytes 45088 | tf_op jit(solution)/shard_map/ppermute | solution.py:522
  11.3 0.0 copy-start.2
  11.3 1.8 %collective-permute-start.3 = (bf16[224,128]{1,0:T(8,128)(2,1)S(1)}, bf16[224,128]{1,0:T(8,128)(2,1)S(1)}, u32[]{:S(2)}, u32[]{:S(2)}) collective-permute-start(bf16[224,128]{1,0:T(8,128)(2,1)S(1)} %get-tuple-element.29.own_ref), channel_id=1, source_target_pairs={{0,8},{8,0},{16,24},{24,16},{1,9},{9,1},{17,25},{25,17},{2,10},{10... | collective-permute-start | bytes 172040 | tf_op jit(solution)/shard_map/ppermute | solution.py:535
  13.1 2.5 %collective-permute-start.4 = (bf16[224,128]{1,0:T(8,128)(2,1)S(1)}, bf16[224,128]{1,0:T(8,128)(2,1)S(1)}, u32[]{:S(2)}, u32[]{:S(2)}) collective-permute-start(bf16[224,128]{1,0:T(8,128)(2,1)S(1)} %get-tuple-element.29.own_ref), channel_id=1, source_target_pairs={{0,24},{8,16},{16,8},{24,0},{1,25},{9,17},{17,9},{25,1},{2,26},{10... | collective-permute-start | bytes 172040 | tf_op jit(solution)/shard_map/ppermute | solution.py:540
  15.6 0.0 copy-done
  15.6 0.0 copy-done.1
  15.6 1.8 %band.1 = (bf16[816,384]{1,0:T(8,128)(2,1)S(1)}, bf16[3,816,256]{2,1,0:T(8,128)(2,1)S(1)}, f32[2,352,128]{2,1,0:T(8,128)S(1)}) custom-call(bf16[17,17,17]{2,1,0:T(8,128)(2,1)S(1)} %copy-done.3, f32[96,128]{1,0:T(8,128)S(1)} %bitcast.5, s32[64,128]{1,0:T(8,128)S(1)} %bitcast.8), custom_call_target="tpu_custom_call" | custom-call | flops 400000000 | bytes 2000000 | tf_op jit(solution)/shard_map/band/pallas_call | solution.py:557
  17.4 0.2 collective-permute-start.5
  17.6 1.1 %own.1 = (f32[144,128]{1,0:T(8,128)S(1)}, f32[144,128]{1,0:T(8,128)S(1)}) custom-call(bf16[224,128]{1,0:T(8,128)(2,1)S(1)} %get-tuple-element.29.own_ref, bf16[816,384]{1,0:T(8,128)(2,1)S(1)} %get-tuple-element.32.band_ref), custom_call_target="tpu_custom_call" | custom-call | flops 400000000 | bytes 2000000 | tf_op jit(solution)/shard_map/own/pallas_call | solution.py:558
  18.7 4.0 %collective-permute-done.5.lower_ref.upper_ref = bf16[144,128]{1,0:T(8,128)(2,1)S(1)} collective-permute-done((bf16[144,128]{1,0:T(8,128)(2,1)S(1)}, bf16[144,128]{1,0:T(8,128)(2,1)S(1)}, u32[]{:S(2)}, u32[]{:S(2)}) %collective-permute-start.5) | collective-permute-done | bytes 36896 | tf_op jit(solution)/shard_map/ppermute | solution.py:536
  22.7 0.0 collective-permute-done.3.got1_ref
  22.7 0.0 collective-permute-done.4.got3_ref
  22.7 2.9 %field.1 = (f32[8,8,128]{2,1,0:T(8,128)}, f32[3,32,128]{2,1,0:T(8,128)}) custom-call(f32[144,128]{1,0:T(8,128)S(1)} %get-tuple-element.28.own_ref, bf16[224,128]{1,0:T(8,128)(2,1)S(1)} %collective-permute-done.3.got1_ref, bf16[224,128]{1,0:T(8,128)(2,1)S(1)} %collective-permute-done.4.got3_ref, ...), custom_call_target="tpu_custom_call" | custom-call | tf_op jit(solution)/shard_map/field/pallas_call | solution.py:571
  (3 shorter events, 0.0 us)
Async XLA Ops:
  0.6 14.9 %copy-start = (f32[3,8,1,1,512]{4,3,2,1,0:T(1,128)S(1)}, f32[3,8,1,1,512]{4,3,2,1,0:T(1,128)}, u32[]{:S(2)}) copy-start(f32[3,8,1,1,512]{4,3,2,1,0:T(1,128)} %param.5) | copy-start | bytes 147460
  0.6 14.9 %copy-start.1 = (s32[2,8,1,1,512]{4,3,2,1,0:T(1,128)S(1)}, s32[2,8,1,1,512]{4,3,2,1,0:T(1,128)}, u32[]{:S(2)}) copy-start(s32[2,8,1,1,512]{4,3,2,1,0:T(1,128)} %param.6) | copy-start | bytes 98308
  0.7 14.9 %copy-start.3 = (bf16[17,17,17]{2,1,0:T(8,128)(2,1)S(1)}, bf16[17,17,17]{2,1,0:T(8,128)(2,1)}, u32[]{:S(2)}) copy-start(bf16[17,17,17]{2,1,0:T(8,128)(2,1)} %kernel_ref.1) | copy-start | bytes 29482
  2.5 4.1 %collective-permute-start = (bf16[48,128]{1,0:T(8,128)(2,1)S(1)}, bf16[48,128]{1,0:T(8,128)(2,1)S(1)}, u32[]{:S(2)}, u32[]{:S(2)}) collective-permute-start(bf16[48,128]{1,0:T(8,128)(2,1)S(1)} %get-tuple-element.24.z0_ref), channel_id=1, source_target_pairs={{0,1},{1,0},{2,3},{3,2},{4,5},{5,4},{6,7},{7,6},{8,9},{9,8},{10,11... | collective-permute-start | bytes 36872 | tf_op jit(solution)/shard_map/ppermute | solution.py:502
  3.0 4.0 %collective-permute-start.1 = (bf16[48,128]{1,0:T(8,128)(2,1)S(1)}, bf16[48,128]{1,0:T(8,128)(2,1)S(1)}, u32[]{:S(2)}, u32[]{:S(2)}) collective-permute-start(bf16[48,128]{1,0:T(8,128)(2,1)S(1)} %get-tuple-element.25.z1_ref), channel_id=1, source_target_pairs={{0,3},{1,2},{2,1},{3,0},{4,7},{5,6},{6,5},{7,4},{8,11},{9,10},{10,... | collective-permute-start | bytes 36872 | tf_op jit(solution)/shard_map/ppermute | solution.py:503
  7.1 4.1 %collective-permute-start.2 = (bf16[176,128]{1,0:T(8,128)(2,1)S(1)}, bf16[176,128]{1,0:T(8,128)(2,1)S(1)}, u32[]{:S(2)}, u32[]{:S(2)}) collective-permute-start(bf16[176,128]{1,0:T(8,128)(2,1)S(1)} %get-tuple-element.27), channel_id=1, source_target_pairs={{0,4},{4,0},{1,5},{5,1},{2,6},{6,2},{3,7},{7,3},{8,12},{12,8},{9,1... | collective-permute-start | bytes 135176 | tf_op jit(solution)/shard_map/ppermute | solution.py:522
  11.3 11.5 %copy-start.2 = (f32[8,1,1,512]{3,2,1,0:T(1,128)S(1)}, f32[8,1,1,512]{3,2,1,0:T(1,128)}, u32[]{:S(2)}) copy-start(f32[8,1,1,512]{3,2,1,0:T(1,128)} %param.4) | copy-start | bytes 49156
  11.3 11.4 %collective-permute-start.3 = (bf16[224,128]{1,0:T(8,128)(2,1)S(1)}, bf16[224,128]{1,0:T(8,128)(2,1)S(1)}, u32[]{:S(2)}, u32[]{:S(2)}) collective-permute-start(bf16[224,128]{1,0:T(8,128)(2,1)S(1)} %get-tuple-element.29.own_ref), channel_id=1, source_target_pairs={{0,8},{8,0},{16,24},{24,16},{1,9},{9,1},{17,25},{25,17},{2,10},{10... | collective-permute-start | bytes 172040 | tf_op jit(solution)/shard_map/ppermute | solution.py:535
  13.1 9.7 %collective-permute-start.4 = (bf16[224,128]{1,0:T(8,128)(2,1)S(1)}, bf16[224,128]{1,0:T(8,128)(2,1)S(1)}, u32[]{:S(2)}, u32[]{:S(2)}) collective-permute-start(bf16[224,128]{1,0:T(8,128)(2,1)S(1)} %get-tuple-element.29.own_ref), channel_id=1, source_target_pairs={{0,24},{8,16},{16,8},{24,0},{1,25},{9,17},{17,9},{25,1},{2,26},{10... | collective-permute-start | bytes 172040 | tf_op jit(solution)/shard_map/ppermute | solution.py:540
  17.4 5.3 %collective-permute-start.5 = (bf16[144,128]{1,0:T(8,128)(2,1)S(1)}, bf16[144,128]{1,0:T(8,128)(2,1)S(1)}, u32[]{:S(2)}, u32[]{:S(2)}) collective-permute-start(bf16[144,128]{1,0:T(8,128)(2,1)S(1)} %get-tuple-element.30), channel_id=1, source_target_pairs={{0,16},{8,24},{16,0},{24,8},{1,17},{9,25},{17,1},{25,9},{2,18},{10... | collective-permute-start | bytes 110600 | tf_op jit(solution)/shard_map/ppermute | solution.py:536

commit v4 on v3

--- a/solution.py
+++ b/solution.py
@@ -75,14 +75,19 @@
 
 
 def edge_kernel(
-    tiles, chunks, group_planes, charge_hbm, offset_hbm, cell_hbm,
+    tiles, chunks, group_planes, charge_hbm, offset_hbm, cell_hbm, kernel_hbm,
     z0_ref, z1_ref, high_ref, low_ref, weight_ref, cell_ref,
-    charge_in, offset_in, cell_in, x_rows, y_rows, acc, sems,
+    charge_in, offset_in, cell_in, kernel_in, x_rows, y_rows, acc, sems,
 ):
     copies = [
         pltpu.make_async_copy(source, target, sems.at[n])
         for n, (source, target) in enumerate(
-            ((charge_hbm, charge_in), (offset_hbm, offset_in), (cell_hbm, cell_in))
+            (
+                (charge_hbm, charge_in),
+                (offset_hbm, offset_in),
+                (cell_hbm, cell_in),
+                (kernel_hbm, kernel_in),
+            )
         )
     ]
     for copy in copies:
@@ -93,7 +98,7 @@
     z_of_row = jnp.where(row < LANES // 2, row - 1, row + (CZ + 2 - LANES // 2 - 11))
     y_row = iota((ROWS, 128), 0)
     y_of_row = jnp.where(y_row < 12, y_row, y_row - ROWS)
-    for copy in copies:
+    for copy in copies[:3]:
         copy.wait()
     for r in range(0, rows, 8):
         at = pl.ds(r, 8)
@@ -137,6 +142,7 @@
     even = lax.rem(lax.axis_index("gz"), 2) == 0
     z0_ref[...] = jnp.where(even, upper_out, lower_out).astype(BF16)
     z1_ref[...] = jnp.where(even, lower_out, upper_out).astype(BF16)
+    copies[3].wait()
 
 
 def spread_kernel(tiles, chunks, high_ref, low_ref, weight_ref, cell_ref, main_ref):
@@ -290,8 +296,8 @@
 
 def field_kernel(
     tiles, chunks, group_planes, wide, span,
-    own_ref, got1_ref, got3_ref, lower_ref, upper_ref, band_ref, total_ref, outside_ref, y_ref,
-    charge_ref, offset_ref, cell_ref, potential_ref, force_ref, window, parts, samples,
+    own_ref, got1_ref, got3_ref, lower_ref, upper_ref, band_ref, total_ref, outside_ref,
+    hot_ref, weight_ref, z_ref, potential_ref, force_ref, window, parts, samples,
 ):
     planes = tiles + EXT
     radius = span // 2
@@ -364,52 +370,72 @@
     for x in range(tiles):
         potential_ref[x] = samples[1, row_of(x + 1) + 1 : row_of(x + 1) + 1 + CY, :]
 
-    rows_total = tiles * chunks
-    per = 8 // chunks
-    pairs = tiles // per
-    upper_half = [iota((8, 128), 0) >= chunks * h for h in range(per)]
-    for p in range(pairs):
-        at = pl.ds(p * 8, 8)
-        cz = cell_ref[pl.ds(rows_total + p * 8, 8), :] & (CZ - 1)
-        zv, zs = spline(offset_ref[pl.ds(2 * rows_total + p * 8, 8), :])
-        xv, xs = spline(offset_ref[at, :])
-        force = [jnp.zeros((8, 128), F32)] * 3
-        for k in range(4):
-            plain = [jnp.zeros((8, 128), F32)] * 4
-            sloped = [jnp.zeros((8, 128), F32)] * 4
-            for y in range(TALL):
-                y_at = pl.ds((p * TALL + y) * 8, 8)
-                y_value = y_ref[0, y_at, :]
-                y_slope = y_ref[1, y_at, :]
-                for c in range(4):
-                    source = None
-                    for h in range(per):
-                        row = row_of(p * per + k + h) + y
-                        line = jnp.broadcast_to(samples[c, row : row + 1, :], (8, 128))
-                        source = line if h == 0 else jnp.where(upper_half[h], line, source)
-                    picked = jnp.take_along_axis(source, cz, axis=1)
-                    plain[c] = plain[c] + y_value * picked
-                    sloped[c] = sloped[c] + y_slope * picked
-            value = sum(zv[c] * plain[c] for c in range(4))
-            along_y = sum(zv[c] * sloped[c] for c in range(4))
-            along_z = sum(zs[c] * plain[c] for c in range(4))
-            force[0] = force[0] + xs[k] * value
-            force[1] = force[1] + xv[k] * along_y
-            force[2] = force[2] + xv[k] * along_z
+    for t in range(tiles):
+        rows = slice(row_of(t), row_of(t) + STEP)
+        halves = [jnp.concatenate(split(samples[c, rows, :]), 1) for c in range(4)]
+        picked = jnp.dot(jnp.concatenate(halves, 0), hot_ref[t], preferred_element_type=F32)
+        for j in range(chunks):
+            at = t * chunks + j
+            lanes = slice(j * 128, (j + 1) * 128)
+            four = [picked[c * STEP : (c + 1) * STEP, lanes] for c in range(4)]
+            value = sum(z_ref[c, at : at + 1, :] * four[c] for c in range(4))
+            slope = sum(z_ref[4 + c, at : at + 1, :] * four[c] for c in range(4))
+            for d, part in enumerate((value, value, slope)):
+                force_ref[d, at : at + 1, :] = jnp.sum(
+                    weight_ref[t, d, :, lanes] * part, axis=0, keepdims=True
+                )
+
+
+def weight_kernel(tiles, chunks, charge_ref, offset_ref, cell_ref, hot_ref, weight_ref, z_ref, x_rows, y_rows):
+    rows = tiles * chunks
+    for r in range(0, rows, 8):
+        at = pl.ds(r, 8)
         charge = charge_ref[at, :]
-        for d in range(3):
-            force_ref[d, at, :] = -charge * force[d]
-
-
-def band_kernel(tiles, chunks, wide, kernel_ref, offset_ref, cell_ref, out_ref, other_ref, y_ref, rows_ref):
-    rows_total = tiles * chunks
-    for p in range(rows_total // 8):
-        yv, ys = spline(offset_ref[pl.ds(rows_total + p * 8, 8), :])
-        cy = cell_ref[pl.ds(p * 8, 8), :] & (CY - 1)
-        for y in range(TALL):
-            at = pl.ds((p * TALL + y) * 8, 8)
-            y_ref[0, at, :] = pick(y - cy, yv)
-            y_ref[1, at, :] = pick(y - cy, ys)
+        xs = spline(offset_ref[at, :])
+        ys = spline(offset_ref[pl.ds(rows + r, 8), :])
+        zs = spline(offset_ref[pl.ds(2 * rows + r, 8), :])
+        for w in range(2):
+            for c in range(4):
+                x_rows[4 * w + c, at, :] = -charge * xs[w][c]
+                y_rows[4 * w + c, at, :] = ys[w][c]
+                z_ref[4 * w + c, at, :] = zs[w][c]
+    z_of_row = iota((CZ, 128), 0, jnp.int16)
+    one, zero = jnp.ones((CZ, 128), BF16), jnp.zeros((CZ, 128), BF16)
+    row = iota((STEP, 128), 0)
+    for t in range(tiles):
+        starts = [row_of(t + k) - row_of(t) for k in range(4)]
+        plane = [row >= start for start in starts]
+        y_of_row = row - sum(
+            jnp.where(plane[k], starts[k] - starts[k - 1], 0) for k in range(1, 4)
+        )
+        for j in range(chunks):
+            at = pl.ds(t * chunks + j, 1)
+            lanes = slice(j * 128, (j + 1) * 128)
+            cy = cell_ref[at, :] & (CY - 1)
+            cz = cell_ref[pl.ds(rows + t * chunks + j, 1), :] & (CZ - 1)
+            hot = jnp.where(z_of_row == tall(cz, jnp.int16, CZ), one, zero)
+            hot_ref[t, :CZ, lanes] = hot
+            hot_ref[t, CZ:, lanes] = hot
+            gap = y_of_row - cy
+            here = [gap == c for c in range(4)]
+
+            def line(ref, n):
+                return ref[n, at, :]
+
+            y_value = y_slope = jnp.zeros((STEP, 128), F32)
+            for c in range(4):
+                y_value = jnp.where(here[c], line(y_rows, c), y_value)
+                y_slope = jnp.where(here[c], line(y_rows, 4 + c), y_slope)
+            x_value = x_slope = jnp.zeros((STEP, 128), F32)
+            for k in range(4):
+                x_value = jnp.where(plane[k], line(x_rows, k), x_value)
+                x_slope = jnp.where(plane[k], line(x_rows, 4 + k), x_slope)
+            weight_ref[t, 0, :, lanes] = x_slope * y_value
+            weight_ref[t, 1, :, lanes] = x_value * y_slope
+            weight_ref[t, 2, :, lanes] = x_value * y_value
+
+
+def band_kernel(tiles, wide, kernel_ref, out_ref, other_ref, rows_ref):
     span = kernel_ref.shape[0]
     radius = span // 2
     columns = out_ref.shape[1]
@@ -478,27 +504,26 @@
     other = lambda n: [(i, (i + 1 if i % 2 else i - 1) % n) for i in range(n)]
     shift = lambda n, s: [(i, (i + s) % n) for i in range(n)]
 
-    z0, z1, s_high, s_low, weights, z_cell = pl.pallas_call(
+    z0, z1, s_high, s_low, weights, z_cell, charge_in, offset_in, cell_in, kernel_in = pl.pallas_call(
         functools.partial(edge_kernel, tiles, chunks, group_planes),
         out_shape=(
             shape(group, 128, kind=BF16), shape(group, 128, kind=BF16),
             shape(tiles * 4 * ROWS, slots, kind=BF16), shape(tiles * 4 * ROWS, slots, kind=BF16),
             shape(8, rows, 128), shape(rows, 128, kind=jnp.int32),
+            shape(rows, 128), shape(3 * rows, 128), shape(2 * rows, 128, kind=jnp.int32),
+            shape(*kernel.shape, kind=kernel.dtype),
         ),
-        in_specs=[pl.BlockSpec(memory_space=pltpu.HBM)] * 3,
-        out_specs=tuple(vmem(6)),
+        in_specs=[pl.BlockSpec(memory_space=pltpu.HBM)] * 4,
+        out_specs=tuple(vmem(10)),
         scratch_shapes=[
-            pltpu.VMEM((rows, 128), F32),
-            pltpu.VMEM((3 * rows, 128), F32),
-            pltpu.VMEM((2 * rows, 128), jnp.int32),
             pltpu.VMEM((4, rows, 128), F32),
             pltpu.VMEM((4, rows, 128), F32),
             pltpu.VMEM((GROUPS * group, 128), F32),
-            pltpu.SemaphoreType.DMA((3,)),
+            pltpu.SemaphoreType.DMA((4,)),
         ],
         compiler_params=pltpu.CompilerParams(vmem_limit_bytes=8 << 20),
         name="edge",
-    )(*(pltpu.with_memory_space_constraint(x, pltpu.HBM) for x in (charge, offset, cell)))
+    )(*(pltpu.with_memory_space_constraint(x, pltpu.HBM) for x in (charge, offset, cell, kernel)))
     got0 = lax.ppermute(z0, "gz", near(n_gz))
     got1 = lax.ppermute(z1, "gz", other(n_gz))
     main = pl.pallas_call(
@@ -541,20 +566,33 @@
     other_columns = -(-(span + AHEAD - 1 - (tiles - EXT)) * wide // 128) * 128
     batches = -(-planes // AHEAD)
     band_call = pl.pallas_call(
-        functools.partial(band_kernel, tiles, chunks, wide),
+        functools.partial(band_kernel, tiles, wide),
         out_shape=(
             shape(span * STEP, band_columns, kind=BF16),
             shape(batches, span * STEP, other_columns, kind=BF16),
-            shape(2, rows * TALL, 128),
         ),
-        in_specs=vmem(3),
-        out_specs=tuple(vmem(3)),
+        in_specs=vmem(1),
+        out_specs=tuple(vmem(2)),
         scratch_shapes=[pltpu.VMEM((band_columns // 128, span * STEP, 128), F32)],
         compiler_params=pltpu.CompilerParams(vmem_limit_bytes=16 << 20),
         cost_estimate=pl.CostEstimate(flops=400_000_000, bytes_accessed=2_000_000, transcendentals=0),
         name="band",
     )
-    band, band_other, y_dense = band_call(kernel, offset, cell)
+    band, band_other = band_call(kernel_in)
+    hot, weights_xy, weights_z = pl.pallas_call(
+        functools.partial(weight_kernel, tiles, chunks),
+        out_shape=(
+            shape(tiles, 2 * CZ, slots, kind=BF16),
+            shape(tiles, 3, STEP, slots),
+            shape(8, rows, 128),
+        ),
+        in_specs=vmem(3),
+        out_specs=tuple(vmem(3)),
+        scratch_shapes=[pltpu.VMEM((8, rows, 128), F32), pltpu.VMEM((8, rows, 128), F32)],
+        compiler_params=pltpu.CompilerParams(vmem_limit_bytes=12 << 20),
+        cost_estimate=pl.CostEstimate(flops=400_000_000, bytes_accessed=2_000_000, transcendentals=0),
+        name="weights",
+    )(charge_in, offset_in, cell_in)
     own_total, own_outside = pl.pallas_call(
         functools.partial(own_kernel, tiles, group_planes, wide, span),
         out_shape=(shape(batches * STEP, 128), shape(batches * STEP, 128)),
@@ -571,7 +609,7 @@
     potential, forces = pl.pallas_call(
         functools.partial(field_kernel, tiles, chunks, group_planes, wide, span),
         out_shape=(shape(tiles, CY, CZ), shape(3, rows, 128)),
-        in_specs=vmem(12),
+        in_specs=vmem(11),
         out_specs=tuple(vmem(2)),
         scratch_shapes=[
             pltpu.VMEM(((2 * (span // 2) + planes) * wide, 256), BF16),
@@ -580,7 +618,7 @@
         ],
         compiler_params=pltpu.CompilerParams(vmem_limit_bytes=16 << 20),
         name="field",
-    )(exact, x1, x3, lower, upper, band_other, own_total, own_outside, y_dense, charge, offset, cell)
+    )(exact, x1, x3, lower, upper, band_other, own_total, own_outside, hot, weights_xy, weights_z)
     return potential, forces.reshape(3, tiles, 1, 1, slots)
 
 

time: 25.8 us -> 23.6 us (0.915)
  waiting for transfers between devices: 6.97 us -> 4.29 us
  Pallas kernels: 8.6 us -> 8.98 us
    ppermute x1, starting transfers between devices: 1.8 us -> 0.01 us  [local(): x1 = lax.ppermute(mine, 'gx', near(n_gx))]
    ppermute x1, waiting for transfers between devices: 2.4 us -> 0.63 us  [local(): lax.ppermute(sent, 'gy', shift(n_gy, -s))]
    ppermute x1, starting transfers between devices: 2.48 us -> 3.82 us  [local(): x3 = lax.ppermute(mine, 'gx', other(n_gx))]
    ppermute x1, waiting for transfers between devices: 4.05 us -> 3.14 us  [local(): lower = lax.ppermute(far, 'gx', shift(n_gx, 2))]
    pallas_call x1 -> x2, Pallas kernels: 1.84 us -> 2.7 us  [the longest x1 1.75 us: local(): band, band_other = band_call(kernel_in)]
    ppermute x1, starting transfers between devices: 0.19 us -> 0.7 us  [local(): lower = lax.ppermute(far, 'gx', shift(n_gx, 2))]
    pallas_call x1, Pallas kernels: 2.9 us -> 2.44 us  [local(): pl.pallas_call(functools.partial(field_kernel, tiles, chunks, group_plane...]
  transfers between devices with their start and end apart: 6 -> 6, of which waited for: 3 -> 3; matrix products, arithmetic and copies ran while one was open for 0% -> 0% of each run, Pallas kernels for 15% -> 20%
where the time goes in v4:
time: 23.6 us; the launch traced here: 23.4 us
  starting transfers between devices  9.42 us (40%)
  Pallas kernels  8.98 us (38%)
  waiting for transfers between devices  4.29 us (18%)
  between operations  0.68 us (3%)
    ppermute x1, starting transfers between devices, local(): x3 = lax.ppermute(mine, 'gx', other(n_gx))  3.82 us
    ppermute x1, waiting for transfers between devices, local(): lower = lax.ppermute(far, 'gx', shift(n_gx, 2))  3.14 us
    ppermute x1, starting transfers between devices, local(): got1 = lax.ppermute(z1, 'gz', other(n_gz))  2.62 us
    pallas_call x1, Pallas kernels, local(): pl.pallas_call(functools.partial(field_kernel, tiles, chunks, group_plane...  2.44 us
    pallas_call x1, Pallas kernels, local(): pl.pallas_call(functools.partial(edge_kernel, tiles, chunks, group_planes...  1.77 us
    pallas_call x1, Pallas kernels, local(): band, band_other = band_call(kernel_in)  1.75 us
    ppermute x1, starting transfers between devices, local(): lax.ppermute(sent, 'gy', shift(n_gy, -s))  1.72 us
    pallas_call x1, Pallas kernels, local(): pl.pallas_call(functools.partial(own_kernel, tiles, group_planes, wide, s...  1.08 us
  transfers between devices with their start and end apart: 6, of which 3 were waited for; matrix products, arithmetic and copies ran while one was open for 0% of the time, Pallas kernels for 20%

profile of v4, /device:TPU:0, one launch (start us, length us, event | category | flops | bytes accessed | tf_op | source)
XLA Modules:
  0.0 23.4 jit_solution(15338747778475144340)
XLA Ops:
  0.6 1.8 %edge.1 = (bf16[48,128]{1,0:T(8,128)(2,1)S(1)}, bf16[48,128]{1,0:T(8,128)(2,1)S(1)}, bf16[512,512]{1,0:T(8,128)(2,1)S(1)}, bf16[512,512]{1,0:T(8,128)(2,1)S(1)},...) custom-call(f32[32,128]{1,0:T(8,128)} %bitcast.6, ...), custom_call_target="tpu_custom_call" | custom-call | tf_op jit(solution)/shard_map/edge/pallas_call | solution.py:507
  2.4 0.6 %collective-permute-start = (bf16[48,128]{1,0:T(8,128)(2,1)S(1)}, bf16[48,128]{1,0:T(8,128)(2,1)S(1)}, u32[]{:S(2)}, u32[]{:S(2)}) collective-permute-start(bf16[48,128]{1,0:T(8,128)(2,1)S(1)} %get-tuple-element.30.z0_ref), channel_id=1, source_target_pairs={{0,1},{1,0},{2,3},{3,2},{4,5},{5,4},{6,7},{7,6},{8,9},{9,8},{10,11... | collective-permute-start | bytes 36872 | tf_op jit(solution)/shard_map/ppermute | solution.py:527
  3.0 2.6 %collective-permute-start.1 = (bf16[48,128]{1,0:T(8,128)(2,1)S(1)}, bf16[48,128]{1,0:T(8,128)(2,1)S(1)}, u32[]{:S(2)}, u32[]{:S(2)}) collective-permute-start(bf16[48,128]{1,0:T(8,128)(2,1)S(1)} %get-tuple-element.31.z1_ref), channel_id=1, source_target_pairs={{0,3},{1,2},{2,1},{3,0},{4,7},{5,6},{6,5},{7,4},{8,11},{9,10},{10,... | collective-permute-start | bytes 36872 | tf_op jit(solution)/shard_map/ppermute | solution.py:528
  5.6 0.9 %spread.1.main_ref = f32[176,128]{1,0:T(8,128)S(1)} custom-call(bf16[512,512]{1,0:T(8,128)(2,1)S(1)} %get-tuple-element.26.high_ref, bf16[512,512]{1,0:T(8,128)(2,1)S(1)} %get-tuple-element.27.low_ref, f32[8,32,128]{2,1,0:T(8,128)S(1)} %get-tuple-element.28.weight_ref, s32[32,128]{1,0:T(8,128)S(1)} %get-tuple-element.29.cell_ref), custom_call_target="tpu_custom_call" | custom-call | flops 400000000 | bytes 2000000 | tf_op jit(solution)/shard_map/spread/pallas_call | solution.py:529
  6.5 0.0 collective-permute-done.got0_ref
  6.5 0.5 %collective-permute-done.1.got1_ref = bf16[48,128]{1,0:T(8,128)(2,1)S(1)} collective-permute-done((bf16[48,128]{1,0:T(8,128)(2,1)S(1)}, bf16[48,128]{1,0:T(8,128)(2,1)S(1)}, u32[]{:S(2)}, u32[]{:S(2)}) %collective-permute-start.1) | collective-permute-done | bytes 12320 | tf_op jit(solution)/shard_map/ppermute | solution.py:528
  7.0 0.1 z_fold.1
  7.1 1.7 %collective-permute-start.2 = (bf16[176,128]{1,0:T(8,128)(2,1)S(1)}, bf16[176,128]{1,0:T(8,128)(2,1)S(1)}, u32[]{:S(2)}, u32[]{:S(2)}) collective-permute-start(bf16[176,128]{1,0:T(8,128)(2,1)S(1)} %get-tuple-element.33), channel_id=1, source_target_pairs={{0,4},{4,0},{1,5},{5,1},{2,6},{6,2},{3,7},{7,3},{8,12},{12,8},{9,1... | collective-permute-start | bytes 135176 | tf_op jit(solution)/shard_map/ppermute | solution.py:547
  8.8 1.8 %band.1 = (bf16[816,384]{1,0:T(8,128)(2,1)S(1)}, bf16[3,816,256]{2,1,0:T(8,128)(2,1)S(1)}) custom-call(bf16[17,17,17]{2,1,0:T(8,128)(2,1)S(1)} %get-tuple-element.37.kernel_ref), custom_call_target="tpu_custom_call" | custom-call | flops 400000000 | bytes 2000000 | tf_op jit(solution)/shard_map/band/pallas_call | solution.py:581
  10.6 0.6 %collective-permute-done.2.refs_1_ = bf16[176,128]{1,0:T(8,128)(2,1)S(1)} collective-permute-done((bf16[176,128]{1,0:T(8,128)(2,1)S(1)}, bf16[176,128]{1,0:T(8,128)(2,1)S(1)}, u32[]{:S(2)}, u32[]{:S(2)}) %collective-permute-start.2) | collective-permute-done | bytes 45088 | tf_op jit(solution)/shard_map/ppermute | solution.py:547
  11.2 3.8 %collective-permute-start.4 = (bf16[224,128]{1,0:T(8,128)(2,1)S(1)}, bf16[224,128]{1,0:T(8,128)(2,1)S(1)}, u32[]{:S(2)}, u32[]{:S(2)}) collective-permute-start(bf16[224,128]{1,0:T(8,128)(2,1)S(1)} %get-tuple-element.35.own_ref), channel_id=1, source_target_pairs={{0,24},{8,16},{16,8},{24,0},{1,25},{9,17},{17,9},{25,1},{2,26},{10... | collective-permute-start | bytes 172040 | tf_op jit(solution)/shard_map/ppermute | solution.py:565
  15.0 0.0 collective-permute-start.3
  15.0 1.0 %weights.1 = (bf16[8,256,512]{2,1,0:T(8,128)(2,1)S(1)}, f32[8,3,48,512]{3,2,1,0:T(8,128)S(1)}, f32[8,32,128]{2,1,0:T(8,128)S(1)}) custom-call(f32[32,128]{1,0:T(8,128)S(1)} %get-tuple-element.42.charge_ref, f32[96,128]{1,0:T(8,128)S(1)} %get-tuple-element.43.offset_ref, s32[64,128]{1,0:T(8,128)S(1)} %get-tuple-element.44.cell_ref), custom_call_target="tpu_custom_call" | custom-call | flops 400000000 | bytes 2000000 | tf_op jit(solution)/shard_map/weights/pallas_call | solution.py:582
  16.0 0.7 %collective-permute-start.5 = (bf16[144,128]{1,0:T(8,128)(2,1)S(1)}, bf16[144,128]{1,0:T(8,128)(2,1)S(1)}, u32[]{:S(2)}, u32[]{:S(2)}) collective-permute-start(bf16[144,128]{1,0:T(8,128)(2,1)S(1)} %get-tuple-element.36), channel_id=1, source_target_pairs={{0,16},{8,24},{16,0},{24,8},{1,17},{9,25},{17,1},{25,9},{2,18},{10... | collective-permute-start | bytes 110600 | tf_op jit(solution)/shard_map/ppermute | solution.py:561
  16.7 1.1 %own.1 = (f32[144,128]{1,0:T(8,128)S(1)}, f32[144,128]{1,0:T(8,128)S(1)}) custom-call(bf16[224,128]{1,0:T(8,128)(2,1)S(1)} %get-tuple-element.35.own_ref, bf16[816,384]{1,0:T(8,128)(2,1)S(1)} %get-tuple-element.39.band_ref), custom_call_target="tpu_custom_call" | custom-call | flops 400000000 | bytes 2000000 | tf_op jit(solution)/shard_map/own/pallas_call | solution.py:596
  17.8 3.1 %collective-permute-done.5.lower_ref.upper_ref = bf16[144,128]{1,0:T(8,128)(2,1)S(1)} collective-permute-done((bf16[144,128]{1,0:T(8,128)(2,1)S(1)}, bf16[144,128]{1,0:T(8,128)(2,1)S(1)}, u32[]{:S(2)}, u32[]{:S(2)}) %collective-permute-start.5) | collective-permute-done | bytes 36896 | tf_op jit(solution)/shard_map/ppermute | solution.py:561
  20.9 0.0 collective-permute-done.4.got3_ref
  20.9 0.0 collective-permute-done.3.got1_ref
  20.9 2.4 %field.1 = (f32[8,8,128]{2,1,0:T(8,128)}, f32[3,32,128]{2,1,0:T(8,128)}) custom-call(f32[144,128]{1,0:T(8,128)S(1)} %get-tuple-element.34.own_ref, bf16[224,128]{1,0:T(8,128)(2,1)S(1)} %collective-permute-done.3.got1_ref, bf16[224,128]{1,0:T(8,128)(2,1)S(1)} %collective-permute-done.4.got3_ref, ...), custom_call_target="tpu_custom_call" | custom-call | tf_op jit(solution)/shard_map/field/pallas_call | solution.py:609
  (1 shorter events, 0.0 us)
Async XLA Ops:
  2.4 4.1 %collective-permute-start = (bf16[48,128]{1,0:T(8,128)(2,1)S(1)}, bf16[48,128]{1,0:T(8,128)(2,1)S(1)}, u32[]{:S(2)}, u32[]{:S(2)}) collective-permute-start(bf16[48,128]{1,0:T(8,128)(2,1)S(1)} %get-tuple-element.30.z0_ref), channel_id=1, source_target_pairs={{0,1},{1,0},{2,3},{3,2},{4,5},{5,4},{6,7},{7,6},{8,9},{9,8},{10,11... | collective-permute-start | bytes 36872 | tf_op jit(solution)/shard_map/ppermute | solution.py:527
  3.0 4.0 %collective-permute-start.1 = (bf16[48,128]{1,0:T(8,128)(2,1)S(1)}, bf16[48,128]{1,0:T(8,128)(2,1)S(1)}, u32[]{:S(2)}, u32[]{:S(2)}) collective-permute-start(bf16[48,128]{1,0:T(8,128)(2,1)S(1)} %get-tuple-element.31.z1_ref), channel_id=1, source_target_pairs={{0,3},{1,2},{2,1},{3,0},{4,7},{5,6},{6,5},{7,4},{8,11},{9,10},{10,... | collective-permute-start | bytes 36872 | tf_op jit(solution)/shard_map/ppermute | solution.py:528
  7.1 4.1 %collective-permute-start.2 = (bf16[176,128]{1,0:T(8,128)(2,1)S(1)}, bf16[176,128]{1,0:T(8,128)(2,1)S(1)}, u32[]{:S(2)}, u32[]{:S(2)}) collective-permute-start(bf16[176,128]{1,0:T(8,128)(2,1)S(1)} %get-tuple-element.33), channel_id=1, source_target_pairs={{0,4},{4,0},{1,5},{5,1},{2,6},{6,2},{3,7},{7,3},{8,12},{12,8},{9,1... | collective-permute-start | bytes 135176 | tf_op jit(solution)/shard_map/ppermute | solution.py:547
  11.2 9.7 %collective-permute-start.4 = (bf16[224,128]{1,0:T(8,128)(2,1)S(1)}, bf16[224,128]{1,0:T(8,128)(2,1)S(1)}, u32[]{:S(2)}, u32[]{:S(2)}) collective-permute-start(bf16[224,128]{1,0:T(8,128)(2,1)S(1)} %get-tuple-element.35.own_ref), channel_id=1, source_target_pairs={{0,24},{8,16},{16,8},{24,0},{1,25},{9,17},{17,9},{25,1},{2,26},{10... | collective-permute-start | bytes 172040 | tf_op jit(solution)/shard_map/ppermute | solution.py:565
  15.0 5.9 %collective-permute-start.3 = (bf16[224,128]{1,0:T(8,128)(2,1)S(1)}, bf16[224,128]{1,0:T(8,128)(2,1)S(1)}, u32[]{:S(2)}, u32[]{:S(2)}) collective-permute-start(bf16[224,128]{1,0:T(8,128)(2,1)S(1)} %get-tuple-element.35.own_ref), channel_id=1, source_target_pairs={{0,8},{8,0},{16,24},{24,16},{1,9},{9,1},{17,25},{25,17},{2,10},{10... | collective-permute-start | bytes 172040 | tf_op jit(solution)/shard_map/ppermute | solution.py:560
  16.0 4.9 %collective-permute-start.5 = (bf16[144,128]{1,0:T(8,128)(2,1)S(1)}, bf16[144,128]{1,0:T(8,128)(2,1)S(1)}, u32[]{:S(2)}, u32[]{:S(2)}) collective-permute-start(bf16[144,128]{1,0:T(8,128)(2,1)S(1)} %get-tuple-element.36), channel_id=1, source_target_pairs={{0,16},{8,24},{16,0},{24,8},{1,17},{9,25},{17,1},{25,9},{2,18},{10... | collective-permute-start | bytes 110600 | tf_op jit(solution)/shard_map/ppermute | solution.py:561

commit v5 on v4

--- a/solution.py
+++ b/solution.py
@@ -372,14 +372,16 @@
 
     for t in range(tiles):
         rows = slice(row_of(t), row_of(t) + STEP)
-        halves = [jnp.concatenate(split(samples[c, rows, :]), 1) for c in range(4)]
+        points = [samples[c, rows, :] for c in range(4)]
+        points = points[:1] + [point - points[0] for point in points[1:]]
+        halves = [jnp.concatenate(split(point), 1) for point in points]
         picked = jnp.dot(jnp.concatenate(halves, 0), hot_ref[t], preferred_element_type=F32)
         for j in range(chunks):
             at = t * chunks + j
             lanes = slice(j * 128, (j + 1) * 128)
             four = [picked[c * STEP : (c + 1) * STEP, lanes] for c in range(4)]
-            value = sum(z_ref[c, at : at + 1, :] * four[c] for c in range(4))
-            slope = sum(z_ref[4 + c, at : at + 1, :] * four[c] for c in range(4))
+            value = four[0] + sum(z_ref[c, at : at + 1, :] * four[c] for c in range(1, 4))
+            slope = sum(z_ref[4 + c, at : at + 1, :] * four[c] for c in range(1, 4))
             for d, part in enumerate((value, value, slope)):
                 force_ref[d, at : at + 1, :] = jnp.sum(
                     weight_ref[t, d, :, lanes] * part, axis=0, keepdims=True
@@ -468,7 +470,7 @@
                 at = pl.ds(n * TALL + y + 1, span, stride=STEP)
                 rows_ref[tile, at, :] = there[:, tile * 128 : (tile + 1) * 128]
     alone = (tiles - EXT) * wide
-    whole = jnp.concatenate([rows_ref[tile] for tile in range(columns // 128)], 1)
+    whole = jnp.concatenate([rows_ref[tile, : span * STEP] for tile in range(columns // 128)], 1)
     out_ref[...] = whole.astype(BF16)
     kept = other_ref.shape[2]
     moved = pltpu.roll(whole, columns - alone, 1)[:, :kept]
@@ -573,7 +575,7 @@
         ),
         in_specs=vmem(1),
         out_specs=tuple(vmem(2)),
-        scratch_shapes=[pltpu.VMEM((band_columns // 128, span * STEP, 128), F32)],
+        scratch_shapes=[pltpu.VMEM((band_columns // 128, -(-span // 8) * 8 * STEP, 128), F32)],
         compiler_params=pltpu.CompilerParams(vmem_limit_bytes=16 << 20),
         cost_estimate=pl.CostEstimate(flops=400_000_000, bytes_accessed=2_000_000, transcendentals=0),
         name="band",

time: 23.6 us -> 23.6 us (level)
  no operation moved by 1% of the time
where the time goes in v5:
time: 23.6 us; the launch traced here: 23.3 us
  starting transfers between devices  9.42 us (40%)
  Pallas kernels  8.93 us (38%)
  waiting for transfers between devices  4.29 us (18%)
  between operations  0.68 us (3%)
    ppermute x1, starting transfers between devices, local(): x3 = lax.ppermute(mine, 'gx', other(n_gx))  3.82 us
    ppermute x1, waiting for transfers between devices, local(): lower = lax.ppermute(far, 'gx', shift(n_gx, 2))  3.14 us
    ppermute x1, starting transfers between devices, local(): got1 = lax.ppermute(z1, 'gz', other(n_gz))  2.62 us
    pallas_call x1, Pallas kernels, local(): pl.pallas_call(functools.partial(field_kernel, tiles, chunks, group_plane...  2.39 us
    pallas_call x1, Pallas kernels, local(): pl.pallas_call(functools.partial(edge_kernel, tiles, chunks, group_planes...  1.77 us
    pallas_call x1, Pallas kernels, local(): band, band_other = band_call(kernel_in)  1.75 us
    ppermute x1, starting transfers between devices, local(): lax.ppermute(sent, 'gy', shift(n_gy, -s))  1.72 us
    pallas_call x1, Pallas kernels, local(): pl.pallas_call(functools.partial(own_kernel, tiles, group_planes, wide, s...  1.08 us
  transfers between devices with their start and end apart: 6, of which 3 were waited for; matrix products, arithmetic and copies ran while one was open for 0% of the time, Pallas kernels for 20%

profile of v5, /device:TPU:0, one launch (start us, length us, event | category | flops | bytes accessed | tf_op | source)
XLA Modules:
  0.0 23.3 jit_solution(10304355346667887214)
XLA Ops:
  0.6 1.8 %edge.1 = (bf16[48,128]{1,0:T(8,128)(2,1)S(1)}, bf16[48,128]{1,0:T(8,128)(2,1)S(1)}, bf16[512,512]{1,0:T(8,128)(2,1)S(1)}, bf16[512,512]{1,0:T(8,128)(2,1)S(1)},...) custom-call(f32[32,128]{1,0:T(8,128)} %bitcast.6, ...), custom_call_target="tpu_custom_call" | custom-call | tf_op jit(solution)/shard_map/edge/pallas_call | solution.py:509
  2.4 0.6 %collective-permute-start = (bf16[48,128]{1,0:T(8,128)(2,1)S(1)}, bf16[48,128]{1,0:T(8,128)(2,1)S(1)}, u32[]{:S(2)}, u32[]{:S(2)}) collective-permute-start(bf16[48,128]{1,0:T(8,128)(2,1)S(1)} %get-tuple-element.30.z0_ref), channel_id=1, source_target_pairs={{0,1},{1,0},{2,3},{3,2},{4,5},{5,4},{6,7},{7,6},{8,9},{9,8},{10,11... | collective-permute-start | bytes 36872 | tf_op jit(solution)/shard_map/ppermute | solution.py:529
  3.0 2.6 %collective-permute-start.1 = (bf16[48,128]{1,0:T(8,128)(2,1)S(1)}, bf16[48,128]{1,0:T(8,128)(2,1)S(1)}, u32[]{:S(2)}, u32[]{:S(2)}) collective-permute-start(bf16[48,128]{1,0:T(8,128)(2,1)S(1)} %get-tuple-element.31.z1_ref), channel_id=1, source_target_pairs={{0,3},{1,2},{2,1},{3,0},{4,7},{5,6},{6,5},{7,4},{8,11},{9,10},{10,... | collective-permute-start | bytes 36872 | tf_op jit(solution)/shard_map/ppermute | solution.py:530
  5.6 0.9 %spread.1.main_ref = f32[176,128]{1,0:T(8,128)S(1)} custom-call(bf16[512,512]{1,0:T(8,128)(2,1)S(1)} %get-tuple-element.26.high_ref, bf16[512,512]{1,0:T(8,128)(2,1)S(1)} %get-tuple-element.27.low_ref, f32[8,32,128]{2,1,0:T(8,128)S(1)} %get-tuple-element.28.weight_ref, s32[32,128]{1,0:T(8,128)S(1)} %get-tuple-element.29.cell_ref), custom_call_target="tpu_custom_call" | custom-call | flops 400000000 | bytes 2000000 | tf_op jit(solution)/shard_map/spread/pallas_call | solution.py:531
  6.5 0.0 collective-permute-done.got0_ref
  6.5 0.5 %collective-permute-done.1.got1_ref = bf16[48,128]{1,0:T(8,128)(2,1)S(1)} collective-permute-done((bf16[48,128]{1,0:T(8,128)(2,1)S(1)}, bf16[48,128]{1,0:T(8,128)(2,1)S(1)}, u32[]{:S(2)}, u32[]{:S(2)}) %collective-permute-start.1) | collective-permute-done | bytes 12320 | tf_op jit(solution)/shard_map/ppermute | solution.py:530
  7.0 0.1 z_fold.1
  7.1 1.7 %collective-permute-start.2 = (bf16[176,128]{1,0:T(8,128)(2,1)S(1)}, bf16[176,128]{1,0:T(8,128)(2,1)S(1)}, u32[]{:S(2)}, u32[]{:S(2)}) collective-permute-start(bf16[176,128]{1,0:T(8,128)(2,1)S(1)} %get-tuple-element.33), channel_id=1, source_target_pairs={{0,4},{4,0},{1,5},{5,1},{2,6},{6,2},{3,7},{7,3},{8,12},{12,8},{9,1... | collective-permute-start | bytes 135176 | tf_op jit(solution)/shard_map/ppermute | solution.py:549
  8.8 1.8 %band.1 = (bf16[816,384]{1,0:T(8,128)(2,1)S(1)}, bf16[3,816,256]{2,1,0:T(8,128)(2,1)S(1)}) custom-call(bf16[17,17,17]{2,1,0:T(8,128)(2,1)S(1)} %get-tuple-element.37.kernel_ref), custom_call_target="tpu_custom_call" | custom-call | flops 400000000 | bytes 2000000 | tf_op jit(solution)/shard_map/band/pallas_call | solution.py:583
  10.6 0.6 %collective-permute-done.2.refs_1_ = bf16[176,128]{1,0:T(8,128)(2,1)S(1)} collective-permute-done((bf16[176,128]{1,0:T(8,128)(2,1)S(1)}, bf16[176,128]{1,0:T(8,128)(2,1)S(1)}, u32[]{:S(2)}, u32[]{:S(2)}) %collective-permute-start.2) | collective-permute-done | bytes 45088 | tf_op jit(solution)/shard_map/ppermute | solution.py:549
  11.2 3.8 %collective-permute-start.4 = (bf16[224,128]{1,0:T(8,128)(2,1)S(1)}, bf16[224,128]{1,0:T(8,128)(2,1)S(1)}, u32[]{:S(2)}, u32[]{:S(2)}) collective-permute-start(bf16[224,128]{1,0:T(8,128)(2,1)S(1)} %get-tuple-element.35.own_ref), channel_id=1, source_target_pairs={{0,24},{8,16},{16,8},{24,0},{1,25},{9,17},{17,9},{25,1},{2,26},{10... | collective-permute-start | bytes 172040 | tf_op jit(solution)/shard_map/ppermute | solution.py:567
  15.0 0.0 collective-permute-start.3
  15.0 1.0 %weights.1 = (bf16[8,256,512]{2,1,0:T(8,128)(2,1)S(1)}, f32[8,3,48,512]{3,2,1,0:T(8,128)S(1)}, f32[8,32,128]{2,1,0:T(8,128)S(1)}) custom-call(f32[32,128]{1,0:T(8,128)S(1)} %get-tuple-element.42.charge_ref, f32[96,128]{1,0:T(8,128)S(1)} %get-tuple-element.43.offset_ref, s32[64,128]{1,0:T(8,128)S(1)} %get-tuple-element.44.cell_ref), custom_call_target="tpu_custom_call" | custom-call | flops 400000000 | bytes 2000000 | tf_op jit(solution)/shard_map/weights/pallas_call | solution.py:584
  16.0 0.7 %collective-permute-start.5 = (bf16[144,128]{1,0:T(8,128)(2,1)S(1)}, bf16[144,128]{1,0:T(8,128)(2,1)S(1)}, u32[]{:S(2)}, u32[]{:S(2)}) collective-permute-start(bf16[144,128]{1,0:T(8,128)(2,1)S(1)} %get-tuple-element.36), channel_id=1, source_target_pairs={{0,16},{8,24},{16,0},{24,8},{1,17},{9,25},{17,1},{25,9},{2,18},{10... | collective-permute-start | bytes 110600 | tf_op jit(solution)/shard_map/ppermute | solution.py:563
  16.7 1.1 %own.1 = (f32[144,128]{1,0:T(8,128)S(1)}, f32[144,128]{1,0:T(8,128)S(1)}) custom-call(bf16[224,128]{1,0:T(8,128)(2,1)S(1)} %get-tuple-element.35.own_ref, bf16[816,384]{1,0:T(8,128)(2,1)S(1)} %get-tuple-element.39.band_ref), custom_call_target="tpu_custom_call" | custom-call | flops 400000000 | bytes 2000000 | tf_op jit(solution)/shard_map/own/pallas_call | solution.py:598
  17.8 3.1 %collective-permute-done.5.lower_ref.upper_ref = bf16[144,128]{1,0:T(8,128)(2,1)S(1)} collective-permute-done((bf16[144,128]{1,0:T(8,128)(2,1)S(1)}, bf16[144,128]{1,0:T(8,128)(2,1)S(1)}, u32[]{:S(2)}, u32[]{:S(2)}) %collective-permute-start.5) | collective-permute-done | bytes 36896 | tf_op jit(solution)/shard_map/ppermute | solution.py:563
  20.9 0.0 collective-permute-done.4.got3_ref
  20.9 0.0 collective-permute-done.3.got1_ref
  20.9 2.4 %field.1 = (f32[8,8,128]{2,1,0:T(8,128)}, f32[3,32,128]{2,1,0:T(8,128)}) custom-call(f32[144,128]{1,0:T(8,128)S(1)} %get-tuple-element.34.own_ref, bf16[224,128]{1,0:T(8,128)(2,1)S(1)} %collective-permute-done.3.got1_ref, bf16[224,128]{1,0:T(8,128)(2,1)S(1)} %collective-permute-done.4.got3_ref, ...), custom_call_target="tpu_custom_call" | custom-call | tf_op jit(solution)/shard_map/field/pallas_call | solution.py:611
  (1 shorter events, 0.0 us)
Async XLA Ops:
  2.4 4.1 %collective-permute-start = (bf16[48,128]{1,0:T(8,128)(2,1)S(1)}, bf16[48,128]{1,0:T(8,128)(2,1)S(1)}, u32[]{:S(2)}, u32[]{:S(2)}) collective-permute-start(bf16[48,128]{1,0:T(8,128)(2,1)S(1)} %get-tuple-element.30.z0_ref), channel_id=1, source_target_pairs={{0,1},{1,0},{2,3},{3,2},{4,5},{5,4},{6,7},{7,6},{8,9},{9,8},{10,11... | collective-permute-start | bytes 36872 | tf_op jit(solution)/shard_map/ppermute | solution.py:529
  3.0 4.0 %collective-permute-start.1 = (bf16[48,128]{1,0:T(8,128)(2,1)S(1)}, bf16[48,128]{1,0:T(8,128)(2,1)S(1)}, u32[]{:S(2)}, u32[]{:S(2)}) collective-permute-start(bf16[48,128]{1,0:T(8,128)(2,1)S(1)} %get-tuple-element.31.z1_ref), channel_id=1, source_target_pairs={{0,3},{1,2},{2,1},{3,0},{4,7},{5,6},{6,5},{7,4},{8,11},{9,10},{10,... | collective-permute-start | bytes 36872 | tf_op jit(solution)/shard_map/ppermute | solution.py:530
  7.1 4.1 %collective-permute-start.2 = (bf16[176,128]{1,0:T(8,128)(2,1)S(1)}, bf16[176,128]{1,0:T(8,128)(2,1)S(1)}, u32[]{:S(2)}, u32[]{:S(2)}) collective-permute-start(bf16[176,128]{1,0:T(8,128)(2,1)S(1)} %get-tuple-element.33), channel_id=1, source_target_pairs={{0,4},{4,0},{1,5},{5,1},{2,6},{6,2},{3,7},{7,3},{8,12},{12,8},{9,1... | collective-permute-start | bytes 135176 | tf_op jit(solution)/shard_map/ppermute | solution.py:549
  11.2 9.7 %collective-permute-start.4 = (bf16[224,128]{1,0:T(8,128)(2,1)S(1)}, bf16[224,128]{1,0:T(8,128)(2,1)S(1)}, u32[]{:S(2)}, u32[]{:S(2)}) collective-permute-start(bf16[224,128]{1,0:T(8,128)(2,1)S(1)} %get-tuple-element.35.own_ref), channel_id=1, source_target_pairs={{0,24},{8,16},{16,8},{24,0},{1,25},{9,17},{17,9},{25,1},{2,26},{10... | collective-permute-start | bytes 172040 | tf_op jit(solution)/shard_map/ppermute | solution.py:567
  15.0 5.9 %collective-permute-start.3 = (bf16[224,128]{1,0:T(8,128)(2,1)S(1)}, bf16[224,128]{1,0:T(8,128)(2,1)S(1)}, u32[]{:S(2)}, u32[]{:S(2)}) collective-permute-start(bf16[224,128]{1,0:T(8,128)(2,1)S(1)} %get-tuple-element.35.own_ref), channel_id=1, source_target_pairs={{0,8},{8,0},{16,24},{24,16},{1,9},{9,1},{17,25},{25,17},{2,10},{10... | collective-permute-start | bytes 172040 | tf_op jit(solution)/shard_map/ppermute | solution.py:562
  16.0 4.9 %collective-permute-start.5 = (bf16[144,128]{1,0:T(8,128)(2,1)S(1)}, bf16[144,128]{1,0:T(8,128)(2,1)S(1)}, u32[]{:S(2)}, u32[]{:S(2)}) collective-permute-start(bf16[144,128]{1,0:T(8,128)(2,1)S(1)} %get-tuple-element.36), channel_id=1, source_target_pairs={{0,16},{8,24},{16,0},{24,8},{1,17},{9,25},{17,1},{25,9},{2,18},{10... | collective-permute-start | bytes 110600 | tf_op jit(solution)/shard_map/ppermute | solution.py:563

commit v6 on v5

--- a/solution.py
+++ b/solution.py
@@ -239,7 +239,8 @@
 def along_z_taps(parts, row, radius):
     lane = iota((8, 128), 1)
     total = parts[radius, row : row + 8, :128]
-    outside = [jnp.zeros((8, 128), F32)] * 3
+    below = jnp.zeros((8, 128), F32)
+    above = [jnp.zeros((8, 128), F32)] * 2
     for k in range(2 * radius + 1):
         inner = parts[k, row : row + 8, :128]
         outer = parts[k, row : row + 8, 128:]
@@ -247,10 +248,16 @@
         if step:
             taken = lane >= 128 - step if step > 0 else lane < -step
             total = total + pltpu.roll(jnp.where(taken, outer, inner), step % 128, 1)
-        for n, z in enumerate((-1, CZ, CZ + 1)):
-            at = z - step
-            value = inner if 0 <= at < CZ else outer
-            outside[n] = jnp.where(lane == at % 128, value, outside[n])
+        below = jnp.where(lane == (-1 - step) % 128, inner if step < 0 else outer, below)
+        at, parity = CZ - step, step % 2
+        if at == CZ - 1:
+            above[parity] = jnp.where(lane == at, inner, jnp.where(lane == 0, outer, above[parity]))
+        else:
+            first = at % 128
+            pair = (lane == first) | (lane == first + 1)
+            above[parity] = jnp.where(pair, inner if at < CZ else outer, above[parity])
+    even = (lane & 1) == 0
+    outside = (below, jnp.where(even, above[0], above[1]), jnp.where(even, above[1], above[0]))
     return total, [jnp.sum(v, axis=1, keepdims=True) for v in outside]
 
 

time: 23.6 us -> 23.6 us (level)
  no operation moved by 1% of the time
where the time goes in v6:
time: 23.6 us; the launch traced here: 23.3 us
  starting transfers between devices  9.42 us (40%)
  Pallas kernels  8.93 us (38%)
  waiting for transfers between devices  4.28 us (18%)
  between operations  0.68 us (3%)
    ppermute x1, starting transfers between devices, local(): x3 = lax.ppermute(mine, 'gx', other(n_gx))  3.82 us
    ppermute x1, waiting for transfers between devices, local(): lower = lax.ppermute(far, 'gx', shift(n_gx, 2))  3.14 us
    ppermute x1, starting transfers between devices, local(): got1 = lax.ppermute(z1, 'gz', other(n_gz))  2.62 us
    pallas_call x1, Pallas kernels, local(): pl.pallas_call(functools.partial(field_kernel, tiles, chunks, group_plane...  2.39 us
    pallas_call x1, Pallas kernels, local(): pl.pallas_call(functools.partial(edge_kernel, tiles, chunks, group_planes...  1.77 us
    pallas_call x1, Pallas kernels, local(): band, band_other = band_call(kernel_in)  1.75 us
    ppermute x1, starting transfers between devices, local(): lax.ppermute(sent, 'gy', shift(n_gy, -s))  1.72 us
    pallas_call x1, Pallas kernels, local(): pl.pallas_call(functools.partial(own_kernel, tiles, group_planes, wide, s...  1.08 us
  transfers between devices with their start and end apart: 6, of which 3 were waited for; matrix products, arithmetic and copies ran while one was open for 0% of the time, Pallas kernels for 20%

profile of v6, /device:TPU:0, one launch (start us, length us, event | category | flops | bytes accessed | tf_op | source)
XLA Modules:
  0.0 23.3 jit_solution(17348744994881035358)
XLA Ops:
  0.6 1.8 %edge.1 = (bf16[48,128]{1,0:T(8,128)(2,1)S(1)}, bf16[48,128]{1,0:T(8,128)(2,1)S(1)}, bf16[512,512]{1,0:T(8,128)(2,1)S(1)}, bf16[512,512]{1,0:T(8,128)(2,1)S(1)},...) custom-call(f32[32,128]{1,0:T(8,128)} %bitcast.6, ...), custom_call_target="tpu_custom_call" | custom-call | tf_op jit(solution)/shard_map/edge/pallas_call | solution.py:516
  2.4 0.6 %collective-permute-start = (bf16[48,128]{1,0:T(8,128)(2,1)S(1)}, bf16[48,128]{1,0:T(8,128)(2,1)S(1)}, u32[]{:S(2)}, u32[]{:S(2)}) collective-permute-start(bf16[48,128]{1,0:T(8,128)(2,1)S(1)} %get-tuple-element.30.z0_ref), channel_id=1, source_target_pairs={{0,1},{1,0},{2,3},{3,2},{4,5},{5,4},{6,7},{7,6},{8,9},{9,8},{10,11... | collective-permute-start | bytes 36872 | tf_op jit(solution)/shard_map/ppermute | solution.py:536
  3.0 2.6 %collective-permute-start.1 = (bf16[48,128]{1,0:T(8,128)(2,1)S(1)}, bf16[48,128]{1,0:T(8,128)(2,1)S(1)}, u32[]{:S(2)}, u32[]{:S(2)}) collective-permute-start(bf16[48,128]{1,0:T(8,128)(2,1)S(1)} %get-tuple-element.31.z1_ref), channel_id=1, source_target_pairs={{0,3},{1,2},{2,1},{3,0},{4,7},{5,6},{6,5},{7,4},{8,11},{9,10},{10,... | collective-permute-start | bytes 36872 | tf_op jit(solution)/shard_map/ppermute | solution.py:537
  5.6 0.9 %spread.1.main_ref = f32[176,128]{1,0:T(8,128)S(1)} custom-call(bf16[512,512]{1,0:T(8,128)(2,1)S(1)} %get-tuple-element.26.high_ref, bf16[512,512]{1,0:T(8,128)(2,1)S(1)} %get-tuple-element.27.low_ref, f32[8,32,128]{2,1,0:T(8,128)S(1)} %get-tuple-element.28.weight_ref, s32[32,128]{1,0:T(8,128)S(1)} %get-tuple-element.29.cell_ref), custom_call_target="tpu_custom_call" | custom-call | flops 400000000 | bytes 2000000 | tf_op jit(solution)/shard_map/spread/pallas_call | solution.py:538
  6.5 0.0 collective-permute-done.got0_ref
  6.5 0.5 %collective-permute-done.1.got1_ref = bf16[48,128]{1,0:T(8,128)(2,1)S(1)} collective-permute-done((bf16[48,128]{1,0:T(8,128)(2,1)S(1)}, bf16[48,128]{1,0:T(8,128)(2,1)S(1)}, u32[]{:S(2)}, u32[]{:S(2)}) %collective-permute-start.1) | collective-permute-done | bytes 12320 | tf_op jit(solution)/shard_map/ppermute | solution.py:537
  7.0 0.1 z_fold.1
  7.1 1.7 %collective-permute-start.2 = (bf16[176,128]{1,0:T(8,128)(2,1)S(1)}, bf16[176,128]{1,0:T(8,128)(2,1)S(1)}, u32[]{:S(2)}, u32[]{:S(2)}) collective-permute-start(bf16[176,128]{1,0:T(8,128)(2,1)S(1)} %get-tuple-element.33), channel_id=1, source_target_pairs={{0,4},{4,0},{1,5},{5,1},{2,6},{6,2},{3,7},{7,3},{8,12},{12,8},{9,1... | collective-permute-start | bytes 135176 | tf_op jit(solution)/shard_map/ppermute | solution.py:556
  8.8 1.8 %band.1 = (bf16[816,384]{1,0:T(8,128)(2,1)S(1)}, bf16[3,816,256]{2,1,0:T(8,128)(2,1)S(1)}) custom-call(bf16[17,17,17]{2,1,0:T(8,128)(2,1)S(1)} %get-tuple-element.37.kernel_ref), custom_call_target="tpu_custom_call" | custom-call | flops 400000000 | bytes 2000000 | tf_op jit(solution)/shard_map/band/pallas_call | solution.py:590
  10.6 0.6 %collective-permute-done.2.refs_1_ = bf16[176,128]{1,0:T(8,128)(2,1)S(1)} collective-permute-done((bf16[176,128]{1,0:T(8,128)(2,1)S(1)}, bf16[176,128]{1,0:T(8,128)(2,1)S(1)}, u32[]{:S(2)}, u32[]{:S(2)}) %collective-permute-start.2) | collective-permute-done | bytes 45088 | tf_op jit(solution)/shard_map/ppermute | solution.py:556
  11.2 3.8 %collective-permute-start.4 = (bf16[224,128]{1,0:T(8,128)(2,1)S(1)}, bf16[224,128]{1,0:T(8,128)(2,1)S(1)}, u32[]{:S(2)}, u32[]{:S(2)}) collective-permute-start(bf16[224,128]{1,0:T(8,128)(2,1)S(1)} %get-tuple-element.35.own_ref), channel_id=1, source_target_pairs={{0,24},{8,16},{16,8},{24,0},{1,25},{9,17},{17,9},{25,1},{2,26},{10... | collective-permute-start | bytes 172040 | tf_op jit(solution)/shard_map/ppermute | solution.py:574
  15.0 0.0 collective-permute-start.3
  15.0 1.0 %weights.1 = (bf16[8,256,512]{2,1,0:T(8,128)(2,1)S(1)}, f32[8,3,48,512]{3,2,1,0:T(8,128)S(1)}, f32[8,32,128]{2,1,0:T(8,128)S(1)}) custom-call(f32[32,128]{1,0:T(8,128)S(1)} %get-tuple-element.42.charge_ref, f32[96,128]{1,0:T(8,128)S(1)} %get-tuple-element.43.offset_ref, s32[64,128]{1,0:T(8,128)S(1)} %get-tuple-element.44.cell_ref), custom_call_target="tpu_custom_call" | custom-call | flops 400000000 | bytes 2000000 | tf_op jit(solution)/shard_map/weights/pallas_call | solution.py:591
  16.0 0.7 %collective-permute-start.5 = (bf16[144,128]{1,0:T(8,128)(2,1)S(1)}, bf16[144,128]{1,0:T(8,128)(2,1)S(1)}, u32[]{:S(2)}, u32[]{:S(2)}) collective-permute-start(bf16[144,128]{1,0:T(8,128)(2,1)S(1)} %get-tuple-element.36), channel_id=1, source_target_pairs={{0,16},{8,24},{16,0},{24,8},{1,17},{9,25},{17,1},{25,9},{2,18},{10... | collective-permute-start | bytes 110600 | tf_op jit(solution)/shard_map/ppermute | solution.py:570
  16.7 1.1 %own.1 = (f32[144,128]{1,0:T(8,128)S(1)}, f32[144,128]{1,0:T(8,128)S(1)}) custom-call(bf16[224,128]{1,0:T(8,128)(2,1)S(1)} %get-tuple-element.35.own_ref, bf16[816,384]{1,0:T(8,128)(2,1)S(1)} %get-tuple-element.39.band_ref), custom_call_target="tpu_custom_call" | custom-call | flops 400000000 | bytes 2000000 | tf_op jit(solution)/shard_map/own/pallas_call | solution.py:605
  17.8 3.1 %collective-permute-done.5.lower_ref.upper_ref = bf16[144,128]{1,0:T(8,128)(2,1)S(1)} collective-permute-done((bf16[144,128]{1,0:T(8,128)(2,1)S(1)}, bf16[144,128]{1,0:T(8,128)(2,1)S(1)}, u32[]{:S(2)}, u32[]{:S(2)}) %collective-permute-start.5) | collective-permute-done | bytes 36896 | tf_op jit(solution)/shard_map/ppermute | solution.py:570
  20.9 0.0 collective-permute-done.4.got3_ref
  20.9 0.0 collective-permute-done.3.got1_ref
  20.9 2.4 %field.1 = (f32[8,8,128]{2,1,0:T(8,128)}, f32[3,32,128]{2,1,0:T(8,128)}) custom-call(f32[144,128]{1,0:T(8,128)S(1)} %get-tuple-element.34.own_ref, bf16[224,128]{1,0:T(8,128)(2,1)S(1)} %collective-permute-done.3.got1_ref, bf16[224,128]{1,0:T(8,128)(2,1)S(1)} %collective-permute-done.4.got3_ref, ...), custom_call_target="tpu_custom_call" | custom-call | tf_op jit(solution)/shard_map/field/pallas_call | solution.py:618
  (1 shorter events, 0.0 us)
Async XLA Ops:
  2.4 4.1 %collective-permute-start = (bf16[48,128]{1,0:T(8,128)(2,1)S(1)}, bf16[48,128]{1,0:T(8,128)(2,1)S(1)}, u32[]{:S(2)}, u32[]{:S(2)}) collective-permute-start(bf16[48,128]{1,0:T(8,128)(2,1)S(1)} %get-tuple-element.30.z0_ref), channel_id=1, source_target_pairs={{0,1},{1,0},{2,3},{3,2},{4,5},{5,4},{6,7},{7,6},{8,9},{9,8},{10,11... | collective-permute-start | bytes 36872 | tf_op jit(solution)/shard_map/ppermute | solution.py:536
  3.0 4.0 %collective-permute-start.1 = (bf16[48,128]{1,0:T(8,128)(2,1)S(1)}, bf16[48,128]{1,0:T(8,128)(2,1)S(1)}, u32[]{:S(2)}, u32[]{:S(2)}) collective-permute-start(bf16[48,128]{1,0:T(8,128)(2,1)S(1)} %get-tuple-element.31.z1_ref), channel_id=1, source_target_pairs={{0,3},{1,2},{2,1},{3,0},{4,7},{5,6},{6,5},{7,4},{8,11},{9,10},{10,... | collective-permute-start | bytes 36872 | tf_op jit(solution)/shard_map/ppermute | solution.py:537
  7.1 4.1 %collective-permute-start.2 = (bf16[176,128]{1,0:T(8,128)(2,1)S(1)}, bf16[176,128]{1,0:T(8,128)(2,1)S(1)}, u32[]{:S(2)}, u32[]{:S(2)}) collective-permute-start(bf16[176,128]{1,0:T(8,128)(2,1)S(1)} %get-tuple-element.33), channel_id=1, source_target_pairs={{0,4},{4,0},{1,5},{5,1},{2,6},{6,2},{3,7},{7,3},{8,12},{12,8},{9,1... | collective-permute-start | bytes 135176 | tf_op jit(solution)/shard_map/ppermute | solution.py:556
  11.2 9.7 %collective-permute-start.4 = (bf16[224,128]{1,0:T(8,128)(2,1)S(1)}, bf16[224,128]{1,0:T(8,128)(2,1)S(1)}, u32[]{:S(2)}, u32[]{:S(2)}) collective-permute-start(bf16[224,128]{1,0:T(8,128)(2,1)S(1)} %get-tuple-element.35.own_ref), channel_id=1, source_target_pairs={{0,24},{8,16},{16,8},{24,0},{1,25},{9,17},{17,9},{25,1},{2,26},{10... | collective-permute-start | bytes 172040 | tf_op jit(solution)/shard_map/ppermute | solution.py:574
  15.0 5.9 %collective-permute-start.3 = (bf16[224,128]{1,0:T(8,128)(2,1)S(1)}, bf16[224,128]{1,0:T(8,128)(2,1)S(1)}, u32[]{:S(2)}, u32[]{:S(2)}) collective-permute-start(bf16[224,128]{1,0:T(8,128)(2,1)S(1)} %get-tuple-element.35.own_ref), channel_id=1, source_target_pairs={{0,8},{8,0},{16,24},{24,16},{1,9},{9,1},{17,25},{25,17},{2,10},{10... | collective-permute-start | bytes 172040 | tf_op jit(solution)/shard_map/ppermute | solution.py:569
  16.0 4.9 %collective-permute-start.5 = (bf16[144,128]{1,0:T(8,128)(2,1)S(1)}, bf16[144,128]{1,0:T(8,128)(2,1)S(1)}, u32[]{:S(2)}, u32[]{:S(2)}) collective-permute-start(bf16[144,128]{1,0:T(8,128)(2,1)S(1)} %get-tuple-element.36), channel_id=1, source_target_pairs={{0,16},{8,24},{16,0},{24,8},{1,17},{9,25},{17,1},{25,9},{2,18},{10... | collective-permute-start | bytes 110600 | tf_op jit(solution)/shard_map/ppermute | solution.py:570
